TPU v7x, 32 devices: a whole 2x2x4 slice. The times are simulated.
32 devices in a mesh: dp: 8 (over y, x, core), tp: 4 (over z).
Axes of the slice: x: 2, y: 2, z: 4, core: 2. Of those that a mesh axis runs over, the one named last changes fastest.
Arguments:
- tokens: bfloat16 [16384, 2048], P('dp'), may hold values from -6 to 6
- doc_ids: int32 [16, 1024], P('dp'), may hold values from 0 to 3, never falling along the last dimension, each value on 1 to 512 neighbouring positions
- norm1_gain: bfloat16 [2048], replicated, may hold values from 0.5 to 1.5
- norm1_bias: bfloat16 [2048], replicated, may hold values from -4 to 4
- query_weight: bfloat16 [2048, 2048], P(None, 'tp'), may hold values from -0.125 to 0.125
- query_bias: bfloat16 [2048], P('tp'), may hold values from -6 to 6
- keyval_weight: bfloat16 [2048, 256], replicated, may hold values from -0.125 to 0.125
- value_bias: bfloat16 [128], replicated, may hold values from -3 to 3
- out_weight: bfloat16 [2048, 2048], P('tp'), may hold values from -0.5 to 0.5
- out_bias: bfloat16 [2048], replicated, may hold values from -6 to 6
- norm2_gain: bfloat16 [2048], replicated, may hold values from 0.5 to 1.5
- norm2_bias: bfloat16 [2048], replicated, may hold values from -4 to 4
- up_weight: bfloat16 [2048, 8192], P(None, 'tp'), may hold values from -0.125 to 0.125
- up_bias: bfloat16 [8192], P('tp'), may hold values from -6 to 6
- down_weight: bfloat16 [8192, 2048], P('tp'), may hold values from -0.0625 to 0.0625
- down_bias: bfloat16 [2048], replicated, may hold values from -6 to 6
- grad_out: bfloat16 [16384, 2048], P('dp'), may hold values from -6 to 6
Outputs:
- output: bfloat16 [16384, 2048], P('dp')
- grad_tokens: bfloat16 [16384, 2048], P('dp')
- grad_norm1_gain: float32 [2048], P('dp')
- grad_norm1_bias: float32 [2048], P('dp')
- grad_query_weight: float32 [2048, 2048], P('dp', 'tp')
- grad_query_bias: float32 [2048], P(('tp', 'dp'))
- grad_keyval_weight: float32 [2048, 256], P(('dp', 'tp'))
- grad_value_bias: float32 [128], P(('dp', 'tp'))
- grad_out_weight: float32 [2048, 2048], P('tp', 'dp')
- grad_out_bias: float32 [2048], P('dp')
- grad_norm2_gain: float32 [2048], P('dp')
- grad_norm2_bias: float32 [2048], P('dp')
- grad_up_weight: float32 [2048, 8192], P('dp', 'tp')
- grad_up_bias: float32 [8192], P(('tp', 'dp'))
- grad_down_weight: float32 [8192, 2048], P('tp', 'dp')
- grad_down_bias: float32 [2048], P('dp')
Inputs may be any that keep to these rules, and one draw needn't show every extreme that they name: `doc_ids`: document numbers never fall along a row of a window; a document spans 1 to half of 1024 tokens.
All inputs are finite; a program needn't handle non-finite values.
Results may differ from a plain program's by a relative error of at most 0.02.
Values may be sent and summed in bfloat16 or wider, within the bound.
A program may use at most 384 MiB of HBM per device.

v0:
```python
import jax
import jax.numpy as jnp
from jax import lax
from jax.sharding import PartitionSpec as P


def layer_norm(values, gain_vec, shift_vec):
    center = values - jnp.mean(values, axis=-1, keepdims=True)
    spread = jnp.mean(center * center, axis=-1, keepdims=True)
    return center * lax.rsqrt(spread + 1e-05) * gain_vec + shift_vec


def gelu_tanh(values):
    return jax.nn.gelu(values, approximate=True)


def allowed_mask(doc_row):
    places = jnp.arange(doc_row.shape[0])
    return (doc_row[:, None] == doc_row[None, :]) & (places[:, None] >= places[None, :])


def masked_scores(heads_q, keys_low, allowed, score_scale):
    scores = (
        jnp.einsum("shd,td->hst", heads_q, keys_low, preferred_element_type=jnp.float32)
        * score_scale
    )
    return jnp.where(allowed[None], scores, -1e30)


def forward_block(seq_rows, doc_row, params, score_scale, head_dim):
    seq_len = seq_rows.shape[0]
    normed1 = layer_norm(seq_rows, params["norm1_gain"], params["norm1_bias"]).astype(jnp.bfloat16)
    queries = (
        jnp.dot(normed1, params["query_weight"], preferred_element_type=jnp.float32)
        + params["query_bias"]
    )
    heads_q = queries.astype(jnp.bfloat16).reshape(seq_len, -1, head_dim)
    keyval = jnp.dot(normed1, params["keyval_weight"], preferred_element_type=jnp.float32)
    keys_low = keyval[:, :head_dim].astype(jnp.bfloat16)
    values_low = (keyval[:, head_dim:] + params["value_bias"]).astype(jnp.bfloat16)
    allowed = allowed_mask(doc_row)
    scores = masked_scores(heads_q, keys_low, allowed, score_scale)
    highest = jnp.max(scores, axis=2, keepdims=True)
    lifted = jnp.exp(scores - highest)
    totals = jnp.sum(lifted, axis=2, keepdims=True)
    chances = lifted / totals
    log_totals = (highest + jnp.log(totals))[..., 0]
    attended = (
        jnp.einsum(
            "hst,td->shd",
            chances.astype(jnp.bfloat16),
            values_low,
            preferred_element_type=jnp.float32,
        )
        .astype(jnp.bfloat16)
        .reshape(seq_len, -1)
    )
    partial_value = jnp.dot(attended, params["out_weight"], preferred_element_type=jnp.float32)
    mixed_sum = lax.psum(partial_value.astype(jnp.bfloat16), "tp").astype(jnp.float32)
    hidden1 = seq_rows + mixed_sum + params["out_bias"]
    normed2 = layer_norm(hidden1, params["norm2_gain"], params["norm2_bias"]).astype(jnp.bfloat16)
    before = (
        jnp.dot(normed2, params["up_weight"], preferred_element_type=jnp.float32)
        + params["up_bias"]
    )
    activated = gelu_tanh(before).astype(jnp.bfloat16)
    down_part = jnp.dot(activated, params["down_weight"], preferred_element_type=jnp.float32)
    summed = lax.psum(down_part.astype(jnp.bfloat16), "tp").astype(jnp.float32)
    result = hidden1 + summed + params["down_bias"]
    kept_state = (
        normed1,
        heads_q,
        keys_low,
        values_low,
        allowed,
        log_totals,
        attended,
        hidden1,
        normed2,
        before,
        activated,
    )
    return (result, kept_state)


def backward_block(seq_rows, cotangent, kept_state, params, score_scale, head_dim):
    (
        normed1,
        heads_q,
        keys_low,
        values_low,
        allowed,
        log_totals,
        attended,
        hidden1,
        normed2,
        before,
        activated,
    ) = kept_state
    seq_len = seq_rows.shape[0]
    grad_low = cotangent.astype(jnp.bfloat16)
    grad_down_bias = jnp.sum(cotangent, axis=0)
    grad_down_weight = jnp.dot(activated.T, grad_low, preferred_element_type=jnp.float32)
    grad_activated = jnp.dot(grad_low, params["down_weight"].T, preferred_element_type=jnp.float32)
    grad_before = jax.vjp(gelu_tanh, before)[1](grad_activated)[0].astype(jnp.bfloat16)
    grad_up_weight = jnp.dot(normed2.T, grad_before, preferred_element_type=jnp.float32)
    grad_up_bias = jnp.sum(grad_before.astype(jnp.float32), axis=0)
    partial2 = jnp.dot(grad_before, params["up_weight"].T, preferred_element_type=jnp.float32)
    grad_normed2 = lax.psum(partial2.astype(jnp.bfloat16), "tp").astype(jnp.float32)
    norm2_pull = jax.vjp(layer_norm, hidden1, params["norm2_gain"], params["norm2_bias"])[1]
    through2, grad_norm2_gain, grad_norm2_bias = norm2_pull(grad_normed2)
    grad_hidden1 = cotangent + through2
    grad_out_bias = jnp.sum(grad_hidden1, axis=0)
    grad_mixed = grad_hidden1.astype(jnp.bfloat16)
    grad_out_weight = jnp.dot(attended.T, grad_mixed, preferred_element_type=jnp.float32)
    grad_attended = jnp.dot(grad_mixed, params["out_weight"].T, preferred_element_type=jnp.float32)
    grad_attended = grad_attended.astype(jnp.bfloat16).reshape(seq_len, -1, head_dim)
    scores = masked_scores(heads_q, keys_low, allowed, score_scale)
    chances = jnp.exp(scores - log_totals[..., None])
    grad_chances = jnp.einsum(
        "shd,td->hst", grad_attended, values_low, preferred_element_type=jnp.float32
    )
    grad_values = jnp.einsum(
        "hst,shd->td",
        chances.astype(jnp.bfloat16),
        grad_attended,
        preferred_element_type=jnp.float32,
    )
    weighted = jnp.sum(chances * grad_chances, axis=2, keepdims=True)
    grad_scores = (chances * (grad_chances - weighted) * score_scale).astype(jnp.bfloat16)
    grad_queries = jnp.einsum(
        "hst,td->shd", grad_scores, keys_low, preferred_element_type=jnp.float32
    )
    grad_queries = grad_queries.reshape(seq_len, -1).astype(jnp.bfloat16)
    grad_keys = jnp.einsum("hst,shd->td", grad_scores, heads_q, preferred_element_type=jnp.float32)
    grad_keyval = jnp.concatenate([grad_keys, grad_values], axis=1).astype(jnp.bfloat16)
    grad_query_weight = jnp.dot(normed1.T, grad_queries, preferred_element_type=jnp.float32)
    grad_query_bias = jnp.sum(grad_queries.astype(jnp.float32), axis=0)
    grad_keyval_weight = jnp.dot(normed1.T, grad_keyval, preferred_element_type=jnp.float32)
    grad_value_bias = jnp.sum(grad_keyval[:, head_dim:].astype(jnp.float32), axis=0)
    partial1 = jnp.dot(grad_queries, params["query_weight"].T, preferred_element_type=jnp.float32)
    partial1 = partial1 + jnp.dot(
        grad_keyval, params["keyval_weight"].T, preferred_element_type=jnp.float32
    )
    grad_normed1 = lax.psum(partial1.astype(jnp.bfloat16), "tp").astype(jnp.float32)
    norm1_pull = jax.vjp(layer_norm, seq_rows, params["norm1_gain"], params["norm1_bias"])[1]
    through1, grad_norm1_gain, grad_norm1_bias = norm1_pull(grad_normed1)
    grad_input = grad_hidden1 + through1
    grad_terms = (
        grad_query_weight,
        grad_up_weight,
        grad_query_bias,
        grad_up_bias,
        grad_norm1_gain,
        grad_norm1_bias,
        grad_out_bias,
        grad_norm2_gain,
        grad_norm2_bias,
        grad_down_bias,
        grad_out_weight,
        grad_down_weight,
        grad_keyval_weight,
        grad_value_bias,
    )
    return (grad_input, grad_terms)


def reduce_once(grad_terms):
    row_shards = (
        lax.psum_scatter(
            grad_terms[0].astype(jnp.bfloat16), "dp", scatter_dimension=0, tiled=True
        ).astype(jnp.float32),
        lax.psum_scatter(
            grad_terms[1].astype(jnp.bfloat16), "dp", scatter_dimension=0, tiled=True
        ).astype(jnp.float32),
        lax.psum_scatter(
            grad_terms[2].astype(jnp.bfloat16), "dp", scatter_dimension=0, tiled=True
        ).astype(jnp.float32),
        lax.psum_scatter(
            grad_terms[3].astype(jnp.bfloat16), "dp", scatter_dimension=0, tiled=True
        ).astype(jnp.float32),
        lax.psum_scatter(
            grad_terms[4].astype(jnp.bfloat16), "dp", scatter_dimension=0, tiled=True
        ).astype(jnp.float32),
        lax.psum_scatter(
            grad_terms[5].astype(jnp.bfloat16), "dp", scatter_dimension=0, tiled=True
        ).astype(jnp.float32),
        lax.psum_scatter(
            grad_terms[6].astype(jnp.bfloat16), "dp", scatter_dimension=0, tiled=True
        ).astype(jnp.float32),
        lax.psum_scatter(
            grad_terms[7].astype(jnp.bfloat16), "dp", scatter_dimension=0, tiled=True
        ).astype(jnp.float32),
        lax.psum_scatter(
            grad_terms[8].astype(jnp.bfloat16), "dp", scatter_dimension=0, tiled=True
        ).astype(jnp.float32),
        lax.psum_scatter(
            grad_terms[9].astype(jnp.bfloat16), "dp", scatter_dimension=0, tiled=True
        ).astype(jnp.float32),
    )
    col_shards = (
        lax.psum_scatter(
            grad_terms[10].astype(jnp.bfloat16), "dp", scatter_dimension=1, tiled=True
        ).astype(jnp.float32),
        lax.psum_scatter(
            grad_terms[11].astype(jnp.bfloat16), "dp", scatter_dimension=1, tiled=True
        ).astype(jnp.float32),
    )
    shared_shards = (
        lax.psum_scatter(grad_terms[12], ("dp", "tp"), scatter_dimension=0, tiled=True),
        lax.psum_scatter(grad_terms[13], ("dp", "tp"), scatter_dimension=0, tiled=True),
    )
    return tuple(row_shards) + tuple(col_shards) + tuple(shared_shards)


def per_device(
    tokens,
    doc_ids,
    norm1_gain,
    norm1_bias,
    query_weight,
    query_bias,
    keyval_weight,
    value_bias,
    out_weight,
    out_bias,
    norm2_gain,
    norm2_bias,
    up_weight,
    up_bias,
    down_weight,
    down_bias,
    grad_out,
):
    micro_count = doc_ids.shape[0]
    seq_len = doc_ids.shape[1]
    head_dim = value_bias.shape[0]
    score_scale = head_dim ** (-0.5)
    params = {
        "norm1_gain": norm1_gain.astype(jnp.float32),
        "norm1_bias": norm1_bias.astype(jnp.float32),
        "query_weight": query_weight,
        "query_bias": query_bias.astype(jnp.float32),
        "keyval_weight": keyval_weight,
        "value_bias": value_bias.astype(jnp.float32),
        "out_weight": out_weight,
        "out_bias": out_bias.astype(jnp.float32),
        "norm2_gain": norm2_gain.astype(jnp.float32),
        "norm2_bias": norm2_bias.astype(jnp.float32),
        "up_weight": up_weight,
        "up_bias": up_bias.astype(jnp.float32),
        "down_weight": down_weight,
        "down_bias": down_bias.astype(jnp.float32),
    }
    results = []
    input_grads = []
    running = None
    for micro_index in range(micro_count):
        seq_rows = tokens[micro_index * seq_len : (micro_index + 1) * seq_len].astype(jnp.float32)
        cotangent = grad_out[micro_index * seq_len : (micro_index + 1) * seq_len].astype(
            jnp.float32
        )
        result, kept_state = forward_block(
            seq_rows, doc_ids[micro_index], params, score_scale, head_dim
        )
        results.append(result.astype(jnp.bfloat16))
        grad_input, grad_terms = backward_block(
            seq_rows, cotangent, kept_state, params, score_scale, head_dim
        )
        input_grads.append(grad_input.astype(jnp.bfloat16))
        if running is None:
            running = grad_terms
        else:
            running = tuple((current + incoming for current, incoming in zip(running, grad_terms)))
    running = reduce_once(running)
    return (
        jnp.concatenate(results, axis=0),
        jnp.concatenate(input_grads, axis=0),
        running[4],
        running[5],
        running[0],
        running[2],
        running[12],
        running[13],
        running[10],
        running[6],
        running[7],
        running[8],
        running[1],
        running[3],
        running[11],
        running[9],
    )


def solution(mesh):
    return jax.shard_map(
        per_device,
        mesh=mesh,
        in_specs=(
            P("dp", None),
            P("dp", None),
            P(),
            P(),
            P(None, "tp"),
            P("tp"),
            P(),
            P(),
            P("tp", None),
            P(),
            P(),
            P(),
            P(None, "tp"),
            P("tp"),
            P("tp", None),
            P(),
            P("dp", None),
        ),
        out_specs=(
            P("dp", None),
            P("dp", None),
            P("dp"),
            P("dp"),
            P("dp", "tp"),
            P(("tp", "dp")),
            P(("dp", "tp"), None),
            P(("dp", "tp")),
            P("tp", "dp"),
            P("dp"),
            P("dp"),
            P("dp"),
            P("dp", "tp"),
            P(("tp", "dp")),
            P("tp", "dp"),
            P("dp"),
        ),
        check_vma=False,
    )
```

profile of v0, /device:TPU:0, one launch (start us, length us, event | category | flops | bytes accessed | tf_op | source)
XLA Modules:
  0.0 1856.1 jit_solution(11825210403797541873)
XLA Ops:
  9.2 3.1 convert_reduce_fusion.5
  13.7 4.6 fusion.48
  22.7 2.4 add_convert_fusion.13
  25.1 7.5 fusion.170
  32.7 8.0 fusion.8
  40.7 7.9 fusion.101
  48.6 4.4 convolution_convert_fusion.5
  53.8 157.1 %all-reduce.17.cloned.1.call-done = bf16[1024,2048]{1,0:T(8,128)(2,1)} async-done(((bf16[1024,2048]{1,0:T(8,128)(2,1)}), bf16[1024,2048]{1,0:T(8,128)(2,1)}) %all-reduce.17.cloned.1.call-update) | async-done | bytes 4194320 | tf_op jit(solution)/shard_map/psum | solution.py:59
  210.9 6.2 fusion.71
  218.3 3.3 fusion.29
  221.7 2.4 add_convert_fusion.12
  225.4 7.5 fusion.171
  232.9 8.0 fusion.9
  240.9 7.9 fusion.100
  249.8 4.4 convolution_convert_fusion.3
  254.4 154.0 %all-reduce.19.cloned.1.call-done = bf16[1024,2048]{1,0:T(8,128)(2,1)} async-done(((bf16[1024,2048]{1,0:T(8,128)(2,1)}), bf16[1024,2048]{1,0:T(8,128)(2,1)}) %all-reduce.19.cloned.1.call-update) | async-done | bytes 4194320 | tf_op jit(solution)/shard_map/psum | solution.py:59
  408.4 8.8 multiply_reduce_fusion.1
  417.2 4.0 multiply_reduce_fusion
  421.3 15.1 fusion.162
  436.4 21.1 %convert_reduce_fusion.8 = (f32[2048]{0:T(1024)}, bf16[1024,2048]{1,0:T(8,128)(2,1)}) fusion(f32[1024,2048]{1,0:T(8,128)} %fusion.162, f32[2048]{0:T(1024)S(1)} %convert_element_type.317, bf16[2048,2048]{1,0:T(8,128)(2,1)} %param.31, bf16[2048,2048]{1,0:T(8,128)(2,1)} %param.33), kind=kOutput, calls=%fused_computation.106 | convolution fusion | flops 8638167040 | bytes 25182208 | tf_op jit(solution)/shard_map/dot_general | solution.py:104
  457.5 14.1 convolution_convert_fusion
  471.6 13.9 fusion.161
  485.5 19.2 %convert_reduce_fusion.9 = (f32[2048]{0:T(1024)}, bf16[1024,2048]{1,0:T(8,128)(2,1)S(1)}) fusion(f32[1024,2048]{1,0:T(8,128)} %fusion.161, f32[2048]{0:T(1024)S(1)} %convert_element_type.317, bf16[2048,2048]{1,0:T(8,128)(2,1)} %param.31, bf16[2048,2048]{1,0:T(8,128)(2,1)} %param.33), kind=kOutput, calls=%fused_computation.107 | convolution fusion | flops 8638167040 | bytes 25182208 | tf_op jit(solution)/shard_map/dot_general | solution.py:104
  506.6 12.8 convolution_convert_fusion.1
  520.2 289.9 %all-reduce.23.cloned.1.call-done = (bf16[1024,2048]{1,0:T(8,128)(2,1)}, bf16[1024,2048]{1,0:T(8,128)(2,1)}) async-done(((bf16[1024,2048]{1,0:T(8,128)(2,1)}, bf16[1024,2048]{1,0:T(8,128)(2,1)}), (bf16[1024,2048]{1,0:T(8,128)(2,1)}, bf16[1024,2048]{1,0:T(8,128)(2,1)})) %all-reduce.23.cloned.1.call-update) | async-done | bytes 8388624 | tf_op jit(solution)/shard_map/psum | solution.py:109
  810.2 12.3 fusion.33
  823.3 12.4 fusion.54
  835.7 14.1 fusion.168
  849.8 5.9 fusion.105
  859.7 3.7 add_convert_fusion.10
  863.5 9.8 fusion.135
  873.3 26.1 %convert_reduce_fusion.10 = (f32[128,4]{0,1:T(4,128)}, bf16[128,4,1024]{2,0,1:T(8,128)(2,1)}) fusion(f32[1024,1024,4]{1,0,2:T(8,128)} %fusion.135, f32[4,1024,1024]{1,2,0:T(8,128)} %get-tuple-element.75, f32[4,1024]{1,0:T(4,128)S(1)} %log_add_fusion, f32[1024,256]{1,0:T(8,128)} %copy-done.32), kind=kOutput, calls=%fused_computation.155 | convolution fusion | flops 1104679424 | bytes 68454400 | tf_op jit(solution)/shard_map/hst,td->shd/dot_general | solution.py:131
  899.4 5.9 fusion.102
  906.3 8.0 fusion.138
  914.4 24.0 %convert_reduce_fusion.11 = (f32[128,4]{0,1:T(4,128)}, bf16[128,4,1024]{2,0,1:T(8,128)(2,1)S(1)}) fusion(f32[1024,1024,4]{1,0,2:T(8,128)} %fusion.138, f32[4,1024,1024]{1,2,0:T(8,128)} %get-tuple-element.73, f32[4,1024]{1,0:T(4,128)S(1)} %log_add_fusion.1, f32[1024,256]{1,0:T(8,128)S(1)} %copy-done.31), kind=kOutput, calls=%fused_computation.156 | convolution fusion | flops 1104679424 | bytes 68454400 | tf_op jit(solution)/shard_map/hst,td->shd/dot_general | solution.py:131
  938.3 5.0 fusion.176
  943.4 3.7 add_convert_fusion.11
  947.2 20.6 %fusion.85 = f32[2048,2048]{1,0:T(8,128)} fusion(bf16[2048,2048]{1,0:T(8,128)(2,1)} %param.33, f32[1024,2048]{1,0:T(8,128)} %fusion.161, f32[2048]{0:T(1024)S(1)} %convert_element_type.317), kind=kOutput, calls=%fused_computation.150 | convolution fusion | flops 8610906112 | bytes 29368320 | tf_op jit(solution)/shard_map/dot_general | solution.py:103
  967.8 21.9 %add_convert_fusion = bf16[2048,2048]{1,0:T(8,128)(2,1)} fusion(f32[2048,2048]{1,0:T(8,128)} %fusion.85, bf16[2048,2048]{1,0:T(8,128)(2,1)} %param.33, f32[1024,2048]{1,0:T(8,128)} %fusion.162, f32[2048]{0:T(1024)S(1)} %convert_element_type.317), kind=kOutput, calls=%fused_computation.14 | convolution fusion | flops 8619294720 | bytes 37756928 | tf_op jit(solution)/shard_map/dot_general | solution.py:103
  990.4 17.5 fusion.160
  1007.9 17.5 add_convert_fusion.1
  1025.4 16.5 convolution_convert_fusion.2
  1041.9 16.0 convolution_convert_fusion.4
  1058.0 26.8 %fusion.123 = bf16[1024,128]{0,1:T(8,128)(2,1)S(1)} fusion(bf16[1024,4,128]{0,2,1:T(8,128)(2,1)S(1)} %bitcast.204, f32[1024,1024,4]{1,0,2:T(8,128)} %fusion.135, f32[4,1024,1024]{1,2,0:T(8,128)} %get-tuple-element.75, f32[4,1024]{1,0:T(4,128)S(1)} %copy-done.38), kind=kOutput, calls=%fused_computation.179 | convolution fusion | flops 1103238144 | bytes 34881536 | tf_op jit(solution)/shard_map/hst,shd->td/dot_general | solution.py:135
  1084.9 24.9 %fusion.122 = bf16[1024,128]{0,1:T(8,128)(2,1)S(1)} fusion(bf16[1024,4,128]{0,2,1:T(8,128)(2,1)S(1)} %bitcast.202, f32[1024,1024,4]{1,0,2:T(8,128)} %fusion.138, f32[4,1024,1024]{1,2,0:T(8,128)} %get-tuple-element.73, f32[4,1024]{1,0:T(4,128)S(1)} %copy-done.36), kind=kOutput, calls=%fused_computation.178 | convolution fusion | flops 1103238144 | bytes 34881536 | tf_op jit(solution)/shard_map/hst,shd->td/dot_general | solution.py:135
  1109.8 7.5 fusion.175
  1119.8 9.6 convert_reduce_fusion.12
  1129.5 7.0 add_convert_fusion.3
  1136.4 3.4 convert_reduce_fusion.13
  1139.8 3.4 add_convert_fusion.5
  1145.8 5.4 convert_reduce_fusion.6
  1151.2 43.5 %all-reduce.3 = f32[128]{0:T(128)S(1)} all-reduce(f32[128]{0:T(128)S(1)} %add.343), channel_id=7, replica_groups=mesh['dp'=8,'tp'=4] {'dp','tp'}, use_global_device_ids=true, to_apply=%region_43.44.clone | all-reduce | flops 128 | bytes 1024
  1195.4 3.6 fusion.126
  1199.0 4.9 convolution_add_fusion
  1207.6 2.7 convert_element_type.392
  1210.3 2.8 convert_element_type.386
  1213.1 496.3 %all-reduce.21.cloned.1.call-done = (bf16[1024,2048]{1,0:T(8,128)(2,1)}, bf16[1024,2048]{1,0:T(8,128)(2,1)}, bf16[1024,2048]{1,0:T(8,128)(2,1)}, bf16[1024,2048]{1,0:T(8,128)(2,1)}) async-done(((bf16[1024,2048]{1,0:T(8,128)(2,1)}, bf16[1024,2048]{1,0:T(8,128)(2,1)}, bf16[1024,2048]{1,0:T(8,128)(2,1)}, bf16[1024,2048]{1,0:T(8,128)(2,1)}), (bf16[1024,2048]{1,0:T(8,128)(2,1)}, bf16[1024,2048]{1,0:T(8,128)(2,1)}, ...) | async-done | bytes 16777232 | tf_op jit(solution)/shard_map/psum | solution.py:68
  1709.5 8.8 fusion.49
  1720.2 15.9 fusion.55
  1736.2 25.3 %all-reduce.9 = (bf16[2048]{0:T(1024)(128)(2,1)S(1)}, bf16[2048]{0:T(1024)(128)(2,1)S(1)}, bf16[512]{0:T(512)(128)(2,1)S(1)}, bf16[2048]{0:T(1024)(128)(2,1)S(1)...) all-reduce(bf16[2048]{0:T(1024)(128)(2,1)S(1)} %add_convert_fusion., ...), channel_id=2, replica_groups=mesh['dp'=8,'tp'=4] {'dp'}, use_global_device_ids=true, to_apply=%region_32.33.clone | all-reduce | flops 14848 | bytes 59392
  1766.5 16.8 add_convert_fusion.4
  1783.2 8.6 pad_maximum_fusion.1
  1791.8 8.7 pad_maximum_fusion
  1800.5 48.8 %reduce-scatter.8.cloned.1.call-done = f32[64,256]{1,0:T(8,128)} async-done(((f32[2048,256]{1,0:T(8,128)}), f32[64,256]{1,0:T(8,128)}) %reduce-scatter.8.cloned.1.call-update) | async-done | bytes 65552 | tf_op jit(solution)/shard_map/reduce_scatter | solution.py:210
  (272 shorter events, 36.1 us)
Async XLA Ops:
  7.2 41.4 %copy-start = (bf16[512,2048]{1,0:T(8,128)(2,1)S(1)}, bf16[512,2048]{1,0:T(8,128)(2,1)}, u32[]{:S(2)}) copy-start(bf16[512,2048]{1,0:T(8,128)(2,1)} %param.25) | copy-start | bytes 6291460
  7.2 11.7 copy-start.63
  7.2 203.7 %all-reduce.17.cloned.1.call-start = ((), (), s32[]{:S(2)}) async-start(), calls=%async_computation.5 | async-start | bytes 8388608 | tf_op jit(solution)/shard_map/psum | solution.py:59
  7.3 12.3 copy-start.2
  8.1 232.8 %copy-start.71 = (f32[128]{0:T(128)}, f32[128]{0:T(128)S(1)}, u32[]{:S(2)}) copy-start(f32[128]{0:T(128)S(1)} %convert_element_type.304) | copy-start | bytes 1540
  12.3 9.1 copy-start.39
  13.0 204.1 %copy-start.33 = (f32[2048]{0:T(1024)}, f32[2048]{0:T(1024)S(1)}, u32[]{:S(2)}) copy-start(f32[2048]{0:T(1024)S(1)} %convert_element_type.301) | copy-start | bytes 24580
  22.7 18.0 copy-start.30
  32.7 8.0 copy-start.43
  53.1 355.4 %all-reduce.19.cloned.1.call-start = ((), (), s32[]{:S(2)}) async-start(), calls=%async_computation.6 | async-start | bytes 8388608 | tf_op jit(solution)/shard_map/psum | solution.py:59
  53.2 168.5 %copy-start.41 = (f32[1024]{0:T(1024)}, f32[1024]{0:T(1024)S(1)}, u32[]{:S(2)}) copy-start(f32[1024]{0:T(1024)S(1)} %broadcast_multiply_fusion.1) | copy-start | bytes 12292
  210.9 10.8 copy-start.76
  224.1 8.8 copy-start.28
  225.4 15.5 copy-start.32
  254.3 555.9 %all-reduce.23.cloned.1.call-start = ((), (), s32[]{:S(2)}) async-start(), calls=%async_computation.13 | async-start | bytes 16777216 | tf_op jit(solution)/shard_map/psum | solution.py:109
  254.4 217.2 %copy-start.61 = (f32[2048]{0:T(1024)}, f32[2048]{0:T(1024)S(1)}, u32[]{:S(2)}) copy-start(f32[2048]{0:T(1024)S(1)} %convert_element_type.315) | copy-start | bytes 24580
  408.4 8.8 copy-start.6
  421.3 50.3 %slice-start = ((s8[8388608]{0:T(1024)(128)(4,1)}), s8[4194304]{0:T(1024)(128)(4,1)S(1)}, s32[]{:S(2)}) async-start(s8[8388608]{0:T(1024)(128)(4,1)} %bitcast.191), calls=%async_computation.14 | async-start | bytes 8388608
  436.4 35.2 %slice-start.1 = ((s8[8388608]{0:T(1024)(128)(4,1)}), s8[4194304]{0:T(1024)(128)(4,1)S(1)}, s32[]{:S(2)}) async-start(s8[8388608]{0:T(1024)(128)(4,1)} %bitcast.191), calls=%async_computation.15 | async-start | bytes 8388608
  457.5 14.1 copy-start.3
  519.5 684.5 %reduce-scatter.10.cloned.1.call-start = ((), (), s32[]{:S(2)}) async-start(), calls=%async_computation.9 | async-start | bytes 2359296 | tf_op jit(solution)/shard_map/reduce_scatter | solution.py:202
  520.2 394.2 %copy-start.35 = (f32[4,1024]{1,0:T(4,128)}, f32[4,1024]{1,0:T(4,128)S(1)}, u32[]{:S(2)}) copy-start(f32[4,1024]{1,0:T(4,128)S(1)} %log_add_fusion.1) | copy-start | bytes 49156
  520.2 353.1 %copy-start.37 = (f32[4,1024]{1,0:T(4,128)}, f32[4,1024]{1,0:T(4,128)S(1)}, u32[]{:S(2)}) copy-start(f32[4,1024]{1,0:T(4,128)S(1)} %log_add_fusion) | copy-start | bytes 49156
  810.2 12.3 copy-start.4
  810.2 12.4 copy-start.7
  810.2 12.4 copy-start.12
  810.2 13.1 copy-start.13
  810.2 25.5 %slice-start.2 = ((s8[8388608]{0:T(1024)(128)(4,1)}), s8[4194304]{0:T(1024)(128)(4,1)S(1)}, s32[]{:S(2)}) async-start(s8[8388608]{0:T(1024)(128)(4,1)} %bitcast.193), calls=%async_computation.16 | async-start | bytes 8388608
  823.3 12.4 slice-start.3
  863.4 342.3 %reduce-scatter.6.cloned.1.call-start = ((), (), s32[]{:S(2)}) async-start(), calls=%async_computation.7 | async-start | bytes 2359296 | tf_op jit(solution)/shard_map/reduce_scatter | solution.py:170
  947.1 260.4 %reduce-scatter.14.cloned.1.call-start = ((), (), s32[]{:S(2)}) async-start(), calls=%async_computation.11 | async-start | bytes 9437184 | tf_op jit(solution)/shard_map/reduce_scatter | solution.py:205
  989.7 220.5 %reduce-scatter.12.cloned.1.call-start = ((), (), s32[]{:S(2)}) async-start(), calls=%async_computation.10 | async-start | bytes 9437184 | tf_op jit(solution)/shard_map/reduce_scatter | solution.py:173
  990.4 17.5 copy-start.8
  1025.4 684.0 %all-reduce.21.cloned.1.call-start = ((), (), s32[]{:S(2)}) async-start(), calls=%async_computation.12 | async-start | bytes 33554432 | tf_op jit(solution)/shard_map/psum | solution.py:68
  1041.9 16.0 copy-start.29
  1041.9 16.0 copy-start.38
  1058.0 26.9 %copy-start.27 = (bf16[1024,512]{0,1:T(8,128)(2,1)S(1)}, bf16[1024,512]{0,1:T(8,128)(2,1)}, u32[]{:S(2)}) copy-start(bf16[1024,512]{0,1:T(8,128)(2,1)} %copy-done.26) | copy-start | bytes 3145732
  1058.0 26.9 %copy-start.36 = (f32[4,1024]{1,0:T(4,128)S(1)}, f32[4,1024]{1,0:T(4,128)}, u32[]{:S(2)}) copy-start(f32[4,1024]{1,0:T(4,128)} %copy-done.35) | copy-start | bytes 49156
  1084.9 24.9 %copy-start.83 = (bf16[128,4,1024]{2,0,1:T(8,128)(2,1)S(1)}, bf16[128,4,1024]{2,0,1:T(8,128)(2,1)}, u32[]{:S(2)}) copy-start(bf16[128,4,1024]{2,0,1:T(8,128)(2,1)} %get-tuple-element.79) | copy-start | bytes 3145732
  1119.7 9.7 copy-start.20
  1119.8 16.7 slice-start.4
  1119.8 16.6 slice-start.5
  1119.8 16.6 slice-start.6
  1143.3 52.0 %copy-start.73 = (f32[128,4]{0,1:T(4,128)S(1)}, f32[128,4]{0,1:T(4,128)}, u32[]{:S(2)}) copy-start(f32[128,4]{0,1:T(4,128)} %get-tuple-element.78) | copy-start | bytes 6148
  1143.3 52.0 %copy-start.74 = (f32[128,4]{0,1:T(4,128)S(1)}, f32[128,4]{0,1:T(4,128)}, u32[]{:S(2)}) copy-start(f32[128,4]{0,1:T(4,128)} %get-tuple-element.76) | copy-start | bytes 6148
  1143.3 52.0 %copy-start.55 = (f32[2048]{0:T(1024)S(1)}, f32[2048]{0:T(1024)}, u32[]{:S(2)}) copy-start(f32[2048]{0:T(1024)} %get-tuple-element.41) | copy-start | bytes 24580
  1143.3 52.0 %copy-start.56 = (f32[2048]{0:T(1024)S(1)}, f32[2048]{0:T(1024)}, u32[]{:S(2)}) copy-start(f32[2048]{0:T(1024)} %get-tuple-element.42) | copy-start | bytes 24580
  1143.3 52.0 %copy-start.57 = (f32[2048]{0:T(1024)S(1)}, f32[2048]{0:T(1024)}, u32[]{:S(2)}) copy-start(f32[2048]{0:T(1024)} %get-tuple-element.18) | copy-start | bytes 24580
  1143.3 52.0 %copy-start.58 = (f32[2048]{0:T(1024)S(1)}, f32[2048]{0:T(1024)}, u32[]{:S(2)}) copy-start(f32[2048]{0:T(1024)} %get-tuple-element.25) | copy-start | bytes 24580
  1143.4 52.0 %copy-start.59 = (f32[2048]{0:T(1024)S(1)}, f32[2048]{0:T(1024)}, u32[]{:S(2)}) copy-start(f32[2048]{0:T(1024)} %get-tuple-element.60) | copy-start | bytes 24580
  1143.4 52.0 %copy-start.60 = (f32[2048]{0:T(1024)S(1)}, f32[2048]{0:T(1024)}, u32[]{:S(2)}) copy-start(f32[2048]{0:T(1024)} %get-tuple-element.62) | copy-start | bytes 24580
  1143.4 706.0 %reduce-scatter.8.cloned.1.call-start = ((), (), s32[]{:S(2)}) async-start(), calls=%async_computation.8 | async-start | bytes 2162688 | tf_op jit(solution)/shard_map/reduce_scatter | solution.py:210
  1199.0 510.4 %copy-start.34 = (f32[2048]{0:T(1024)S(1)}, f32[2048]{0:T(1024)}, u32[]{:S(2)}) copy-start(f32[2048]{0:T(1024)} %copy-done.33) | copy-start | bytes 24580
  1199.0 510.4 %copy-start.40 = (f32[1024]{0:T(1024)S(1)}, f32[1024]{0:T(1024)}, u32[]{:S(2)}) copy-start(f32[1024]{0:T(1024)} %copy-done.39) | copy-start | bytes 12292
  1199.0 510.4 %copy-start.42 = (f32[1024]{0:T(1024)S(1)}, f32[1024]{0:T(1024)}, u32[]{:S(2)}) copy-start(f32[1024]{0:T(1024)} %copy-done.41) | copy-start | bytes 12292
  1709.4 8.9 copy-start.52
  1709.4 8.9 copy-start.54
  1709.4 8.9 copy-start.5
  1709.4 8.9 copy-start.9
  1709.4 9.6 copy-start.10
  1709.4 10.7 copy-start.11
  1709.5 10.7 copy-start.46
  1709.5 10.7 copy-start.48
  1791.8 57.5 %copy-start.1 = (bf16[512,2048]{1,0:T(8,128)(2,1)S(1)}, bf16[512,2048]{1,0:T(8,128)(2,1)}, u32[]{:S(2)}) copy-start(bf16[512,2048]{1,0:T(8,128)(2,1)} %param.25) | copy-start | bytes 6291460
  (41 other events, 176.6 us)
Sparse Core Ops, SparseCore 0:
  53.2 157.6 all-reduce.16
  254.4 153.9 all-reduce.18
  519.6 290.5 all-reduce.22
  863.5 40.2 reduce-scatter.9
  947.3 40.2 reduce-scatter.5
  990.9 71.2 reduce-scatter.13
  1066.0 71.2 reduce-scatter.11
  1143.4 565.9 all-reduce.20
  1712.2 137.0 reduce-scatter.7
where the time goes:
time: 1870 us; the launch traced here: 1860 us
  waiting for transfers between devices  1150 us (61%)
  matrix products  441 us (24%)
  other arithmetic  170 us (9%)
  blocking collectives  68.7 us (4%)
    psum x1, waiting for transfers between devices, forward_block(): summed = lax.psum(down_part.astype(jnp.bfloat16), 'tp').astype(jnp.float32)  496 us
    psum x2, waiting for transfers between devices, forward_block(): lax.psum(partial_value.astype(jnp.bfloat16), 'tp').astype(jnp.float32)  311 us
    psum x1, waiting for transfers between devices, backward_block(): lax.psum(partial2.astype(jnp.bfloat16), 'tp').astype(jnp.float32)  290 us
    unnamed x2, blocking collectives  68.7 us
    dot_general x2, matrix products, backward_block(): jnp.einsum('hst,shd->td', grad_scores, heads_q, preferred_element_type=jn...  51.7 us
    dot_general x2, matrix products, backward_block(): jnp.einsum('hst,td->shd', grad_scores, keys_low, preferred_element_type=j...  50 us
    reduce_sum x4, other arithmetic, layer_norm(): return center * lax.rsqrt(spread + 1e-05) * gain_vec + shift_vec  49.5 us
    reduce_scatter x1, waiting for transfers between devices, reduce_once(): lax.psum_scatter(grad_terms[12], ('dp', 'tp'), scatter_dimension=0, tiled...  48.8 us
  transfers between devices with their start and end apart: 9, of which 5 were waited for; matrix products, arithmetic and copies ran while one was open for 20% of the time, Pallas kernels for 0%

commit v1 on v0

v1 whole, which is shorter than its diff:
```python
import functools
import math

import jax
import jax.numpy as jnp
from jax import lax
from jax.experimental import pallas as pl
from jax.experimental.pallas import tpu as pltpu
from jax.sharding import PartitionSpec as P

F32 = jnp.float32
BF16 = jnp.bfloat16
NEG = -1e30
EPS = 1e-05
GELU_A = math.sqrt(2.0 / math.pi)
GELU_B = 0.044715
LOG2E = math.log2(math.e)
VMEM_LIMIT = 56 * 1024 * 1024


def dot_nn(a, b):
    return lax.dot_general(a, b, (((1,), (0,)), ((), ())), preferred_element_type=F32)


def dot_nt(a, b):
    return lax.dot_general(a, b, (((1,), (1,)), ((), ())), preferred_element_type=F32)


def dot_tn(a, b):
    return lax.dot_general(a, b, (((0,), (0,)), ((), ())), preferred_element_type=F32)


def call(kernel, grid, in_specs, out_specs, out_shape, scratch=(), prefetch=0, flops=0, nbytes=0, trans=0, name=None):
    return pl.pallas_call(
        kernel,
        grid_spec=pltpu.PrefetchScalarGridSpec(
            num_scalar_prefetch=prefetch,
            grid=grid,
            in_specs=in_specs,
            out_specs=out_specs,
            scratch_shapes=list(scratch),
        ),
        out_shape=out_shape,
        compiler_params=pltpu.CompilerParams(
            dimension_semantics=("arbitrary",) * len(grid), vmem_limit_bytes=VMEM_LIMIT
        ),
        cost_estimate=pl.CostEstimate(flops=flops, bytes_accessed=nbytes, transcendentals=trans),
        name=name,
    )


def whole(shape):
    return pl.BlockSpec(shape, lambda *_: (0,) * len(shape), pipeline_mode=pl.Buffered(1))


def shape_of(shape, dtype):
    return jax.ShapeDtypeStruct(shape, dtype)


def ln_kernel(x_ref, g_ref, b_ref, o_ref):
    x = x_ref[...].astype(F32)
    c = x - jnp.mean(x, axis=-1, keepdims=True)
    v = jnp.mean(c * c, axis=-1, keepdims=True)
    o_ref[...] = (c * lax.rsqrt(v + EPS) * g_ref[...].astype(F32) + b_ref[...].astype(F32)).astype(BF16)


def layer_norm(x, gain, bias):
    t, d = x.shape
    br = 256
    return call(
        ln_kernel,
        (t // br,),
        [pl.BlockSpec((br, d), lambda i: (i, 0)), whole((1, d)), whole((1, d))],
        pl.BlockSpec((br, d), lambda i: (i, 0)),
        shape_of((t, d), BF16),
        flops=8 * t * d,
        nbytes=4 * t * d,
        name="norm1",
    )(x, gain, bias)


def attn_fwd_kernel(scale, qb, q_ref, k_ref, vt_ref, dcol_ref, drow_ref, o_ref, mask):
    s = q_ref.shape[0]
    reach = s // 2

    def span(j):
        start = max(0, j * qb - reach)
        return start, (j + 1) * qb

    @pl.when(pl.program_id(1) == 0)
    def _():
        for j in range(s // qb):
            lo, hi = span(j)
            kpos = lo + lax.broadcasted_iota(jnp.int32, (hi - lo, qb), 0)
            qpos = j * qb + lax.broadcasted_iota(jnp.int32, (hi - lo, qb), 1)
            ok = (dcol_ref[pl.ds(lo, hi - lo), :] == drow_ref[0, :, pl.ds(j * qb, qb)]) & (kpos <= qpos)
            mask[j, pl.ds(0, hi - lo), :] = jnp.where(ok, 0.0, NEG)

    for j in range(s // qb):
        lo, hi = span(j)
        q = q_ref[pl.ds(j * qb, qb), :]
        sc = dot_nt(k_ref[pl.ds(lo, hi - lo), :], q) + mask[j, pl.ds(0, hi - lo), :]
        top = jnp.max(sc, axis=0, keepdims=True)
        p = jnp.exp2((sc - top) * (scale * LOG2E))
        total = jnp.sum(p, axis=0, keepdims=True)
        o = dot_nn(vt_ref[:, pl.ds(lo, hi - lo)], p.astype(BF16)) / total
        o_ref[pl.ds(j * qb, qb), :] = o.T.astype(BF16)


def attn_fwd(q, k, vt, dcol, drow, seq, hd):
    t, width = q.shape
    heads = width // hd
    qb = 256
    wins = t // seq
    return call(
        functools.partial(attn_fwd_kernel, hd**-0.5, qb),
        (wins, heads),
        [
            pl.BlockSpec((seq, hd), lambda w, h: (w, h)),
            pl.BlockSpec((seq, hd), lambda w, h: (w, 0)),
            pl.BlockSpec((hd, seq), lambda w, h: (0, w)),
            pl.BlockSpec((seq, 1), lambda w, h: (w, 0)),
            pl.BlockSpec((1, 1, seq), lambda w, h: (w, 0, 0)),
        ],
        pl.BlockSpec((seq, hd), lambda w, h: (w, h)),
        shape_of((t, width), BF16),
        scratch=[pltpu.VMEM((seq // qb, seq // 2 + qb, qb), F32)],
        flops=4 * t * seq * width * 5 // 8,
        nbytes=4 * t * width + 4 * t * hd,
        trans=t * seq * heads * 5 // 8,
        name="attn_fwd",
    )(q, k, vt, dcol, drow)


def proj_ln_kernel(att_ref, w_ref, x_ref, ob_ref, g_ref, b_ref, h_ref, n_ref):
    att = att_ref[...]
    mixed = jnp.concatenate([dot_nn(att, w_ref[i]) for i in range(w_ref.shape[0])], axis=1)
    h = x_ref[...].astype(F32) + mixed + ob_ref[...].astype(F32)
    h_ref[...] = h
    c = h - jnp.mean(h, axis=-1, keepdims=True)
    v = jnp.mean(c * c, axis=-1, keepdims=True)
    n_ref[...] = (c * lax.rsqrt(v + EPS) * g_ref[...].astype(F32) + b_ref[...].astype(F32)).astype(BF16)


def proj_ln(att, w, x, out_bias, gain, bias):
    r, width = att.shape
    d = x.shape[1]
    br = min(128, r)
    row = pl.BlockSpec((br, d), lambda i: (i, 0))
    return call(
        proj_ln_kernel,
        (r // br,),
        [pl.BlockSpec((br, width), lambda i: (i, 0)), whole(w.shape), row] + [whole((1, d))] * 3,
        [row, row],
        [shape_of((r, d), F32), shape_of((r, d), BF16)],
        flops=2 * r * width * d,
        nbytes=2 * width * d + 10 * r * d,
        name="proj_ln",
    )(att, w, x, out_bias, gain, bias)


def up_kernel(n_ref, w_ref, b_ref, da_ref, act_ref, gb_ref, gs_ref):
    v = dot_nn(n_ref[...], w_ref[...]) + b_ref[...].astype(F32)
    v2 = v * v
    t = jnp.tanh(GELU_A * v * (1.0 + GELU_B * v2))
    half = 0.5 * (1.0 + t)
    act_ref[...] = (v * half).astype(BF16)
    slope = half + 0.5 * v * (1.0 - t * t) * (GELU_A * (1.0 + 3.0 * GELU_B * v2))
    gb = (da_ref[...].astype(F32) * slope).astype(BF16)
    gb_ref[...] = gb
    gs_ref[...] = jnp.sum(gb.astype(F32), axis=0, keepdims=True)


def ffn_up(n, w, b, da):
    r, d = n.shape
    u = w.shape[1]
    bn = 256
    col = pl.BlockSpec((r, bn), lambda j: (0, j))
    return call(
        up_kernel,
        (u // bn,),
        [whole((r, d)), pl.BlockSpec((d, bn), lambda j: (0, j)), pl.BlockSpec((1, bn), lambda j: (0, j)), col],
        [col, col, pl.BlockSpec((1, bn), lambda j: (0, j))],
        [shape_of((r, u), BF16), shape_of((r, u), BF16), shape_of((1, u), F32)],
        flops=2 * r * d * u,
        nbytes=2 * d * u + 6 * r * u + 2 * r * d,
        trans=r * u,
        name="ffn_up",
    )(n, w, b, da)


def norm2_back_kernel(count, *refs):
    parts = refs[: count]
    h_ref, go_ref, g_ref, w_ref, gh_ref, gm_ref, ga_ref, sums_ref = refs[count:]

    @pl.when(pl.program_id(0) == 0)
    def _():
        sums_ref[...] = jnp.zeros_like(sums_ref)

    gn = parts[0][...].astype(F32)
    for part in parts[1:]:
        gn = gn + part[...].astype(F32)
    h = h_ref[...]
    c = h - jnp.mean(h, axis=-1, keepdims=True)
    inv = lax.rsqrt(jnp.mean(c * c, axis=-1, keepdims=True) + EPS)
    nrm = c * inv
    u = gn * g_ref[...].astype(F32)
    cot = go_ref[...].astype(F32)
    gh = cot + inv * (u - jnp.mean(u, axis=-1, keepdims=True) - nrm * jnp.mean(u * nrm, axis=-1, keepdims=True))
    gh_ref[...] = gh
    gm = gh.astype(BF16)
    gm_ref[...] = gm
    cols = w_ref.shape[2]
    ga = dot_nt(gm[:, :cols], w_ref[0])
    for i in range(1, w_ref.shape[0]):
        ga = ga + dot_nt(gm[:, i * cols : (i + 1) * cols], w_ref[i])
    ga_ref[...] = ga.astype(BF16)
    sums_ref[0:1, :] += jnp.sum(gn * nrm, axis=0, keepdims=True)
    sums_ref[1:2, :] += jnp.sum(gn, axis=0, keepdims=True)
    sums_ref[2:3, :] += jnp.sum(gh, axis=0, keepdims=True)
    sums_ref[3:4, :] += jnp.sum(cot, axis=0, keepdims=True)


def norm2_back(parts, h, go, gain, w):
    r, d = h.shape
    width = w.shape[1]
    br = min(128, r)
    row = pl.BlockSpec((br, d), lambda i: (i, 0))
    wide = pl.BlockSpec((br, width), lambda i: (i, 0))
    return call(
        functools.partial(norm2_back_kernel, len(parts)),
        (r // br,),
        [row] * len(parts) + [row, row, whole((1, d)), whole(w.shape)],
        [row, row, wide, pl.BlockSpec((8, d), lambda i: (0, 0))],
        [shape_of((r, d), F32), shape_of((r, d), BF16), shape_of((r, width), BF16), shape_of((8, d), F32)],
        flops=2 * r * width * d,
        nbytes=2 * width * d + 20 * r * d,
        name="norm2_back",
    )(*parts, h, go, gain, w)


def attn_bwd_kernel(scale, qb, reach, row0_ref, q_ref, go_ref, k_ref, v_ref, kt_ref, dcol_ref, drow_ref, gq_ref, gk_ref, gv_ref, mask):
    rows = q_ref.shape[0]
    span = reach + qb
    first = pl.program_id(0) == 0

    def start(j):
        at = jnp.maximum(row0_ref[0] + j * qb - reach, 0)
        return pl.multiple_of(at, qb)

    @pl.when(first)
    def _():
        gk_ref[...] = jnp.zeros_like(gk_ref)
        gv_ref[...] = jnp.zeros_like(gv_ref)
        for j in range(rows // qb):
            lo = start(j)
            kpos = lo + lax.broadcasted_iota(jnp.int32, (span, qb), 0)
            qpos = row0_ref[0] + j * qb + lax.broadcasted_iota(jnp.int32, (span, qb), 1)
            ok = (dcol_ref[pl.ds(lo, span), :] == drow_ref[:, pl.ds(j * qb, qb)]) & (kpos <= qpos)
            mask[j] = jnp.where(ok, 0.0, NEG)

    for j in range(rows // qb):
        lo = start(j)
        q = q_ref[pl.ds(j * qb, qb), :]
        go = go_ref[pl.ds(j * qb, qb), :]
        k = k_ref[pl.ds(lo, span), :]
        sc = dot_nt(k, q) + mask[j]
        top = jnp.max(sc, axis=0, keepdims=True)
        e = jnp.exp2((sc - top) * (scale * LOG2E))
        p = e * (1.0 / jnp.sum(e, axis=0, keepdims=True))
        dp = dot_nt(v_ref[pl.ds(lo, span), :], go)
        pd = p * dp
        delta = jnp.sum(pd, axis=0, keepdims=True)
        ds = ((pd - p * delta) * scale).astype(BF16)
        gk_ref[pl.ds(lo, span), :] += dot_nn(ds, q)
        gv_ref[pl.ds(lo, span), :] += dot_nn(p.astype(BF16), go)
        gq_ref[pl.ds(j * qb, qb), :] = dot_nn(kt_ref[:, pl.ds(lo, span)], ds).T.astype(BF16)


def attn_bwd(row0, q, go, k, v, kt, dcol, drow, hd):
    r, width = q.shape
    s = k.shape[0]
    heads = width // hd
    qb = min(256, r)
    reach = s // 2
    head = pl.BlockSpec((r, hd), lambda h, *_: (0, h))
    keep = pl.BlockSpec((s, hd), lambda h, *_: (0, 0))
    return call(
        functools.partial(attn_bwd_kernel, hd**-0.5, qb, reach),
        (heads,),
        [head, head, whole((s, hd)), whole((s, hd)), whole((hd, s)), whole((s, 1)), whole((1, r))],
        [head, keep, keep],
        [shape_of((r, width), BF16), shape_of((s, hd), F32), shape_of((s, hd), F32)],
        scratch=[pltpu.VMEM((r // qb, reach + qb, qb), F32)],
        prefetch=1,
        flops=10 * r * (reach + qb) * width,
        nbytes=6 * r * width + 16 * s * hd,
        trans=r * (reach + qb) * heads,
        name="attn_bwd",
    )(row0, q, go, k, v, kt, dcol, drow)


def norm1_back_kernel(gq_ref, gkv_ref, wq_ref, wkv_ref, x_ref, gh_ref, g_ref, gt_ref, sums_ref, small_ref):
    @pl.when(pl.program_id(0) == 0)
    def _():
        sums_ref[...] = jnp.zeros_like(sums_ref)
        small_ref[...] = jnp.zeros_like(small_ref)

    gq = gq_ref[...]
    gkv = gkv_ref[...]
    gn = dot_nt(gq, wq_ref[...]) + dot_nt(gkv, wkv_ref[...])
    x = x_ref[...].astype(F32)
    c = x - jnp.mean(x, axis=-1, keepdims=True)
    inv = lax.rsqrt(jnp.mean(c * c, axis=-1, keepdims=True) + EPS)
    nrm = c * inv
    u = gn * g_ref[...].astype(F32)
    gx = inv * (u - jnp.mean(u, axis=-1, keepdims=True) - nrm * jnp.mean(u * nrm, axis=-1, keepdims=True))
    gt_ref[...] = (gh_ref[...] + gx).astype(BF16)
    sums_ref[0:1, :] += jnp.sum(gn * nrm, axis=0, keepdims=True)
    sums_ref[1:2, :] += jnp.sum(gn, axis=0, keepdims=True)
    sums_ref[2:3, :] += jnp.sum(gq.astype(F32), axis=0, keepdims=True)
    small_ref[0:1, :] += jnp.sum(gkv.astype(F32), axis=0, keepdims=True)


def norm1_back(gq, gkv, wq, wkv, x, gh, gain):
    r, d = x.shape
    br = min(128, r)
    row = pl.BlockSpec((br, d), lambda i: (i, 0))
    kvw = gkv.shape[1]
    return call(
        norm1_back_kernel,
        (r // br,),
        [row, pl.BlockSpec((br, kvw), lambda i: (i, 0)), whole(wq.shape), whole(wkv.shape), row, row, whole((1, d))],
        [row, pl.BlockSpec((8, d), lambda i: (0, 0)), pl.BlockSpec((8, kvw), lambda i: (0, 0))],
        [shape_of((r, d), BF16), shape_of((8, d), F32), shape_of((8, kvw), F32)],
        flops=2 * r * d * (gq.shape[1] + kvw),
        nbytes=2 * d * (gq.shape[1] + kvw) + 12 * r * d,
        name="norm1_back",
    )(gq, gkv, wq, wkv, x, gh, gain)


def stage_orders(bits):
    order = list(range(bits))
    return [order, order[1:] + order[:1]]


def block_at(m, p, order):
    nb = len(order)
    b = 0
    for k, bit in enumerate(order):
        b = b + ((((p >> (nb - 1 - k)) & 1) ^ 1 ^ ((m >> (bit + 1)) & 1)) << bit)
    return b


def grad_kernel(count, keep, m_ref, *refs):
    left, right = refs[:count], refs[count : 2 * count]
    acc = dot_tn(left[0][...], right[0][...])
    for a, b in zip(left[1:], right[1:]):
        acc = acc + dot_tn(a[...], b[...])
    if not keep:
        refs[2 * count][0, 0] = acc.astype(BF16)
        return
    acc = (acc + refs[2 * count][0, 0].astype(F32)).astype(BF16)
    half = pl.program_id(0)
    p = pl.program_id(1)
    places = pl.num_programs(1)
    for h in range(2):
        send_ref, keep_ref = refs[2 * count + 1 + 2 * h], refs[2 * count + 2 + 2 * h]

        @pl.when((half == h) & (p < places // 2))
        def _(send_ref=send_ref):
            send_ref[0] = acc

        @pl.when((half == h) & (p >= places // 2))
        def _(keep_ref=keep_ref):
            keep_ref[0] = acc


def grad_call(m, ndp, lefts, rights, got=None):
    keep = got is not None
    d, n = lefts[0].shape[1], rights[0].shape[1]
    places = ndp // 2
    hp = places // 2
    f = d // ndp
    orders = stage_orders(places.bit_length() - 1)

    def left_map(h, p, m_ref):
        me = m_ref[0]
        b = jnp.where(h == 0, block_at(me, p, orders[0]), block_at(me, p, orders[1]))
        core = me & 1
        return (0, 2 * b + (core if keep else 1 - core))

    specs = [pl.BlockSpec((a.shape[0], f), left_map) for a in lefts]
    specs += [pl.BlockSpec((b.shape[0], n // 2), lambda h, p, *_: (0, h)) for b in rights]
    block = pl.BlockSpec((1, 1, f, n // 2), lambda h, p, *_: (h, p, 0, 0))
    if keep:
        specs.append(block)
        outs, shapes = [], []
        for half in range(2):
            outs.append(
                pl.BlockSpec((1, f, n // 2), lambda h, p, *_, half=half: (jnp.where(h == half, jnp.minimum(p, hp - 1), (h > half) * (hp - 1)), 0, 0))
            )
            outs.append(
                pl.BlockSpec((1, f, n // 2), lambda h, p, *_, half=half: (jnp.where(h == half, jnp.maximum(p - hp, 0), (h > half) * (hp - 1)), 0, 0))
            )
            shapes += [shape_of((hp, f, n // 2), BF16)] * 2
    else:
        outs, shapes = block, shape_of((2, places, f, n // 2), BF16)
    k = sum(a.shape[0] for a in lefts)
    return call(
        functools.partial(grad_kernel, len(lefts), keep),
        (2, places),
        specs,
        outs,
        shapes,
        prefetch=1,
        flops=k * d * n,
        nbytes=2 * k * (d + n) + d * n,
        name="grad_keep" if keep else "grad_send",
    )(m, *lefts, *rights, *((got,) if keep else ()))


def per_device(
    n,
    ndp,
    tokens,
    doc_ids,
    norm1_gain,
    norm1_bias,
    query_weight,
    query_bias,
    keyval_weight,
    value_bias,
    out_weight,
    out_bias,
    norm2_gain,
    norm2_bias,
    up_weight,
    up_bias,
    down_weight,
    down_bias,
    grad_out,
):
    t_all, d = tokens.shape
    wins, seq = doc_ids.shape
    hd = value_bias.shape[0]
    lq = query_weight.shape[1]
    units = up_weight.shape[1]
    group = n // wins
    rows = t_all // n
    ti = lax.axis_index("tp")
    m = lax.axis_index("dp")
    mv = m.reshape(1)
    r = lax.rem(ti, group)
    win = lax.div(ti, group)
    tok = [None]

    def perm(x, to_dp=lambda a: a, to_tp=lambda a: a):
        pairs = [(a * n + b, to_dp(a) * n + to_tp(b)) for a in range(ndp) for b in range(n)]
        return lax.ppermute(x, ("dp", "tp"), pairs)

    def tp_shift(x, s):
        return perm(x, to_tp=lambda b: (b + s) % n)

    def group_shift(x, s):
        return perm(x, to_tp=lambda b: (b // group) * group + (b + s) % group)

    def tp_at(s):
        return lax.rem(ti + (s % n), n)

    def after(x, *marks):
        return lax.optimization_barrier((x,) + marks)[0]

    def seq_in(x):
        return x if tok[0] is None else after(x, tok[0])

    def seq_out(x):
        tok[0] = x[0] if isinstance(x, (tuple, list)) else x
        return x

    def rows_at(x, start, size):
        return lax.dynamic_slice_in_dim(x, start, size, axis=0)

    vec = lambda v: v.reshape(1, -1)
    n1g, n1b, n2g, n2b = vec(norm1_gain), vec(norm1_bias), vec(norm2_gain), vec(norm2_bias)

    def spread(piece, axis):
        size = piece.shape[axis]
        shape = list(piece.shape)
        shape[axis] = n * size
        full = jnp.zeros(shape, piece.dtype)
        for s in range(n):
            got = piece if s == 0 else tp_shift(piece, s)
            at = [0, 0]
            at[axis] = tp_at(-s) * size
            full = lax.dynamic_update_slice(full, got, at)
        return full

    slab = d // ndp
    uslab = units // ndp
    wo_cols = lax.dynamic_slice_in_dim(out_weight, m * slab, slab, axis=1)
    wo_z = spread(wo_cols, 0)
    wo = lax.all_gather(wo_z, "dp", axis=0, tiled=False)

    n1 = seq_out(layer_norm(tokens, n1g, n1b))
    kv = seq_out(jnp.dot(n1, keyval_weight, preferred_element_type=F32))
    keys = kv[:, :hd].astype(BF16)
    values = (kv[:, hd:] + value_bias.astype(F32)).astype(BF16)
    q = seq_out((jnp.dot(seq_in(n1), query_weight, preferred_element_type=F32) + query_bias.astype(F32)).astype(BF16))
    dcol = doc_ids.reshape(t_all, 1)
    att = seq_out(attn_fwd(q, keys, values.T, dcol, doc_ids.reshape(wins, 1, seq), seq, hd))

    up_far, down_far, upb_far = [], [], []
    att_gots = []
    for t in range(1, wins):
        up_far.append(tp_shift(after(rows_at(up_weight, m * slab, slab), wo_z), t * group))
        upb_far.append(tp_shift(vec(up_bias), t * group))
    for s in range(1, n):
        att_gots.append(tp_shift(rows_at(att, tp_at(s) * rows, rows), s))
    for t in range(1, wins):
        down_far.append(tp_shift(after(rows_at(down_weight, m * uslab, uslab), att_gots[n // 2 - 1]), t * group))
    up_far = [lax.all_gather(after(a, wo), "dp", axis=0, tiled=True) for a in up_far]
    down_far = [lax.all_gather(after(b, a), "dp", axis=0, tiled=True) for a, b in zip(up_far, down_far)]

    go = [rows_at(grad_out, (win * group + lax.rem(r + group - s, group)) * rows, rows) for s in range(group)]

    def grad_act(s, w):
        return seq_out(lax.dot_general(seq_in(go[s]), w, (((1,), (1,)), ((), ())), preferred_element_type=F32).astype(BF16))

    das = [[grad_act(s, down_weight)] for s in range(group)]

    att_own = jnp.zeros((rows, n * lq), BF16)
    att_own = lax.dynamic_update_slice(att_own, rows_at(att, ti * rows, rows), (0, ti * lq))
    for s in range(1, n):
        att_own = lax.dynamic_update_slice(att_own, after(att_gots[s - 1], tok[0]), (0, tp_at(-s) * lq))
    x_own = rows_at(tokens, ti * rows, rows)
    h1, n2 = seq_out(proj_ln(att_own, wo, x_own, vec(out_bias), n2g, n2b))

    ns = [n2] + [group_shift(n2, s) for s in range(1, group)]
    wq_z = spread(after(rows_at(query_weight, m * slab, slab), n2), 1)
    wq = lax.all_gather(after(wq_z, *down_far), "dp", axis=0, tiled=True)
    qb_all = jnp.zeros((n * lq,), BF16)
    qb_all = lax.dynamic_update_slice(qb_all, query_bias, (ti * lq,))
    for s in range(1, n):
        qb_all = lax.dynamic_update_slice(qb_all, tp_shift(query_bias, s), (tp_at(-s) * lq,))

    ups = [up_weight] + up_far
    downs = [down_weight] + down_far
    upbs = [vec(up_bias)] + upb_far
    acts = [[None] * wins for _ in range(group)]
    gbs = [[None] * wins for _ in range(group)]
    gsums = [[None] * wins for _ in range(group)]

    def up(s, k):
        acts[s][k], gbs[s][k], gsums[s][k] = seq_out(ffn_up(seq_in(ns[s]), ups[k], upbs[k], das[s][k]))

    def back_up(s):
        out = None
        for k in range(wins):
            part = lax.dot_general(seq_in(gbs[s][k]) if k == 0 else gbs[s][k], ups[k], (((1,), (1,)), ((), ())), preferred_element_type=F32)
            out = part if out is None else out + part
        return seq_out(out.astype(BF16))

    def down(s):
        out = None
        for k in range(wins):
            part = jnp.dot(seq_in(acts[s][k]) if k == 0 else acts[s][k], downs[k], preferred_element_type=F32)
            out = part if out is None else out + part
        return seq_out(out.astype(BF16))

    def grad_send(lefts, rights):
        return perm(seq_out(grad_call(mv, ndp, [seq_in(lefts[0])] + lefts[1:], rights)), to_dp=lambda a: a ^ 1)

    def grad_keep(lefts, rights, got):
        sa, ka, sb, kb = seq_out(grad_call(mv, ndp, [seq_in(lefts[0])] + lefts[1:], rights, got))
        res = []
        for order, send, keep in zip(stage_orders((ndp // 2).bit_length() - 1), (sa, sb), (ka, kb)):
            for b in order:
                x = keep.astype(F32) + perm(send, to_dp=lambda a: a ^ (2 << b)).astype(F32)
                x = x.astype(BF16)
                half = x.shape[0] // 2
                if half:
                    send, keep = x[:half], x[half:]
            res.append(x[0])
        return jnp.concatenate(res, axis=1)

    late = list(range(1, group)) + [0]
    up(0, 0)
    for s in range(1, group):
        up(s, 0)
    act_k = lambda k: [acts[s][k] for s in range(group)]
    gb_k = lambda k: [gbs[s][k] for s in range(group)]
    got_up, got_down, g_up, g_down = {}, {}, {}, {}
    got_up[0] = grad_send(ns, gb_k(0))
    got_down[0] = grad_send(go, act_k(0))
    g_up[0] = grad_keep(ns, gb_k(0), got_up[0])
    g_down[0] = grad_keep(go, act_k(0), got_down[0])
    gn2_parts, sum_parts = [None] * group, [None] * group
    for s in late:
        for k in range(1, wins):
            das[s].append(grad_act(s, downs[k]))
            up(s, k)
        part = back_up(s)
        gn2_parts[s] = part if s == 0 else group_shift(part, -s)
    for s in late:
        part = down(s)
        sum_parts[s] = part if s == 0 else group_shift(after(part, gn2_parts[1]), -s)
    for k in range(1, wins):
        got_up[k] = grad_send(ns, gb_k(k))
        got_down[k] = grad_send(go, act_k(k))
    n1_own = rows_at(n1, ti * rows, rows)
    q_own = seq_out((jnp.dot(seq_in(n1_own), wq, preferred_element_type=F32) + qb_all.astype(F32)).astype(BF16))

    gh1, gm, gatt, sums2 = seq_out(norm2_back(gn2_parts, seq_in(h1), go[0], n2g, wo))
    k_win = rows_at(keys, win * seq, seq)
    v_win = rows_at(values, win * seq, seq)
    row0 = r * rows
    d_win = rows_at(dcol, win * seq, seq)
    d_own = rows_at(dcol, ti * rows, rows).reshape(1, rows)
    gq, gk, gv = seq_out(attn_bwd(row0.reshape(1), q_own, gatt, k_win, v_win, k_win.T, d_win, d_own, hd))
    gkv_part = jnp.concatenate([gk, gv], axis=1)
    gkv = rows_at(gkv_part, row0, rows)
    got_kv = [
        group_shift(rows_at(gkv_part, lax.rem(r + s, group) * rows, rows).astype(BF16), s) for s in range(1, group)
    ]
    for k in range(1, wins):
        g_up[k] = grad_keep(ns, gb_k(k), got_up[k])
    for got in got_kv:
        gkv = gkv + after(got, tok[0]).astype(F32)
    gkv = gkv.astype(BF16)
    gt, sums1, small = seq_out(norm1_back(seq_in(gq), gkv, wq, keyval_weight, x_own, gh1, n1g))
    grad_tokens = lax.all_gather(gt, "tp", axis=0, tiled=True)
    for k in range(1, wins):
        g_down[k] = grad_keep(go, act_k(k), got_down[k])

    total = h1 + down_bias.astype(F32)
    for sp in sum_parts:
        total = total + sp.astype(F32)
    output = lax.all_gather(total.astype(BF16), "tp", axis=0, tiled=True)

    gqkv = jnp.concatenate([gq, gkv], axis=1)
    got_out = grad_send([gm], [att_own])
    got_qkv = grad_send([n1_own], [gqkv])
    g_out = grad_keep([gm], [att_own], got_out)
    g_qkv = grad_keep([n1_own], [gqkv], got_qkv)

    g_upw, g_downw = g_up[0].astype(F32), g_down[0].astype(F32)
    for t in range(1, wins):
        g_upw = g_upw + tp_shift(g_up[t], -t * group).astype(F32)
        g_downw = g_downw + tp_shift(g_down[t], -t * group).astype(F32)

    def tp_scatter(x, cut):
        out = cut(x, ti).astype(F32)
        for s in range(1, n):
            out = out + tp_shift(cut(x, tp_at(s)), s).astype(F32)
        return out

    take_cols = lambda x, i: lax.dynamic_slice_in_dim(x, i * lq, lq, axis=1)
    g_outw = tp_scatter(g_out, take_cols).T
    g_qw = tp_scatter(g_qkv[:, : n * lq], take_cols)
    kv_rows = g_qkv.shape[0] // n
    g_kvw = tp_scatter(g_qkv[:, n * lq :], lambda x, i: rows_at(x, i * kv_rows, kv_rows))

    ub = jnp.zeros((n * units,), F32)
    for k in range(wins):
        part = sum(gsums[s][k] for s in range(group)).reshape(units)
        ub = lax.dynamic_update_slice(ub, part, (tp_at(-k * group) * units,))
    pack = jnp.concatenate(
        [sums2[:4].reshape(-1), sums1[:3].reshape(-1), jnp.pad(small[0, hd:], (0, d - hd)), ub]
    )
    step = 1
    while step < ndp:
        pack = pack + perm(pack, to_dp=lambda a: a ^ step)
        step *= 2
    step = 1
    while step < n:
        pack = pack + perm(pack, to_tp=lambda b: b ^ step)
        step *= 2
    piece = lambda row, at, size: lax.dynamic_slice_in_dim(pack, row * d + at, size)
    vs = d // ndp
    qs = lq // ndp
    us = units // ndp
    bs = hd // (ndp * n)
    return (
        output,
        grad_tokens,
        piece(4, m * vs, vs),
        piece(5, m * vs, vs),
        g_qw,
        piece(6, ti * lq + m * qs, qs),
        g_kvw,
        piece(7, (m * n + ti) * bs, bs),
        g_outw,
        piece(2, m * vs, vs),
        piece(0, m * vs, vs),
        piece(1, m * vs, vs),
        g_upw,
        piece(8, ti * units + m * us, us),
        g_downw.T,
        piece(3, m * vs, vs),
    )


def solution(mesh):
    n = mesh.shape["tp"]
    ndp = mesh.shape["dp"]
    return jax.shard_map(
        functools.partial(per_device, n, ndp),
        mesh=mesh,
        in_specs=(
            P("dp", None),
            P("dp", None),
            P(),
            P(),
            P(None, "tp"),
            P("tp"),
            P(),
            P(),
            P("tp", None),
            P(),
            P(),
            P(),
            P(None, "tp"),
            P("tp"),
            P("tp", None),
            P(),
            P("dp", None),
        ),
        out_specs=(
            P("dp", None),
            P("dp", None),
            P("dp"),
            P("dp"),
            P("dp", "tp"),
            P(("tp", "dp")),
            P(("dp", "tp"), None),
            P(("dp", "tp")),
            P("tp", "dp"),
            P("dp"),
            P("dp"),
            P("dp"),
            P("dp", "tp"),
            P(("tp", "dp")),
            P("tp", "dp"),
            P("dp"),
        ),
        check_vma=False,
    )
```

time: 1870 us -> 1080 us (0.58)
  waiting for transfers between devices: 1150 us -> 407 us
  matrix products: 441 us -> 124 us
  Pallas kernels: 0 us -> 300 us
  other arithmetic: 170 us -> 41.6 us
  starting transfers between devices: 0.37 us -> 103 us
  blocking collectives: 68.7 us -> 0 us
  local copies, waits for them, and re-layouts: 13.2 us -> 75.4 us
    psum x4 -> x0, waiting for transfers between devices: 1100 us -> none  [the longest x1 496 us: forward_block(): summed = lax.psum(down_part.astype(jnp.bfloat16), 'tp').astype(jnp.float32)]
    ppermute x0 -> x65, waiting for transfers between devices: none -> 399 us  [perm(): return lax.ppermute(x, ('dp', 'tp'), pairs)]
    dot_general x42 -> x15, matrix products: 441 us -> 124 us  [the longest x4 37 us: back_up(): lax.dot_general(seq_in(gbs[s][k]) if k == 0 else gbs[s][k], ups[k], (((1,...]
    pallas_call x0 -> x22, Pallas kernels: none -> 300 us  [the longest x12 132 us: grad_call(): call(functools.partial(grad_kernel, len(lefts), keep), (2, places), specs...]
    reduce_sum x13 -> x0, other arithmetic: 112 us -> none  [the longest x4 49.5 us: layer_norm(): return center * lax.rsqrt(spread + 1e-05) * gain_vec + shift_vec]
    ppermute x0 -> x65, starting transfers between devices: none -> 102 us  [perm(): return lax.ppermute(x, ('dp', 'tp'), pairs)]
    unnamed x2 -> x0, blocking collectives: 68.7 us -> none
    reduce_scatter x5 -> x0, waiting for transfers between devices: 48.9 us -> none  [the longest x1 48.8 us: reduce_once(): lax.psum_scatter(grad_terms[12], ('dp', 'tp'), scatter_dimension=0, tiled...]
  transfers between devices with their start and end apart: 9 -> 71, of which waited for: 5 -> 28; matrix products, arithmetic and copies ran while one was open for 20% -> 20% of each run, Pallas kernels for 0% -> 28%
where the time goes in v1:
time: 1080 us; the launch traced here: 1070 us
  waiting for transfers between devices  407 us (38%)
  Pallas kernels  300 us (28%)
  matrix products  124 us (11%)
  starting transfers between devices  103 us (10%)
  local copies, waits for them, and re-layouts  75.4 us (7%)
  other arithmetic  41.6 us (4%)
  between operations  15.7 us (1%)
    ppermute x65, waiting for transfers between devices, perm(): return lax.ppermute(x, ('dp', 'tp'), pairs)  399 us
    pallas_call x12, Pallas kernels, grad_call(): call(functools.partial(grad_kernel, len(lefts), keep), (2, places), specs...  132 us
    ppermute x65, starting transfers between devices, perm(): return lax.ppermute(x, ('dp', 'tp'), pairs)  102 us
    pallas_call x4, Pallas kernels, ffn_up(): call(up_kernel, (u // bn,), [whole((r, d)), pl.BlockSpec((d, bn), lambda...  52.2 us
    dot_general x4, matrix products, back_up(): lax.dot_general(seq_in(gbs[s][k]) if k == 0 else gbs[s][k], ups[k], (((1,...  37 us
    dot_general x4, matrix products, grad_act(): lax.dot_general(seq_in(go[s]), w, (((1,), (1,)), ((), ())), preferred_ele...  35.1 us
    pallas_call x1, Pallas kernels, attn_bwd(): call(functools.partial(attn_bwd_kernel, hd ** (-0.5), qb, reach), (heads,...  34.4 us
    unnamed x177, local copies, waits for them, and re-layouts  32.4 us
  transfers between devices with their start and end apart: 71, of which 28 were waited for; matrix products, arithmetic and copies ran while one was open for 20% of the time, Pallas kernels for 28%

profile of v1, /device:TPU:0, one launch (start us, length us, event | category | flops | bytes accessed | tf_op | source)
XLA Modules:
  0.0 1066.6 jit_solution(3673543134862026712)
XLA Ops:
  16.1 5.7 collective-permute-done.3
  22.8 9.4 collective-permute-done.4
  35.6 4.1 collective-permute-start.10
  39.7 45.8 %collective-permute-done.10 = bf16[256,2048]{1,0:T(8,128)(2,1)S(1)} collective-permute-done((bf16[256,2048]{1,0:T(8,128)(2,1)S(1)}, bf16[256,2048]{1,0:T(8,128)(2,1)S(1)}, u32[]{:S(2)}, u32[]{:S(2)}) %collective-permute-start.10) | collective-permute-done | bytes 1048608 | tf_op jit(solution)/shard_map/ppermute | solution.py:460
  85.5 8.0 all-gather.18.cloned.1.call-done
  94.8 11.3 %norm1.1 = bf16[2048,2048]{1,0:T(8,128)(2,1)} custom-call(bf16[2048,2048]{1,0:T(8,128)(2,1)} %x_ref.1, bf16[1,2048]{1,0:T(2,128)(2,1)} %reshape.82.g_ref, bf16[1,2048]{1,0:T(2,128)(2,1)} %reshape.83.b_ref), custom_call_target="tpu_custom_call" | custom-call | flops 33554432 | bytes 16777216 | tf_op jit(solution)/shard_map/norm1/pallas_call | solution.py:70
  106.1 5.9 fusion.26
  119.6 9.1 add_convert_fusion.6.q_ref
  128.7 19.0 %attn_fwd.1 = bf16[2048,512]{1,0:T(8,128)(2,1)} custom-call(bf16[2048,512]{1,0:T(8,128)(2,1)} %add_convert_fusion.6.q_ref, bf16[2048,128]{1,0:T(8,128)(2,1)} %copy.40.k_ref, bf16[128,2048]{1,0:T(8,128)(2,1)} %copy.41.vt_ref, s32[2048,1]{1,0:T(8,128)} %copy.42.dcol_ref, s32[2,1,1024]{2,1,0:T(1,128)} %reshape.85.drow_ref), custom_call_target="tpu_custom_call" | custom-call | flops 2684354560 | bytes 5242880 | tf_op jit(solution)/shard_map/attn_fwd/pallas_call | solution.py:115
  154.9 22.5 %collective-permute-done.1 = bf16[512,512]{1,0:T(8,128)(2,1)S(1)} collective-permute-done((bf16[512,512]{1,0:T(8,128)(2,1)S(1)}, bf16[512,512]{1,0:T(8,128)(2,1)S(1)}, u32[]{:S(2)}, u32[]{:S(2)}) %collective-permute-start.1) | collective-permute-done | bytes 524320 | tf_op jit(solution)/shard_map/ppermute | solution.py:460
  178.2 47.1 %collective-permute-done.9 = bf16[256,2048]{1,0:T(8,128)(2,1)S(1)} collective-permute-done((bf16[256,2048]{1,0:T(8,128)(2,1)S(1)}, bf16[256,2048]{1,0:T(8,128)(2,1)S(1)}, u32[]{:S(2)}, u32[]{:S(2)}) %collective-permute-start.9) | collective-permute-done | bytes 1048608 | tf_op jit(solution)/shard_map/ppermute | solution.py:460
  231.5 10.8 %convolution_convert_fusion.3.da_ref = bf16[512,2048]{1,0:T(8,128)(2,1)} fusion(bf16[512,2048]{1,0:T(8,128)(2,1)S(1)} %get-tuple-element.164.refs_0_.refs_3_, bf16[2048,2048]{1,0:T(8,128)(2,1)} %param.31), kind=kOutput, calls=%fused_computation.10 | convolution fusion | flops 4296015872 | bytes 12582912 | tf_op jit(solution)/shard_map/dot_general | solution.py:528
  242.4 6.0 convolution_convert_fusion.2.da_ref
  255.9 11.1 %proj_ln.1 = (f32[512,2048]{1,0:T(8,128)}, bf16[512,2048]{1,0:T(8,128)(2,1)}) custom-call(bf16[512,2048]{1,0:T(8,128)(2,1)} %constant_dynamic-update-slice_fusion.8.att_ref.refs_1_, bf16[8,2048,256]{2,1,0:T(8,128)(2,1)} %bitcast.78, bf16[512,2048]{1,0:T(8,128)(2,1)} %constant_dynamic-slice_fusion.11.x_ref, bf16[1,2048]{1,0:T(2,128)(2,1)} %reshape.86.ob_ref, ...), custom_call_target="tpu_custom_call" | custom-call | flops 4294967296 | bytes 18874368 | tf_op jit(solution)/shard_map/proj_ln/pallas_call | solution.py:150
  268.0 12.9 %ffn_up.4 = (bf16[512,2048]{1,0:T(8,128)(2,1)}, bf16[512,2048]{1,0:T(8,128)(2,1)}, f32[1,2048]{1,0:T(1,128)}) custom-call(bf16[512,2048]{1,0:T(8,128)(2,1)} %get-tuple-element.148.n_ref.refs_0_, bf16[2048,2048]{1,0:T(8,128)(2,1)} %w_ref.3, bf16[1,2048]{1,0:T(2,128)(2,1)} %reshape.89.b_ref, bf16[512,2048]{1,0:T(8,128)(2,1)} %convolution_convert_fusion.3.da_ref), custom_call_target="tpu_custom_call" | custom-call | flops 4294967296 | bytes 16777216 | tf_op jit(solution)/shard_map/ffn_up/pallas_call | solution.py:179
  280.9 33.1 %collective-permute-done.6.n_ref.refs_1_ = bf16[512,2048]{1,0:T(8,128)(2,1)S(1)} collective-permute-done((bf16[512,2048]{1,0:T(8,128)(2,1)}, bf16[512,2048]{1,0:T(8,128)(2,1)S(1)}, u32[]{:S(2)}, u32[]{:S(2)}) %collective-permute-start.6) | collective-permute-done | bytes 2097184 | tf_op jit(solution)/shard_map/ppermute | solution.py:460
  315.3 12.8 %ffn_up.5 = (bf16[512,2048]{1,0:T(8,128)(2,1)}, bf16[512,2048]{1,0:T(8,128)(2,1)}, f32[1,2048]{1,0:T(1,128)}) custom-call(bf16[512,2048]{1,0:T(8,128)(2,1)} %copy-done.65, bf16[2048,2048]{1,0:T(8,128)(2,1)} %w_ref.3, bf16[1,2048]{1,0:T(2,128)(2,1)} %reshape.89.b_ref, bf16[512,2048]{1,0:T(8,128)(2,1)} %convolution_convert_fusion.2.da_ref), custom_call_target="tpu_custom_call" | custom-call | flops 4294967296 | bytes 16777216 | tf_op jit(solution)/shard_map/ffn_up/pallas_call | solution.py:179
  328.1 10.9 %grad_send.6 = bf16[2,4,256,1024]{3,2,1,0:T(8,128)(2,1)} custom-call(s32[1]{0:T(128)} %bitcast.2.m_ref, bf16[512,2048]{1,0:T(8,128)(2,1)} %get-tuple-element.148.n_ref.refs_0_, bf16[512,2048]{1,0:T(8,128)(2,1)} %copy-done.65, bf16[512,2048]{1,0:T(8,128)(2,1)} %get-tuple-element.135.refs_2_, bf16[512,2048]{1,0:T(8,128)(2,1)} %get-tuple-element.130.refs_3_), custom_call_target="tpu_custom_call" | custom-call | flops 4294967296 | bytes 12582912 | tf_op jit(solution)/shard_map/grad_send/pallas_call | solution.py:410
  339.1 10.9 %grad_send.7 = bf16[2,4,256,1024]{3,2,1,0:T(8,128)(2,1)} custom-call(s32[1]{0:T(128)} %bitcast.2.m_ref, bf16[512,2048]{1,0:T(8,128)(2,1)} %copy-done.4, bf16[512,2048]{1,0:T(8,128)(2,1)} %copy-done.21, bf16[512,2048]{1,0:T(8,128)(2,1)} %get-tuple-element.138.refs_2_, bf16[512,2048]{1,0:T(8,128)(2,1)} %get-tuple-element.137.refs_3_), custom_call_target="tpu_custom_call" | custom-call | flops 4294967296 | bytes 12582912 | tf_op jit(solution)/shard_map/grad_send/pallas_call | solution.py:410
  355.9 5.7 collective-permute-done.14
  361.6 11.6 %collective-permute-start.11 = (bf16[1,2048]{1,0:T(2,128)(2,1)S(1)}, bf16[1,2048]{1,0:T(2,128)(2,1)S(1)}, u32[]{:S(2)}, u32[]{:S(2)}) collective-permute-start(bf16[1,2048]{1,0:T(2,128)(2,1)S(1)} %copy-done.53), channel_id=1, source_target_pairs={{0,2},{1,3},{2,0},{3,1},{4,6},{5,7},{6,4},{7,5},{8,10},{9,11},{10,... | collective-permute-start | bytes 12296 | tf_op jit(solution)/shard_map/ppermute | solution.py:460
  373.4 12.6 %grad_keep.6 = (bf16[2,256,1024]{2,1,0:T(8,128)(2,1)}, bf16[2,256,1024]{2,1,0:T(8,128)(2,1)}, bf16[2,256,1024]{2,1,0:T(8,128)(2,1)}, bf16[2,256,1024]{2,1,0:T(8,128)(2,1)}) custom-call(s32[1]{0:T(128)} %bitcast.2.m_ref, bf16[512,2048]{1,0:T(8,128)(2,1)} %get-tuple-element.148.n_ref.refs_0_, bf16[512,2048]{1,0:T(8,128)(2,1)} %copy-done.65, ...), custom_call_target="tpu_custom_call" | custom-call | flops 4294967296 | bytes 12582912 | tf_op jit(solution)/shard_map/grad_keep/pallas_call | solution.py:410
  386.0 12.4 %grad_keep.7 = (bf16[2,256,1024]{2,1,0:T(8,128)(2,1)}, bf16[2,256,1024]{2,1,0:T(8,128)(2,1)}, bf16[2,256,1024]{2,1,0:T(8,128)(2,1)}, bf16[2,256,1024]{2,1,0:T(8,128)(2,1)}) custom-call(s32[1]{0:T(128)} %bitcast.2.m_ref, bf16[512,2048]{1,0:T(8,128)(2,1)} %copy-done.4, bf16[512,2048]{1,0:T(8,128)(2,1)} %copy-done.21, ...), custom_call_target="tpu_custom_call" | custom-call | flops 4294967296 | bytes 12582912 | tf_op jit(solution)/shard_map/grad_keep/pallas_call | solution.py:410
  398.9 9.1 convolution_convert_fusion.1.da_ref
  408.6 13.4 %ffn_up.6 = (bf16[512,2048]{1,0:T(8,128)(2,1)}, bf16[512,2048]{1,0:T(8,128)(2,1)}, f32[1,2048]{1,0:T(1,128)}) custom-call(bf16[512,2048]{1,0:T(8,128)(2,1)} %copy-done.65, bf16[2048,2048]{1,0:T(8,128)(2,1)} %all-gather.8.cloned.1.call-done.w_ref, bf16[1,2048]{1,0:T(2,128)(2,1)} %copy-done.68, bf16[512,2048]{1,0:T(8,128)(2,1)} %convolution_convert_fusion.1.da_ref), custom_call_target="tpu_custom_call" | custom-call | flops 4294967296 | bytes 16777216 | tf_op jit(solution)/shard_map/ffn_up/pallas_call | solution.py:179
  422.1 9.6 fusion.27
  431.7 7.7 add_convert_fusion.5
  439.5 4.4 collective-permute-start.12
  443.9 9.2 convolution_convert_fusion.da_ref
  453.1 13.1 %ffn_up.7 = (bf16[512,2048]{1,0:T(8,128)(2,1)}, bf16[512,2048]{1,0:T(8,128)(2,1)}, f32[1,2048]{1,0:T(1,128)}) custom-call(bf16[512,2048]{1,0:T(8,128)(2,1)} %get-tuple-element.148.n_ref.refs_0_, bf16[2048,2048]{1,0:T(8,128)(2,1)} %all-gather.8.cloned.1.call-done.w_ref, bf16[1,2048]{1,0:T(2,128)(2,1)} %copy-done.68, ...), custom_call_target="tpu_custom_call" | custom-call | flops 4294967296 | bytes 16777216 | tf_op jit(solution)/shard_map/ffn_up/pallas_call | solution.py:179
  466.2 9.8 fusion.28
  476.0 9.9 add_convert_fusion.4.refs_0_
  485.9 4.6 fusion.29
  490.5 8.3 add_convert_fusion.3
  499.0 6.2 fusion.30
  505.1 8.9 add_convert_fusion.2
  514.1 31.9 %collective-permute-done.13 = bf16[512,2048]{1,0:T(8,128)(2,1)S(1)} collective-permute-done((bf16[512,2048]{1,0:T(8,128)(2,1)S(1)}, bf16[512,2048]{1,0:T(8,128)(2,1)S(1)}, u32[]{:S(2)}, u32[]{:S(2)}) %collective-permute-start.13) | collective-permute-done | bytes 2097184 | tf_op jit(solution)/shard_map/ppermute | solution.py:460
  566.7 10.9 %grad_send.8 = bf16[2,4,256,1024]{3,2,1,0:T(8,128)(2,1)} custom-call(s32[1]{0:T(128)} %bitcast.2.m_ref, bf16[512,2048]{1,0:T(8,128)(2,1)} %get-tuple-element.148.n_ref.refs_0_, bf16[512,2048]{1,0:T(8,128)(2,1)} %copy-done.65, bf16[512,2048]{1,0:T(8,128)(2,1)} %get-tuple-element.136.refs_2_, bf16[512,2048]{1,0:T(8,128)(2,1)} %get-tuple-element.131.refs_3_), custom_call_target="tpu_custom_call" | custom-call | flops 4294967296 | bytes 12582912 | tf_op jit(solution)/shard_map/grad_send/pallas_call | solution.py:410
  590.2 10.9 %grad_send.9 = bf16[2,4,256,1024]{3,2,1,0:T(8,128)(2,1)} custom-call(s32[1]{0:T(128)} %bitcast.2.m_ref, bf16[512,2048]{1,0:T(8,128)(2,1)} %copy-done.4, bf16[512,2048]{1,0:T(8,128)(2,1)} %copy-done.21, bf16[512,2048]{1,0:T(8,128)(2,1)} %get-tuple-element.134.refs_2_, bf16[512,2048]{1,0:T(8,128)(2,1)} %get-tuple-element.129.refs_3_), custom_call_target="tpu_custom_call" | custom-call | flops 4294967296 | bytes 12582912 | tf_op jit(solution)/shard_map/grad_send/pallas_call | solution.py:410
  606.6 9.1 add_convert_fusion.q_ref
  615.7 20.1 %norm2_back.1 = (f32[512,2048]{1,0:T(8,128)}, bf16[512,2048]{1,0:T(8,128)(2,1)}, bf16[512,2048]{1,0:T(8,128)(2,1)}, f32[8,2048]{1,0:T(8,128)}) custom-call(bf16[512,2048]{1,0:T(8,128)(2,1)} %add_convert_fusion.4.refs_0_, bf16[512,2048]{1,0:T(8,128)(2,1)} %copy-done.23, f32[512,2048]{1,0:T(8,128)} %get-tuple-element.145.refs_2_, bf16[512,2048]{1,0:T(8,128)(2,1)} %copy-done.4, ...), custom_call_target="tpu_custom_call" | custom-call | flops 4294967296 | bytes 29360128 | tf_op jit(solution)/shard_map/norm2_back/pallas_call | solution.py:230
  635.9 34.4 %attn_bwd.1 = (bf16[512,2048]{1,0:T(8,128)(2,1)}, f32[1024,128]{1,0:T(8,128)}, f32[1024,128]{1,0:T(8,128)}) custom-call(s32[1]{0:T(128)} %bitcast.3.row0_ref, bf16[512,2048]{1,0:T(8,128)(2,1)} %add_convert_fusion.q_ref, bf16[512,2048]{1,0:T(8,128)(2,1)} %get-tuple-element.146.go_ref, bf16[1024,128]{1,0:T(8,128)(2,1)} %copy.44.k_ref, ...), custom_call_target="tpu_custom_call" | custom-call | flops 8053063680 | bytes 8388608 | tf_op jit(solution)/shard_map/attn_bwd/pallas_call | solution.py:288
  673.2 12.3 %grad_keep.8 = (bf16[2,256,1024]{2,1,0:T(8,128)(2,1)}, bf16[2,256,1024]{2,1,0:T(8,128)(2,1)}, bf16[2,256,1024]{2,1,0:T(8,128)(2,1)}, bf16[2,256,1024]{2,1,0:T(8,128)(2,1)}) custom-call(s32[1]{0:T(128)} %bitcast.2.m_ref, bf16[512,2048]{1,0:T(8,128)(2,1)} %get-tuple-element.148.n_ref.refs_0_, bf16[512,2048]{1,0:T(8,128)(2,1)} %copy-done.65, ...), custom_call_target="tpu_custom_call" | custom-call | flops 4294967296 | bytes 12582912 | tf_op jit(solution)/shard_map/grad_keep/pallas_call | solution.py:410
  685.5 12.9 %collective-permute-done.21 = bf16[512,256]{1,0:T(8,128)(2,1)S(1)} collective-permute-done((bf16[512,256]{1,0:T(8,128)(2,1)S(1)}, bf16[512,256]{1,0:T(8,128)(2,1)S(1)}, u32[]{:S(2)}, u32[]{:S(2)}) %collective-permute-start.21) | collective-permute-done | bytes 262176 | tf_op jit(solution)/shard_map/ppermute | solution.py:460
  700.8 19.9 %norm1_back.1 = (bf16[512,2048]{1,0:T(8,128)(2,1)}, f32[8,2048]{1,0:T(8,128)}, f32[8,256]{1,0:T(8,128)}) custom-call(bf16[512,2048]{1,0:T(8,128)(2,1)} %get-tuple-element.150.gq_ref, bf16[512,256]{1,0:T(8,128)(2,1)} %add_convert_fusion.31.gkv_ref, bf16[2048,2048]{1,0:T(8,128)(2,1)} %all-gather.14.cloned.1.call-done.wq_ref, bf16[2048,256]{1,0:T(8,128)(2,1)} %wkv_ref.1, ...), custom_call_target="tpu_custom_call" | custom-call | flops 4831838208 | bytes 22020096 | tf_op jit(solution)/shard_map/norm1_back/pallas_call | solution.py:330
  720.7 12.8 %grad_keep.9 = (bf16[2,256,1024]{2,1,0:T(8,128)(2,1)}, bf16[2,256,1024]{2,1,0:T(8,128)(2,1)}, bf16[2,256,1024]{2,1,0:T(8,128)(2,1)}, bf16[2,256,1024]{2,1,0:T(8,128)(2,1)}) custom-call(s32[1]{0:T(128)} %bitcast.2.m_ref, bf16[512,2048]{1,0:T(8,128)(2,1)} %copy-done.4, bf16[512,2048]{1,0:T(8,128)(2,1)} %copy-done.21, ...), custom_call_target="tpu_custom_call" | custom-call | flops 4294967296 | bytes 12582912 | tf_op jit(solution)/shard_map/grad_keep/pallas_call | solution.py:410
  734.3 8.5 grad_send.10
  755.0 9.1 grad_send.11
  773.5 8.0 collective-permute-done.26
  784.2 6.3 collective-permute-done.53
  797.3 13.2 %collective-permute-done.62 = bf16[2,256,1024]{2,1,0:T(8,128)(2,1)S(1)} collective-permute-done((bf16[2,256,1024]{2,1,0:T(8,128)(2,1)S(1)}, bf16[2,256,1024]{2,1,0:T(8,128)(2,1)S(1)}, u32[]{:S(2)}, u32[]{:S(2)}) %collective-permute-start.62) | collective-permute-done | bytes 1048608 | tf_op jit(solution)/shard_map/ppermute | solution.py:460
  811.7 4.9 collective-permute-done.60
  817.9 10.0 collective-permute-done.54
  837.3 9.8 grad_keep.10
  849.3 4.2 collective-permute-start.64
  853.7 87.1 %collective-permute-done.55 = bf16[256,2048]{1,0:T(8,128)(2,1)} collective-permute-done((bf16[256,2048]{1,0:T(8,128)(2,1)}, bf16[256,2048]{1,0:T(8,128)(2,1)}, u32[]{:S(2)}, u32[]{:S(2)}) %collective-permute-start.55) | collective-permute-done | bytes 1048608 | tf_op jit(solution)/shard_map/ppermute | solution.py:460
  943.7 10.9 %grad_keep.11 = (bf16[2,256,1152]{2,1,0:T(8,128)(2,1)}, bf16[2,256,1152]{2,1,0:T(8,128)(2,1)}, bf16[2,256,1152]{2,1,0:T(8,128)(2,1)}, bf16[2,256,1152]{2,1,0:T(8,128)(2,1)}) custom-call(s32[1]{0:T(128)} %bitcast.2.m_ref, bf16[512,2048]{1,0:T(8,128)(2,1)} %copy-done.2, bf16[512,2304]{1,0:T(8,128)(2,1)} %pad_maximum_fusion.refs_1_, ...), custom_call_target="tpu_custom_call" | custom-call | flops 2415919104 | bytes 9175040 | tf_op jit(solution)/shard_map/grad_keep/pallas_call | solution.py:410
  967.7 6.2 collective-permute-done.43
  975.2 18.3 %collective-permute-done.41 = bf16[1,256,1024]{2,1,0:T(8,128)(2,1)} collective-permute-done((bf16[1,256,1024]{2,1,0:T(8,128)(2,1)}, bf16[1,256,1024]{2,1,0:T(8,128)(2,1)}, u32[]{:S(2)}, u32[]{:S(2)}) %collective-permute-start.41) | collective-permute-done | bytes 524320 | tf_op jit(solution)/shard_map/ppermute | solution.py:460
  1004.6 9.8 collective-permute-done.33
  1020.8 9.3 collective-permute-start.35
  1036.3 4.2 collective-permute-done.35
  1042.5 8.5 copy.71
  1051.0 8.6 copy.72
  (419 shorter events, 185.9 us)
Async XLA Ops:
  7.2 86.3 %all-gather.18.cloned.1.call-start = ((), (), s32[]{:S(2)}) async-start(), calls=%async_computation.5 | async-start | bytes 9437184 | tf_op jit(solution)/shard_map/all_gather | solution.py:503
  9.1 12.6 %collective-permute-start.3 = (bf16[512,256]{1,0:T(8,128)(2,1)}, bf16[512,256]{1,0:T(8,128)(2,1)}, u32[]{:S(2)}, u32[]{:S(2)}) collective-permute-start(bf16[512,256]{1,0:T(8,128)(2,1)} %get-tuple-element.223), channel_id=1, source_target_pairs={{0,1},{1,2},{2,3},{3,0},{4,5},{5,6},{6,7},{7,4},{8,9},{9,10},{10,1... | collective-permute-start | bytes 786440 | tf_op jit(solution)/shard_map/ppermute | solution.py:460
  12.2 20.0 %collective-permute-start.4 = (bf16[512,256]{1,0:T(8,128)(2,1)}, bf16[512,256]{1,0:T(8,128)(2,1)}, u32[]{:S(2)}, u32[]{:S(2)}) collective-permute-start(bf16[512,256]{1,0:T(8,128)(2,1)} %get-tuple-element.223), channel_id=1, source_target_pairs={{0,2},{1,3},{2,0},{3,1},{4,6},{5,7},{6,4},{7,5},{8,10},{9,11},{10,... | collective-permute-start | bytes 786440 | tf_op jit(solution)/shard_map/ppermute | solution.py:460
  14.8 18.4 %collective-permute-start.5 = (bf16[512,256]{1,0:T(8,128)(2,1)}, bf16[512,256]{1,0:T(8,128)(2,1)S(1)}, u32[]{:S(2)}, u32[]{:S(2)}) collective-permute-start(bf16[512,256]{1,0:T(8,128)(2,1)} %get-tuple-element.223), channel_id=1, source_target_pairs={{0,3},{1,0},{2,1},{3,2},{4,7},{5,4},{6,5},{7,6},{8,11},{9,8},{10,9... | collective-permute-start | bytes 786440 | tf_op jit(solution)/shard_map/ppermute | solution.py:460
  34.2 191.1 %all-gather.8.cloned.1.call-start = ((), (), s32[]{:S(2)}) async-start(), calls=%async_computation | async-start | bytes 9437184 | tf_op jit(solution)/shard_map/all_gather | solution.py:522
  35.6 50.0 %collective-permute-start.10 = (bf16[256,2048]{1,0:T(8,128)(2,1)S(1)}, bf16[256,2048]{1,0:T(8,128)(2,1)S(1)}, u32[]{:S(2)}, u32[]{:S(2)}) collective-permute-start(bf16[256,2048]{1,0:T(8,128)(2,1)S(1)} %constant_dynamic-slice_fusion.9), channel_id=1, source_target_pairs={{0,2},{1,3},{2,0},{3,1},{4,6},{5,7},{6,4},{7,5},{8,10},{9,11},{10,... | collective-permute-start | bytes 3145736 | tf_op jit(solution)/shard_map/ppermute | solution.py:460
  93.5 304.9 %all-gather.10.cloned.1.call-start = ((), (), s32[]{:S(2)}) async-start(), calls=%async_computation.1 | async-start | bytes 9437184 | tf_op jit(solution)/shard_map/all_gather | solution.py:523
  151.2 26.2 %collective-permute-start.1 = (bf16[512,512]{1,0:T(8,128)(2,1)S(1)}, bf16[512,512]{1,0:T(8,128)(2,1)S(1)}, u32[]{:S(2)}, u32[]{:S(2)}) collective-permute-start(bf16[512,512]{1,0:T(8,128)(2,1)S(1)} %get-tuple-element.227), channel_id=1, source_target_pairs={{0,2},{1,3},{2,0},{3,1},{4,6},{5,7},{6,4},{7,5},{8,10},{9,11},{10,... | collective-permute-start | bytes 1572872 | tf_op jit(solution)/shard_map/ppermute | solution.py:460
  177.4 47.9 %collective-permute-start.9 = (bf16[256,2048]{1,0:T(8,128)(2,1)S(1)}, bf16[256,2048]{1,0:T(8,128)(2,1)S(1)}, u32[]{:S(2)}, u32[]{:S(2)}) collective-permute-start(bf16[256,2048]{1,0:T(8,128)(2,1)S(1)} %constant_dynamic-slice_fusion.10), channel_id=1, source_target_pairs={{0,2},{1,3},{2,0},{3,1},{4,6},{5,7},{6,4},{7,5},{8,10},{9,11},{10,... | collective-permute-start | bytes 3145736 | tf_op jit(solution)/shard_map/ppermute | solution.py:460
  226.3 380.3 %all-gather.14.cloned.1.call-start = ((), (), s32[]{:S(2)}) async-start(), calls=%async_computation.3 | async-start | bytes 9437184 | tf_op jit(solution)/shard_map/all_gather | solution.py:541
  226.3 27.1 %collective-permute-start.2 = (bf16[512,512]{1,0:T(8,128)(2,1)}, bf16[512,512]{1,0:T(8,128)(2,1)S(1)}, u32[]{:S(2)}, u32[]{:S(2)}) collective-permute-start(bf16[512,512]{1,0:T(8,128)(2,1)} %get-tuple-element.226), channel_id=1, source_target_pairs={{0,3},{1,0},{2,1},{3,2},{4,7},{5,4},{6,5},{7,6},{8,11},{9,8},{10,9... | collective-permute-start | bytes 1572872 | tf_op jit(solution)/shard_map/ppermute | solution.py:460
  227.5 25.9 %collective-permute-start = (bf16[512,512]{1,0:T(8,128)(2,1)}, bf16[512,512]{1,0:T(8,128)(2,1)S(1)}, u32[]{:S(2)}, u32[]{:S(2)}) collective-permute-start(bf16[512,512]{1,0:T(8,128)(2,1)} %get-tuple-element.228), channel_id=1, source_target_pairs={{0,1},{1,2},{2,3},{3,0},{4,5},{5,6},{6,7},{7,4},{8,9},{9,10},{10,1... | collective-permute-start | bytes 1572872 | tf_op jit(solution)/shard_map/ppermute | solution.py:460
  267.1 46.9 %collective-permute-start.6 = (bf16[512,2048]{1,0:T(8,128)(2,1)}, bf16[512,2048]{1,0:T(8,128)(2,1)S(1)}, u32[]{:S(2)}, u32[]{:S(2)}) collective-permute-start(bf16[512,2048]{1,0:T(8,128)(2,1)} %get-tuple-element.148.n_ref.refs_0_), channel_id=1, source_target_pairs={{0,1},{1,0},{2,3},{3,2},{4,5},{5,4},{6,7},{7,6},{8,9},{9,8},{10,11... | collective-permute-start | bytes 6291464 | tf_op jit(solution)/shard_map/ppermute | solution.py:460
  339.1 34.3 %collective-permute-start.7 = (bf16[2,4,256,1024]{3,2,1,0:T(8,128)(2,1)}, bf16[2,4,256,1024]{3,2,1,0:T(8,128)(2,1)}, u32[]{:S(2)}, u32[]{:S(2)}) collective-permute-start(bf16[2,4,256,1024]{3,2,1,0:T(8,128)(2,1)} %grad_send.6), channel_id=1, source_target_pairs={{0,4},{1,5},{2,6},{3,7},{4,0},{5,1},{6,2},{7,3},{8,12},{9,13},{10,... | collective-permute-start | bytes 12582920 | tf_op jit(solution)/shard_map/ppermute | solution.py:460
  350.0 36.1 %collective-permute-start.8 = (bf16[2,4,256,1024]{3,2,1,0:T(8,128)(2,1)}, bf16[2,4,256,1024]{3,2,1,0:T(8,128)(2,1)}, u32[]{:S(2)}, u32[]{:S(2)}) collective-permute-start(bf16[2,4,256,1024]{3,2,1,0:T(8,128)(2,1)} %grad_send.7), channel_id=1, source_target_pairs={{0,4},{1,5},{2,6},{3,7},{4,0},{5,1},{6,2},{7,3},{8,12},{9,13},{10,... | collective-permute-start | bytes 12582920 | tf_op jit(solution)/shard_map/ppermute | solution.py:460
  350.8 22.5 %collective-permute-start.15 = (bf16[256,512]{1,0:T(8,128)(2,1)S(1)}, bf16[256,512]{1,0:T(8,128)(2,1)S(1)}, u32[]{:S(2)}, u32[]{:S(2)}) collective-permute-start(bf16[256,512]{1,0:T(8,128)(2,1)S(1)} %constant_dynamic-slice_fusion.7), channel_id=1, source_target_pairs={{0,2},{1,3},{2,0},{3,1},{4,6},{5,7},{6,4},{7,5},{8,10},{9,11},{10,... | collective-permute-start | bytes 786440 | tf_op jit(solution)/shard_map/ppermute | solution.py:460
  354.6 18.7 %collective-permute-start.16 = (bf16[256,512]{1,0:T(8,128)(2,1)S(1)}, bf16[256,512]{1,0:T(8,128)(2,1)S(1)}, u32[]{:S(2)}, u32[]{:S(2)}) collective-permute-start(bf16[256,512]{1,0:T(8,128)(2,1)S(1)} %constant_dynamic-slice_fusion.7), channel_id=1, source_target_pairs={{0,3},{1,0},{2,1},{3,2},{4,7},{5,4},{6,5},{7,6},{8,11},{9,8},{10,9... | collective-permute-start | bytes 786440 | tf_op jit(solution)/shard_map/ppermute | solution.py:460
  361.6 46.4 %collective-permute-start.11 = (bf16[1,2048]{1,0:T(2,128)(2,1)S(1)}, bf16[1,2048]{1,0:T(2,128)(2,1)S(1)}, u32[]{:S(2)}, u32[]{:S(2)}) collective-permute-start(bf16[1,2048]{1,0:T(2,128)(2,1)S(1)} %copy-done.53), channel_id=1, source_target_pairs={{0,2},{1,3},{2,0},{3,1},{4,6},{5,7},{6,4},{7,5},{8,10},{9,11},{10,... | collective-permute-start | bytes 12296 | tf_op jit(solution)/shard_map/ppermute | solution.py:460
  398.5 455.0 %all-gather.12.cloned.1.call-start = ((), (), s32[]{:S(2)}) async-start(), calls=%async_computation.2 | async-start | bytes 10485760 | tf_op jit(solution)/shard_map/all_gather | solution.py:639
  439.5 59.4 %collective-permute-start.12 = (bf16[512,2048]{1,0:T(8,128)(2,1)}, bf16[512,2048]{1,0:T(8,128)(2,1)S(1)}, u32[]{:S(2)}, u32[]{:S(2)}) collective-permute-start(bf16[512,2048]{1,0:T(8,128)(2,1)} %add_convert_fusion.5), channel_id=1, source_target_pairs={{0,1},{1,0},{2,3},{3,2},{4,5},{5,4},{6,7},{7,6},{8,9},{9,8},{10,11... | collective-permute-start | bytes 6291464 | tf_op jit(solution)/shard_map/ppermute | solution.py:460
  498.9 47.1 %collective-permute-start.13 = (bf16[512,2048]{1,0:T(8,128)(2,1)S(1)}, bf16[512,2048]{1,0:T(8,128)(2,1)S(1)}, u32[]{:S(2)}, u32[]{:S(2)}) collective-permute-start(bf16[512,2048]{1,0:T(8,128)(2,1)S(1)} %add_convert_fusion.3), channel_id=1, source_target_pairs={{0,1},{1,0},{2,3},{3,2},{4,5},{5,4},{6,7},{7,6},{8,9},{9,8},{10,11... | collective-permute-start | bytes 6291464 | tf_op jit(solution)/shard_map/ppermute | solution.py:460
  548.5 494.0 %all-gather.16.cloned.1.call-start = ((), (), s32[]{:S(2)}) async-start(), calls=%async_computation.4 | async-start | bytes 10485760 | tf_op jit(solution)/shard_map/all_gather | solution.py:632
  549.2 14.8 %collective-permute-start.17 = (bf16[512]{0:T(512)(128)(2,1)S(1)}, bf16[512]{0:T(512)(128)(2,1)S(1)}, u32[]{:S(2)}, u32[]{:S(2)}) collective-permute-start(bf16[512]{0:T(512)(128)(2,1)S(1)} %copy-done.62), channel_id=1, source_target_pairs={{0,1},{1,2},{2,3},{3,0},{4,5},{5,6},{6,7},{7,4},{8,9},{9,10},{10,1... | collective-permute-start | bytes 3080 | tf_op jit(solution)/shard_map/ppermute | solution.py:460
  549.5 14.8 %collective-permute-start.19 = (bf16[512]{0:T(512)(128)(2,1)S(1)}, bf16[512]{0:T(512)(128)(2,1)S(1)}, u32[]{:S(2)}, u32[]{:S(2)}) collective-permute-start(bf16[512]{0:T(512)(128)(2,1)S(1)} %copy-done.62), channel_id=1, source_target_pairs={{0,3},{1,0},{2,1},{3,2},{4,7},{5,4},{6,5},{7,6},{8,11},{9,8},{10,9... | collective-permute-start | bytes 3080 | tf_op jit(solution)/shard_map/ppermute | solution.py:460
  555.1 26.5 %collective-permute-start.58 = (bf16[2,256,1024]{2,1,0:T(8,128)(2,1)}, bf16[2,256,1024]{2,1,0:T(8,128)(2,1)}, u32[]{:S(2)}, u32[]{:S(2)}) collective-permute-start(bf16[2,256,1024]{2,1,0:T(8,128)(2,1)} %get-tuple-element.186), channel_id=1, source_target_pairs={{0,16},{1,17},{2,18},{3,19},{4,20},{5,21},{6,22},{7,23},{8,24},{9,... | collective-permute-start | bytes 3145736 | tf_op jit(solution)/shard_map/ppermute | solution.py:460
  558.1 27.8 %collective-permute-start.56 = (bf16[2,256,1024]{2,1,0:T(8,128)(2,1)}, bf16[2,256,1024]{2,1,0:T(8,128)(2,1)S(1)}, u32[]{:S(2)}, u32[]{:S(2)}) collective-permute-start(bf16[2,256,1024]{2,1,0:T(8,128)(2,1)} %get-tuple-element.122), channel_id=1, source_target_pairs={{0,8},{1,9},{2,10},{3,11},{4,12},{5,13},{6,14},{7,15},{8,0},{9,1},... | collective-permute-start | bytes 3145736 | tf_op jit(solution)/shard_map/ppermute | solution.py:460
  564.9 178.4 %collective-permute-start.47 = (bf16[2,256,1024]{2,1,0:T(8,128)(2,1)}, bf16[2,256,1024]{2,1,0:T(8,128)(2,1)}, u32[]{:S(2)}, u32[]{:S(2)}) collective-permute-start(bf16[2,256,1024]{2,1,0:T(8,128)(2,1)} %get-tuple-element.120), channel_id=1, source_target_pairs={{0,8},{1,9},{2,10},{3,11},{4,12},{5,13},{6,14},{7,15},{8,0},{9,1},... | collective-permute-start | bytes 3145736 | tf_op jit(solution)/shard_map/ppermute | solution.py:460
  566.0 38.0 %collective-permute-start.49 = (bf16[2,256,1024]{2,1,0:T(8,128)(2,1)}, bf16[2,256,1024]{2,1,0:T(8,128)(2,1)S(1)}, u32[]{:S(2)}, u32[]{:S(2)}) collective-permute-start(bf16[2,256,1024]{2,1,0:T(8,128)(2,1)} %get-tuple-element.180), channel_id=1, source_target_pairs={{0,16},{1,17},{2,18},{3,19},{4,20},{5,21},{6,22},{7,23},{8,24},{9,... | collective-permute-start | bytes 3145736 | tf_op jit(solution)/shard_map/ppermute | solution.py:460
  577.6 94.9 %collective-permute-start.20 = (bf16[2,4,256,1024]{3,2,1,0:T(8,128)(2,1)}, bf16[2,4,256,1024]{3,2,1,0:T(8,128)(2,1)}, u32[]{:S(2)}, u32[]{:S(2)}) collective-permute-start(bf16[2,4,256,1024]{3,2,1,0:T(8,128)(2,1)} %grad_send.8), channel_id=1, source_target_pairs={{0,4},{1,5},{2,6},{3,7},{4,0},{5,1},{6,2},{7,3},{8,12},{9,13},{10,... | collective-permute-start | bytes 12582920 | tf_op jit(solution)/shard_map/ppermute | solution.py:460
  584.2 169.5 %collective-permute-start.59 = (bf16[1,256,1024]{2,1,0:T(8,128)(2,1)}, bf16[1,256,1024]{2,1,0:T(8,128)(2,1)}, u32[]{:S(2)}, u32[]{:S(2)}) collective-permute-start(bf16[1,256,1024]{2,1,0:T(8,128)(2,1)} %slice.147), channel_id=1, source_target_pairs={{0,8},{1,9},{2,10},{3,11},{4,12},{5,13},{6,14},{7,15},{8,0},{9,1},... | collective-permute-start | bytes 1572872 | tf_op jit(solution)/shard_map/ppermute | solution.py:460
  589.4 165.6 %collective-permute-start.57 = (bf16[1,256,1024]{2,1,0:T(8,128)(2,1)}, bf16[1,256,1024]{2,1,0:T(8,128)(2,1)}, u32[]{:S(2)}, u32[]{:S(2)}) collective-permute-start(bf16[1,256,1024]{2,1,0:T(8,128)(2,1)} %slice.145), channel_id=1, source_target_pairs={{0,16},{1,17},{2,18},{3,19},{4,20},{5,21},{6,22},{7,23},{8,24},{9,... | collective-permute-start | bytes 1572872 | tf_op jit(solution)/shard_map/ppermute | solution.py:460
  604.0 116.7 %collective-permute-start.27 = (bf16[2,4,256,1024]{3,2,1,0:T(8,128)(2,1)}, bf16[2,4,256,1024]{3,2,1,0:T(8,128)(2,1)}, u32[]{:S(2)}, u32[]{:S(2)}) collective-permute-start(bf16[2,4,256,1024]{3,2,1,0:T(8,128)(2,1)} %grad_send.9), channel_id=1, source_target_pairs={{0,4},{1,5},{2,6},{3,7},{4,0},{5,1},{6,2},{7,3},{8,12},{9,13},{10,... | collective-permute-start | bytes 12582920 | tf_op jit(solution)/shard_map/ppermute | solution.py:460
  672.5 25.8 %collective-permute-start.21 = (bf16[512,256]{1,0:T(8,128)(2,1)S(1)}, bf16[512,256]{1,0:T(8,128)(2,1)S(1)}, u32[]{:S(2)}, u32[]{:S(2)}) collective-permute-start(bf16[512,256]{1,0:T(8,128)(2,1)S(1)} %dynamic-slice_convert_fusion), channel_id=1, source_target_pairs={{0,1},{1,0},{2,3},{3,2},{4,5},{5,4},{6,7},{7,6},{8,9},{9,8},{10,11... | collective-permute-start | bytes 786440 | tf_op jit(solution)/shard_map/ppermute | solution.py:460
  698.3 68.1 %collective-permute-start.50 = (bf16[1,256,1024]{2,1,0:T(8,128)(2,1)}, bf16[1,256,1024]{2,1,0:T(8,128)(2,1)}, u32[]{:S(2)}, u32[]{:S(2)}) collective-permute-start(bf16[1,256,1024]{2,1,0:T(8,128)(2,1)} %slice.139), channel_id=1, source_target_pairs={{0,8},{1,9},{2,10},{3,11},{4,12},{5,13},{6,14},{7,15},{8,0},{9,1},... | collective-permute-start | bytes 1572872 | tf_op jit(solution)/shard_map/ppermute | solution.py:460
  742.9 94.5 %collective-permute-start.28 = (bf16[2,4,256,1024]{3,2,1,0:T(8,128)(2,1)}, bf16[2,4,256,1024]{3,2,1,0:T(8,128)(2,1)}, u32[]{:S(2)}, u32[]{:S(2)}) collective-permute-start(bf16[2,4,256,1024]{3,2,1,0:T(8,128)(2,1)} %grad_send.10), channel_id=1, source_target_pairs={{0,4},{1,5},{2,6},{3,7},{4,0},{5,1},{6,2},{7,3},{8,12},{9,13},{10,... | collective-permute-start | bytes 12582920 | tf_op jit(solution)/shard_map/ppermute | solution.py:460
  752.9 15.2 %collective-permute-start.48 = (bf16[1,256,1024]{2,1,0:T(8,128)(2,1)}, bf16[1,256,1024]{2,1,0:T(8,128)(2,1)}, u32[]{:S(2)}, u32[]{:S(2)}) collective-permute-start(bf16[1,256,1024]{2,1,0:T(8,128)(2,1)} %slice.137), channel_id=1, source_target_pairs={{0,16},{1,17},{2,18},{3,19},{4,20},{5,21},{6,22},{7,23},{8,24},{9,... | collective-permute-start | bytes 1572872 | tf_op jit(solution)/shard_map/ppermute | solution.py:460
  753.7 36.8 %collective-permute-start.53 = (bf16[2,256,1024]{2,1,0:T(8,128)(2,1)}, bf16[2,256,1024]{2,1,0:T(8,128)(2,1)}, u32[]{:S(2)}, u32[]{:S(2)}) collective-permute-start(bf16[2,256,1024]{2,1,0:T(8,128)(2,1)} %get-tuple-element.183), channel_id=1, source_target_pairs={{0,16},{1,17},{2,18},{3,19},{4,20},{5,21},{6,22},{7,23},{8,24},{9,... | collective-permute-start | bytes 3145736 | tf_op jit(solution)/shard_map/ppermute | solution.py:460
  764.1 179.7 %collective-permute-start.29 = (bf16[2,4,256,1152]{3,2,1,0:T(8,128)(2,1)}, bf16[2,4,256,1152]{3,2,1,0:T(8,128)(2,1)}, u32[]{:S(2)}, u32[]{:S(2)}) collective-permute-start(bf16[2,4,256,1152]{3,2,1,0:T(8,128)(2,1)} %grad_send.11), channel_id=1, source_target_pairs={{0,4},{1,5},{2,6},{3,7},{4,0},{5,1},{6,2},{7,3},{8,12},{9,13},{10,... | collective-permute-start | bytes 14155784 | tf_op jit(solution)/shard_map/ppermute | solution.py:460
  766.4 29.1 %collective-permute-start.51 = (bf16[2,256,1024]{2,1,0:T(8,128)(2,1)}, bf16[2,256,1024]{2,1,0:T(8,128)(2,1)S(1)}, u32[]{:S(2)}, u32[]{:S(2)}) collective-permute-start(bf16[2,256,1024]{2,1,0:T(8,128)(2,1)} %get-tuple-element.149), channel_id=1, source_target_pairs={{0,8},{1,9},{2,10},{3,11},{4,12},{5,13},{6,14},{7,15},{8,0},{9,1},... | collective-permute-start | bytes 3145736 | tf_op jit(solution)/shard_map/ppermute | solution.py:460
  768.0 13.5 %collective-permute-start.26 = (f32[24576]{0:T(1024)S(1)}, f32[24576]{0:T(1024)S(1)}, u32[]{:S(2)}, u32[]{:S(2)}) collective-permute-start(f32[24576]{0:T(1024)S(1)} %add.403), channel_id=1, source_target_pairs={{0,2},{1,3},{2,0},{3,1},{4,6},{5,7},{6,4},{7,5},{8,10},{9,11},{10,... | collective-permute-start | bytes 294920 | tf_op jit(solution)/shard_map/ppermute | solution.py:460
  781.5 29.0 %collective-permute-start.62 = (bf16[2,256,1024]{2,1,0:T(8,128)(2,1)S(1)}, bf16[2,256,1024]{2,1,0:T(8,128)(2,1)S(1)}, u32[]{:S(2)}, u32[]{:S(2)}) collective-permute-start(bf16[2,256,1024]{2,1,0:T(8,128)(2,1)S(1)} %copy-done.67), channel_id=1, source_target_pairs={{0,16},{1,17},{2,18},{3,19},{4,20},{5,21},{6,22},{7,23},{8,24},{9,... | collective-permute-start | bytes 3145736 | tf_op jit(solution)/shard_map/ppermute | solution.py:460
  790.5 26.1 %collective-permute-start.60 = (bf16[2,256,1024]{2,1,0:T(8,128)(2,1)S(1)}, bf16[2,256,1024]{2,1,0:T(8,128)(2,1)S(1)}, u32[]{:S(2)}, u32[]{:S(2)}) collective-permute-start(bf16[2,256,1024]{2,1,0:T(8,128)(2,1)S(1)} %copy-done.66), channel_id=1, source_target_pairs={{0,8},{1,9},{2,10},{3,11},{4,12},{5,13},{6,14},{7,15},{8,0},{9,1},... | collective-permute-start | bytes 3145736 | tf_op jit(solution)/shard_map/ppermute | solution.py:460
  795.5 32.3 %collective-permute-start.54 = (bf16[1,256,1024]{2,1,0:T(8,128)(2,1)S(1)}, bf16[1,256,1024]{2,1,0:T(8,128)(2,1)S(1)}, u32[]{:S(2)}, u32[]{:S(2)}) collective-permute-start(bf16[1,256,1024]{2,1,0:T(8,128)(2,1)S(1)} %slice.143), channel_id=1, source_target_pairs={{0,8},{1,9},{2,10},{3,11},{4,12},{5,13},{6,14},{7,15},{8,0},{9,1},... | collective-permute-start | bytes 1572872 | tf_op jit(solution)/shard_map/ppermute | solution.py:460
  810.5 18.4 %collective-permute-start.52 = (bf16[1,256,1024]{2,1,0:T(8,128)(2,1)S(1)}, bf16[1,256,1024]{2,1,0:T(8,128)(2,1)S(1)}, u32[]{:S(2)}, u32[]{:S(2)}) collective-permute-start(bf16[1,256,1024]{2,1,0:T(8,128)(2,1)S(1)} %slice.141), channel_id=1, source_target_pairs={{0,16},{1,17},{2,18},{3,19},{4,20},{5,21},{6,22},{7,23},{8,24},{9,... | collective-permute-start | bytes 1572872 | tf_op jit(solution)/shard_map/ppermute | solution.py:460
  816.6 20.5 %collective-permute-start.63 = (bf16[1,256,1024]{2,1,0:T(8,128)(2,1)S(1)}, bf16[1,256,1024]{2,1,0:T(8,128)(2,1)S(1)}, u32[]{:S(2)}, u32[]{:S(2)}) collective-permute-start(bf16[1,256,1024]{2,1,0:T(8,128)(2,1)S(1)} %slice.151), channel_id=1, source_target_pairs={{0,8},{1,9},{2,10},{3,11},{4,12},{5,13},{6,14},{7,15},{8,0},{9,1},... | collective-permute-start | bytes 1572872 | tf_op jit(solution)/shard_map/ppermute | solution.py:460
  827.8 20.2 %collective-permute-start.61 = (bf16[1,256,1024]{2,1,0:T(8,128)(2,1)S(1)}, bf16[1,256,1024]{2,1,0:T(8,128)(2,1)S(1)}, u32[]{:S(2)}, u32[]{:S(2)}) collective-permute-start(bf16[1,256,1024]{2,1,0:T(8,128)(2,1)S(1)} %slice.149), channel_id=1, source_target_pairs={{0,16},{1,17},{2,18},{3,19},{4,20},{5,21},{6,22},{7,23},{8,24},{9,... | collective-permute-start | bytes 1572872 | tf_op jit(solution)/shard_map/ppermute | solution.py:460
  830.1 110.7 %collective-permute-start.55 = (bf16[256,2048]{1,0:T(8,128)(2,1)}, bf16[256,2048]{1,0:T(8,128)(2,1)}, u32[]{:S(2)}, u32[]{:S(2)}) collective-permute-start(bf16[256,2048]{1,0:T(8,128)(2,1)} %pad_maximum_fusion.1), channel_id=1, source_target_pairs={{0,2},{1,3},{2,0},{3,1},{4,6},{5,7},{6,4},{7,5},{8,10},{9,11},{10,... | collective-permute-start | bytes 3145736 | tf_op jit(solution)/shard_map/ppermute | solution.py:460
  847.2 109.0 %collective-permute-start.42 = (bf16[2,256,1024]{2,1,0:T(8,128)(2,1)}, bf16[2,256,1024]{2,1,0:T(8,128)(2,1)}, u32[]{:S(2)}, u32[]{:S(2)}) collective-permute-start(bf16[2,256,1024]{2,1,0:T(8,128)(2,1)} %get-tuple-element.177), channel_id=1, source_target_pairs={{0,16},{1,17},{2,18},{3,19},{4,20},{5,21},{6,22},{7,23},{8,24},{9,... | collective-permute-start | bytes 3145736 | tf_op jit(solution)/shard_map/ppermute | solution.py:460
  849.3 113.7 %collective-permute-start.64 = (bf16[256,2048]{1,0:T(8,128)(2,1)}, bf16[256,2048]{1,0:T(8,128)(2,1)}, u32[]{:S(2)}, u32[]{:S(2)}) collective-permute-start(bf16[256,2048]{1,0:T(8,128)(2,1)} %pad_maximum_fusion.2), channel_id=1, source_target_pairs={{0,2},{1,3},{2,0},{3,1},{4,6},{5,7},{6,4},{7,5},{8,10},{9,11},{10,... | collective-permute-start | bytes 3145736 | tf_op jit(solution)/shard_map/ppermute | solution.py:460
  853.4 106.4 %collective-permute-start.40 = (bf16[2,256,1024]{2,1,0:T(8,128)(2,1)}, bf16[2,256,1024]{2,1,0:T(8,128)(2,1)S(1)}, u32[]{:S(2)}, u32[]{:S(2)}) collective-permute-start(bf16[2,256,1024]{2,1,0:T(8,128)(2,1)} %get-tuple-element.169), channel_id=1, source_target_pairs={{0,8},{1,9},{2,10},{3,11},{4,12},{5,13},{6,14},{7,15},{8,0},{9,1},... | collective-permute-start | bytes 3145736 | tf_op jit(solution)/shard_map/ppermute | solution.py:460
  954.6 44.5 %collective-permute-start.32 = (bf16[2,256,1152]{2,1,0:T(8,128)(2,1)}, bf16[2,256,1152]{2,1,0:T(8,128)(2,1)}, u32[]{:S(2)}, u32[]{:S(2)}) collective-permute-start(bf16[2,256,1152]{2,1,0:T(8,128)(2,1)} %get-tuple-element.174), channel_id=1, source_target_pairs={{0,16},{1,17},{2,18},{3,19},{4,20},{5,21},{6,22},{7,23},{8,24},{9,... | collective-permute-start | bytes 3538952 | tf_op jit(solution)/shard_map/ppermute | solution.py:460
  958.7 15.2 %collective-permute-start.43 = (bf16[1,256,1024]{2,1,0:T(8,128)(2,1)}, bf16[1,256,1024]{2,1,0:T(8,128)(2,1)}, u32[]{:S(2)}, u32[]{:S(2)}) collective-permute-start(bf16[1,256,1024]{2,1,0:T(8,128)(2,1)} %slice.135), channel_id=1, source_target_pairs={{0,8},{1,9},{2,10},{3,11},{4,12},{5,13},{6,14},{7,15},{8,0},{9,1},... | collective-permute-start | bytes 1572872 | tf_op jit(solution)/shard_map/ppermute | solution.py:460
  961.1 32.3 %collective-permute-start.41 = (bf16[1,256,1024]{2,1,0:T(8,128)(2,1)}, bf16[1,256,1024]{2,1,0:T(8,128)(2,1)}, u32[]{:S(2)}, u32[]{:S(2)}) collective-permute-start(bf16[1,256,1024]{2,1,0:T(8,128)(2,1)} %slice.133), channel_id=1, source_target_pairs={{0,16},{1,17},{2,18},{3,19},{4,20},{5,21},{6,22},{7,23},{8,24},{9,... | collective-permute-start | bytes 1572872 | tf_op jit(solution)/shard_map/ppermute | solution.py:460
  966.3 36.3 %collective-permute-start.30 = (bf16[2,256,1152]{2,1,0:T(8,128)(2,1)}, bf16[2,256,1152]{2,1,0:T(8,128)(2,1)S(1)}, u32[]{:S(2)}, u32[]{:S(2)}) collective-permute-start(bf16[2,256,1152]{2,1,0:T(8,128)(2,1)} %get-tuple-element.172), channel_id=1, source_target_pairs={{0,8},{1,9},{2,10},{3,11},{4,12},{5,13},{6,14},{7,15},{8,0},{9,1},... | collective-permute-start | bytes 3538952 | tf_op jit(solution)/shard_map/ppermute | solution.py:460
  995.3 23.8 %collective-permute-start.44 = (bf16[256,512]{1,0:T(8,128)(2,1)S(1)}, bf16[256,512]{1,0:T(8,128)(2,1)S(1)}, u32[]{:S(2)}, u32[]{:S(2)}) collective-permute-start(bf16[256,512]{1,0:T(8,128)(2,1)S(1)} %get-tuple-element.233), channel_id=1, source_target_pairs={{0,1},{1,2},{2,3},{3,0},{4,5},{5,6},{6,7},{7,4},{8,9},{9,10},{10,1... | collective-permute-start | bytes 786440 | tf_op jit(solution)/shard_map/ppermute | solution.py:460
  995.4 23.8 %collective-permute-start.45 = (bf16[256,512]{1,0:T(8,128)(2,1)S(1)}, bf16[256,512]{1,0:T(8,128)(2,1)S(1)}, u32[]{:S(2)}, u32[]{:S(2)}) collective-permute-start(bf16[256,512]{1,0:T(8,128)(2,1)S(1)} %get-tuple-element.234), channel_id=1, source_target_pairs={{0,2},{1,3},{2,0},{3,1},{4,6},{5,7},{6,4},{7,5},{8,10},{9,11},{10,... | collective-permute-start | bytes 786440 | tf_op jit(solution)/shard_map/ppermute | solution.py:460
  996.2 24.6 %collective-permute-start.46 = (bf16[256,512]{1,0:T(8,128)(2,1)S(1)}, bf16[256,512]{1,0:T(8,128)(2,1)S(1)}, u32[]{:S(2)}, u32[]{:S(2)}) collective-permute-start(bf16[256,512]{1,0:T(8,128)(2,1)S(1)} %get-tuple-element.235), channel_id=1, source_target_pairs={{0,3},{1,0},{2,1},{3,2},{4,7},{5,4},{6,5},{7,6},{8,11},{9,8},{10,9... | collective-permute-start | bytes 786440 | tf_op jit(solution)/shard_map/ppermute | solution.py:460
  1000.9 13.6 %collective-permute-start.33 = (bf16[1,256,1152]{2,1,0:T(8,128)(2,1)S(1)}, bf16[1,256,1152]{2,1,0:T(8,128)(2,1)S(1)}, u32[]{:S(2)}, u32[]{:S(2)}) collective-permute-start(bf16[1,256,1152]{2,1,0:T(8,128)(2,1)S(1)} %slice.130), channel_id=1, source_target_pairs={{0,8},{1,9},{2,10},{3,11},{4,12},{5,13},{6,14},{7,15},{8,0},{9,1},... | collective-permute-start | bytes 1769480 | tf_op jit(solution)/shard_map/ppermute | solution.py:460
  1003.0 13.4 %collective-permute-start.31 = (bf16[1,256,1152]{2,1,0:T(8,128)(2,1)S(1)}, bf16[1,256,1152]{2,1,0:T(8,128)(2,1)S(1)}, u32[]{:S(2)}, u32[]{:S(2)}) collective-permute-start(bf16[1,256,1152]{2,1,0:T(8,128)(2,1)S(1)} %slice.128), channel_id=1, source_target_pairs={{0,16},{1,17},{2,18},{3,19},{4,20},{5,21},{6,22},{7,23},{8,24},{9,... | collective-permute-start | bytes 1769480 | tf_op jit(solution)/shard_map/ppermute | solution.py:460
  1014.7 15.4 %collective-permute-start.37 = (bf16[64,256]{1,0:T(8,128)(2,1)S(1)}, bf16[64,256]{1,0:T(8,128)(2,1)S(1)}, u32[]{:S(2)}, u32[]{:S(2)}) collective-permute-start(bf16[64,256]{1,0:T(8,128)(2,1)S(1)} %get-tuple-element.236), channel_id=1, source_target_pairs={{0,1},{1,2},{2,3},{3,0},{4,5},{5,6},{6,7},{7,4},{8,9},{9,10},{10,1... | collective-permute-start | bytes 98312 | tf_op jit(solution)/shard_map/ppermute | solution.py:460
  1016.4 18.4 %collective-permute-start.39 = (bf16[64,256]{1,0:T(8,128)(2,1)S(1)}, bf16[64,256]{1,0:T(8,128)(2,1)S(1)}, u32[]{:S(2)}, u32[]{:S(2)}) collective-permute-start(bf16[64,256]{1,0:T(8,128)(2,1)S(1)} %get-tuple-element.237), channel_id=1, source_target_pairs={{0,3},{1,0},{2,1},{3,2},{4,7},{5,4},{6,5},{7,6},{8,11},{9,8},{10,9... | collective-permute-start | bytes 98312 | tf_op jit(solution)/shard_map/ppermute | solution.py:460
  1019.1 15.8 %collective-permute-start.38 = (bf16[64,256]{1,0:T(8,128)(2,1)S(1)}, bf16[64,256]{1,0:T(8,128)(2,1)}, u32[]{:S(2)}, u32[]{:S(2)}) collective-permute-start(bf16[64,256]{1,0:T(8,128)(2,1)S(1)} %get-tuple-element.238), channel_id=1, source_target_pairs={{0,2},{1,3},{2,0},{3,1},{4,6},{5,7},{6,4},{7,5},{8,10},{9,11},{10,... | collective-permute-start | bytes 98312 | tf_op jit(solution)/shard_map/ppermute | solution.py:460
  1019.2 17.1 %collective-permute-start.34 = (bf16[256,512]{1,0:T(8,128)(2,1)S(1)}, bf16[256,512]{1,0:T(8,128)(2,1)S(1)}, u32[]{:S(2)}, u32[]{:S(2)}) collective-permute-start(bf16[256,512]{1,0:T(8,128)(2,1)S(1)} %get-tuple-element.230), channel_id=1, source_target_pairs={{0,1},{1,2},{2,3},{3,0},{4,5},{5,6},{6,7},{7,4},{8,9},{9,10},{10,1... | collective-permute-start | bytes 786440 | tf_op jit(solution)/shard_map/ppermute | solution.py:460
  1020.8 19.7 %collective-permute-start.35 = (bf16[256,512]{1,0:T(8,128)(2,1)S(1)}, bf16[256,512]{1,0:T(8,128)(2,1)S(1)}, u32[]{:S(2)}, u32[]{:S(2)}) collective-permute-start(bf16[256,512]{1,0:T(8,128)(2,1)S(1)} %get-tuple-element.231), channel_id=1, source_target_pairs={{0,2},{1,3},{2,0},{3,1},{4,6},{5,7},{6,4},{7,5},{8,10},{9,11},{10,... | collective-permute-start | bytes 786440 | tf_op jit(solution)/shard_map/ppermute | solution.py:460
  (91 other events, 1078.1 us)
Sparse Core Ops, SparseCore 0:
  34.3 59.1 all-gather.17
  95.4 54.3 all-gather.7
  226.4 52.2 all-gather.9
  398.6 57.1 all-gather.13
  548.6 150.9 all-gather.11
  720.8 219.3 all-gather.15

commit v2 on v1

--- a/solution.py
+++ b/solution.py
@@ -57,26 +57,27 @@
     return jax.ShapeDtypeStruct(shape, dtype)
 
 
-def ln_kernel(x_ref, g_ref, b_ref, o_ref):
+def ln_kernel(win_ref, x_ref, g_ref, b_ref, o_ref):
     x = x_ref[...].astype(F32)
     c = x - jnp.mean(x, axis=-1, keepdims=True)
     v = jnp.mean(c * c, axis=-1, keepdims=True)
     o_ref[...] = (c * lax.rsqrt(v + EPS) * g_ref[...].astype(F32) + b_ref[...].astype(F32)).astype(BF16)
 
 
-def layer_norm(x, gain, bias):
-    t, d = x.shape
+def layer_norm(win, x, gain, bias, t):
+    d = x.shape[1]
     br = 256
     return call(
         ln_kernel,
         (t // br,),
-        [pl.BlockSpec((br, d), lambda i: (i, 0)), whole((1, d)), whole((1, d))],
-        pl.BlockSpec((br, d), lambda i: (i, 0)),
+        [pl.BlockSpec((br, d), lambda i, win_ref: (win_ref[0] * (t // br) + i, 0)), whole((1, d)), whole((1, d))],
+        pl.BlockSpec((br, d), lambda i, *_: (i, 0)),
         shape_of((t, d), BF16),
+        prefetch=1,
         flops=8 * t * d,
         nbytes=4 * t * d,
         name="norm1",
-    )(x, gain, bias)
+    )(win, x, gain, bias)
 
 
 def attn_fwd_kernel(scale, qb, q_ref, k_ref, vt_ref, dcol_ref, drow_ref, o_ref, mask):
@@ -145,7 +146,7 @@
 def proj_ln(att, w, x, out_bias, gain, bias):
     r, width = att.shape
     d = x.shape[1]
-    br = min(128, r)
+    br = min(256, r)
     row = pl.BlockSpec((br, d), lambda i: (i, 0))
     return call(
         proj_ln_kernel,
@@ -159,34 +160,78 @@
     )(att, w, x, out_bias, gain, bias)
 
 
-def up_kernel(n_ref, w_ref, b_ref, da_ref, act_ref, gb_ref, gs_ref):
-    v = dot_nn(n_ref[...], w_ref[...]) + b_ref[...].astype(F32)
+def gelu_parts(v):
     v2 = v * v
-    t = jnp.tanh(GELU_A * v * (1.0 + GELU_B * v2))
-    half = 0.5 * (1.0 + t)
-    act_ref[...] = (v * half).astype(BF16)
-    slope = half + 0.5 * v * (1.0 - t * t) * (GELU_A * (1.0 + 3.0 * GELU_B * v2))
-    gb = (da_ref[...].astype(F32) * slope).astype(BF16)
-    gb_ref[...] = gb
-    gs_ref[...] = jnp.sum(gb.astype(F32), axis=0, keepdims=True)
-
-
-def ffn_up(n, w, b, da):
+    g = 1.0 / (1.0 + jnp.exp2(v * (-2.0 * GELU_A * LOG2E * (1.0 + GELU_B * v2))))
+    return v * g, g + v * (g * (1.0 - g)) * (2.0 * GELU_A * (1.0 + 3.0 * GELU_B * v2))
+
+
+def up_kernel(ready, n_ref, w_ref, b_ref, *refs):
+    r = n_ref.shape[0]
+    parts = 2 if ready else 1
+    pair_ref, gs_ref = refs[-2:]
+    total = None
+    for i in range(parts):
+        at = pl.ds(i * (r // parts), r // parts)
+        v = dot_nn(n_ref[at, :], w_ref[...]) + b_ref[...].astype(F32)
+        da = refs[0][at, :].astype(F32) if ready else dot_nt(refs[0][at, :], refs[1][...])
+        act, slope = gelu_parts(v)
+        pair_ref[0, at, :] = act.astype(BF16)
+        gb = (da * slope).astype(BF16)
+        pair_ref[1, at, :] = gb
+        part = jnp.sum(gb.astype(F32), axis=0, keepdims=True)
+        total = part if total is None else total + part
+    gs_ref[...] = total
+
+
+def ffn_up(n, w, b, da=None, go=None, down=None):
     r, d = n.shape
     u = w.shape[1]
-    bn = 256
+    ready = da is not None
+    bn = min(512 if ready else 256, u)
     col = pl.BlockSpec((r, bn), lambda j: (0, j))
+    line = pl.BlockSpec((1, bn), lambda j: (0, j))
+    extra = [col] if ready else [whole((r, d)), pl.BlockSpec((bn, d), lambda j: (j, 0))]
     return call(
-        up_kernel,
+        functools.partial(up_kernel, ready),
         (u // bn,),
-        [whole((r, d)), pl.BlockSpec((d, bn), lambda j: (0, j)), pl.BlockSpec((1, bn), lambda j: (0, j)), col],
-        [col, col, pl.BlockSpec((1, bn), lambda j: (0, j))],
-        [shape_of((r, u), BF16), shape_of((r, u), BF16), shape_of((1, u), F32)],
-        flops=2 * r * d * u,
+        [whole((r, d)), pl.BlockSpec((d, bn), lambda j: (0, j)), line] + extra,
+        [pl.BlockSpec((2, r, bn), lambda j: (0, 0, j)), line],
+        [shape_of((2, r, u), BF16), shape_of((1, u), F32)],
+        flops=(2 if ready else 4) * r * d * u,
         nbytes=2 * d * u + 6 * r * u + 2 * r * d,
         trans=r * u,
         name="ffn_up",
-    )(n, w, b, da)
+    )(n, w, b, *((da,) if ready else (go, down)))
+
+
+def product_kernel(count, nt, *refs):
+    acc = None
+    for x, w in zip(refs[:count], refs[count : 2 * count]):
+        part = (dot_nt if nt else dot_nn)(x[...], w[...])
+        acc = part if acc is None else acc + part
+    refs[-1][...] = acc.astype(BF16)
+
+
+def plane(x, i):
+    return pl.BlockSpec((None,) + x.shape[1:], lambda *_: (i, 0, 0), pipeline_mode=pl.Buffered(1))
+
+
+def product(xs, at, ws, nt):
+    r, k = xs[0].shape[1:]
+    n = ws[0].shape[0 if nt else 1]
+    bn = 512
+    wspec = pl.BlockSpec((bn, k), lambda j: (j, 0)) if nt else pl.BlockSpec((k, bn), lambda j: (0, j))
+    return call(
+        functools.partial(product_kernel, len(xs), nt),
+        (n // bn,),
+        [plane(x, at) for x in xs] + [wspec] * len(xs),
+        pl.BlockSpec((r, bn), lambda j: (0, j)),
+        shape_of((r, n), BF16),
+        flops=2 * r * k * n * len(xs),
+        nbytes=len(xs) * 2 * k * (r + n) + 2 * r * n,
+        name="product",
+    )(*xs, *ws)
 
 
 def norm2_back_kernel(count, *refs):
@@ -224,7 +269,7 @@
 def norm2_back(parts, h, go, gain, w):
     r, d = h.shape
     width = w.shape[1]
-    br = min(128, r)
+    br = min(256, r)
     row = pl.BlockSpec((br, d), lambda i: (i, 0))
     wide = pl.BlockSpec((br, width), lambda i: (i, 0))
     return call(
@@ -277,18 +322,19 @@
         gq_ref[pl.ds(j * qb, qb), :] = dot_nn(kt_ref[:, pl.ds(lo, span)], ds).T.astype(BF16)
 
 
-def attn_bwd(row0, q, go, k, v, kt, dcol, drow, hd):
-    r, width = q.shape
+def attn_bwd(part, parts, row0, q, go, k, v, kt, dcol, drow, hd):
+    r, width = q.shape[0], q.shape[1] // parts
     s = k.shape[0]
     heads = width // hd
     qb = min(256, r)
     reach = s // 2
     head = pl.BlockSpec((r, hd), lambda h, *_: (0, h))
+    head_in = pl.BlockSpec((r, hd), lambda h, *_: (0, h + part * heads))
     keep = pl.BlockSpec((s, hd), lambda h, *_: (0, 0))
     return call(
         functools.partial(attn_bwd_kernel, hd**-0.5, qb, reach),
         (heads,),
-        [head, head, whole((s, hd)), whole((s, hd)), whole((hd, s)), whole((s, 1)), whole((1, r))],
+        [head_in, head_in, whole((s, hd)), whole((s, hd)), whole((hd, s)), whole((s, 1)), whole((1, r))],
         [head, keep, keep],
         [shape_of((r, width), BF16), shape_of((s, hd), F32), shape_of((s, hd), F32)],
         scratch=[pltpu.VMEM((r // qb, reach + qb, qb), F32)],
@@ -324,7 +370,7 @@
 
 def norm1_back(gq, gkv, wq, wkv, x, gh, gain):
     r, d = x.shape
-    br = min(128, r)
+    br = min(256, r)
     row = pl.BlockSpec((br, d), lambda i: (i, 0))
     kvw = gkv.shape[1]
     return call(
@@ -344,80 +390,102 @@
     return [order, order[1:] + order[:1]]
 
 
-def block_at(m, p, order):
-    nb = len(order)
-    b = 0
-    for k, bit in enumerate(order):
-        b = b + ((((p >> (nb - 1 - k)) & 1) ^ 1 ^ ((m >> (bit + 1)) & 1)) << bit)
-    return b
-
-
-def grad_kernel(count, keep, m_ref, *refs):
-    left, right = refs[:count], refs[count : 2 * count]
-    acc = dot_tn(left[0][...], right[0][...])
-    for a, b in zip(left[1:], right[1:]):
-        acc = acc + dot_tn(a[...], b[...])
-    if not keep:
-        refs[2 * count][0, 0] = acc.astype(BF16)
-        return
-    acc = (acc + refs[2 * count][0, 0].astype(F32)).astype(BF16)
-    half = pl.program_id(0)
+def place_in(p, bits, order):
+    rel = {bit: (p >> (bits - 1 - k)) & 1 for k, bit in enumerate(range(bits))}
+    out = 0
+    for bit in order:
+        out = 2 * out + rel[bit]
+    return out
+
+
+def table(p, values):
+    out = values[0]
+    for i, v in enumerate(values[1:], 1):
+        out = jnp.where(p == i, v, out)
+    return out
+
+
+def grad_kernel(count, pairs, places, m_ref, *refs):
+    lefts = [refs[i * count : (i + 1) * count] for i in range(pairs)]
+    rights = [refs[(pairs + i) * count : (pairs + i + 1) * count] for i in range(pairs)]
+    outs = refs[2 * pairs * count :]
+    bits = places.bit_length() - 1
     p = pl.program_id(1)
-    places = pl.num_programs(1)
-    for h in range(2):
-        send_ref, keep_ref = refs[2 * count + 1 + 2 * h], refs[2 * count + 2 + 2 * h]
-
-        @pl.when((half == h) & (p < places // 2))
-        def _(send_ref=send_ref):
-            send_ref[0] = acc
-
-        @pl.when((half == h) & (p >= places // 2))
-        def _(keep_ref=keep_ref):
-            keep_ref[0] = acc
-
-
-def grad_call(m, ndp, lefts, rights, got=None):
-    keep = got is not None
-    d, n = lefts[0].shape[1], rights[0].shape[1]
+    cut = rights[0][0].shape[1] // 2
+
+    def run(left, right):
+        acc = dot_tn(left[0][...], right[0][...])
+        for a, b in zip(left[1:], right[1:]):
+            acc = acc + dot_tn(a[...], b[...])
+        acc = acc.astype(BF16)
+        for h, order in enumerate(stage_orders(bits)):
+            sent = [place_in(i, bits, order) < places // 2 for i in range(places)]
+            here = table(p, sent)
+            send_ref, keep_ref = outs[2 * h], outs[2 * h + 1]
+            part = acc[:, h * cut : (h + 1) * cut]
+
+            @pl.when(here)
+            def _(send_ref=send_ref, part=part):
+                send_ref[0, 0] = part
+
+            @pl.when(jnp.logical_not(here))
+            def _(keep_ref=keep_ref, part=part):
+                keep_ref[0, 0] = part
+
+    for i in range(pairs):
+        pl.when(pl.program_id(0) == i)(functools.partial(run, lefts[i], rights[i]))
+
+
+def grad_call(m, ndp, lefts, rights):
+    pairs, count = len(lefts), len(lefts[0])
+    d, n = lefts[0][0].shape[1], rights[0][0][0].shape[2]
     places = ndp // 2
+    bits = places.bit_length() - 1
     hp = places // 2
     f = d // ndp
-    orders = stage_orders(places.bit_length() - 1)
-
-    def left_map(h, p, m_ref):
+
+    def left_map(own, i, p, m_ref):
         me = m_ref[0]
-        b = jnp.where(h == 0, block_at(me, p, orders[0]), block_at(me, p, orders[1]))
-        core = me & 1
-        return (0, 2 * b + (core if keep else 1 - core))
-
-    specs = [pl.BlockSpec((a.shape[0], f), left_map) for a in lefts]
-    specs += [pl.BlockSpec((b.shape[0], n // 2), lambda h, p, *_: (0, h)) for b in rights]
-    block = pl.BlockSpec((1, 1, f, n // 2), lambda h, p, *_: (h, p, 0, 0))
-    if keep:
-        specs.append(block)
-        outs, shapes = [], []
-        for half in range(2):
-            outs.append(
-                pl.BlockSpec((1, f, n // 2), lambda h, p, *_, half=half: (jnp.where(h == half, jnp.minimum(p, hp - 1), (h > half) * (hp - 1)), 0, 0))
-            )
-            outs.append(
-                pl.BlockSpec((1, f, n // 2), lambda h, p, *_, half=half: (jnp.where(h == half, jnp.maximum(p - hp, 0), (h > half) * (hp - 1)), 0, 0))
-            )
-            shapes += [shape_of((hp, f, n // 2), BF16)] * 2
-    else:
-        outs, shapes = block, shape_of((2, places, f, n // 2), BF16)
-    k = sum(a.shape[0] for a in lefts)
+        p = jnp.where(i < own, 0, jnp.where(i > own, places - 1, p))
+        b = 0
+        for k in range(bits):
+            b = b + ((((p >> (bits - 1 - k)) & 1) ^ 1 ^ ((me >> (k + 1)) & 1)) << k)
+        return (0, 2 * b + (me & 1))
+
+    specs = [pl.BlockSpec((a.shape[0], f), functools.partial(left_map, i)) for i in range(pairs) for a in lefts[i]]
+    specs += [plane(b, at) for i in range(pairs) for b, at in rights[i]]
+    outs, shapes = [], []
+    for order in stage_orders(bits):
+        at = [place_in(i, bits, order) for i in range(places)]
+        for first in (0, hp):
+            seen = [next((a - first for a in at[: i + 1][::-1] if 0 <= a - first < hp), None) for i in range(places)]
+            start = next(a for a in seen if a is not None)
+            seen = [start if a is None else a for a in seen]
+            outs.append(pl.BlockSpec((1, 1, f, n // 2), lambda i, p, *_, seen=seen: (i, table(p, seen), 0, 0)))
+            shapes.append(shape_of((pairs, hp, f, n // 2), BF16))
+    k = sum(a.shape[0] for a in lefts[0]) * pairs
     return call(
-        functools.partial(grad_kernel, len(lefts), keep),
-        (2, places),
+        functools.partial(grad_kernel, count, pairs, places),
+        (pairs, places),
         specs,
         outs,
         shapes,
         prefetch=1,
         flops=k * d * n,
-        nbytes=2 * k * (d + n) + d * n,
-        name="grad_keep" if keep else "grad_send",
-    )(m, *lefts, *rights, *((got,) if keep else ()))
+        nbytes=k * d + 2 * k * n + pairs * d * n,
+        name="weight_grad",
+    )(m, *[a for l in lefts for a in l], *[b for r in rights for b, _ in r])
+
+
+def copy_kernel(x_ref, o_ref):
+    o_ref[...] = x_ref[...]
+
+
+def copied(x):
+    t, d = x.shape
+    br = 256
+    row = pl.BlockSpec((br, d), lambda i: (i, 0))
+    return call(copy_kernel, (t // br,), [row], row, shape_of((t, d), x.dtype), nbytes=4 * t * d, name="copied")(x)
 
 
 def per_device(
@@ -498,184 +566,259 @@
 
     slab = d // ndp
     uslab = units // ndp
-    wo_cols = lax.dynamic_slice_in_dim(out_weight, m * slab, slab, axis=1)
-    wo_z = spread(wo_cols, 0)
-    wo = lax.all_gather(wo_z, "dp", axis=0, tiled=False)
-
-    n1 = seq_out(layer_norm(tokens, n1g, n1b))
+
+    def arrive(x):
+        return after(x, tok[0])
+
+    def core_swap(x):
+        return perm(x, to_dp=lambda a: a ^ 1)
+
+    def spread_send(piece):
+        return [piece] + [tp_shift(piece, s) for s in range(1, n)]
+
+    def spread_place(gots, axis):
+        size = gots[0].shape[axis]
+        shape = list(gots[0].shape)
+        shape[axis] = n * size
+        full = jnp.zeros(shape, gots[0].dtype)
+        for s in range(n):
+            at = [0, 0]
+            at[axis] = tp_at(-s) * size
+            full = lax.dynamic_update_slice(full, gots[s] if s == 0 else arrive(gots[s]), at)
+        return seq_out(full)
+
+    wq_far = [tp_shift(rows_at(query_weight, m * slab, slab), t * group) for t in range(1, wins)]
+    qb_far = [tp_shift(query_bias, t * group) for t in range(1, wins)]
+    wo_got = spread_send(lax.dynamic_slice_in_dim(out_weight, m * slab, slab, axis=1))
+    n1 = seq_out(layer_norm(win.reshape(1), tokens, n1g, n1b, seq))
     kv = seq_out(jnp.dot(n1, keyval_weight, preferred_element_type=F32))
     keys = kv[:, :hd].astype(BF16)
     values = (kv[:, hd:] + value_bias.astype(F32)).astype(BF16)
-    q = seq_out((jnp.dot(seq_in(n1), query_weight, preferred_element_type=F32) + query_bias.astype(F32)).astype(BF16))
-    dcol = doc_ids.reshape(t_all, 1)
-    att = seq_out(attn_fwd(q, keys, values.T, dcol, doc_ids.reshape(wins, 1, seq), seq, hd))
-
-    up_far, down_far, upb_far = [], [], []
-    att_gots = []
-    for t in range(1, wins):
-        up_far.append(tp_shift(after(rows_at(up_weight, m * slab, slab), wo_z), t * group))
-        upb_far.append(tp_shift(vec(up_bias), t * group))
-    for s in range(1, n):
-        att_gots.append(tp_shift(rows_at(att, tp_at(s) * rows, rows), s))
-    for t in range(1, wins):
-        down_far.append(tp_shift(after(rows_at(down_weight, m * uslab, uslab), att_gots[n // 2 - 1]), t * group))
-    up_far = [lax.all_gather(after(a, wo), "dp", axis=0, tiled=True) for a in up_far]
-    down_far = [lax.all_gather(after(b, a), "dp", axis=0, tiled=True) for a, b in zip(up_far, down_far)]
-
+    values_t = values.T
+    dcol = rows_at(doc_ids, win, 1).reshape(seq, 1)
+    drow = rows_at(doc_ids, win, 1).reshape(1, 1, seq)
+    wq_far = [lax.all_gather(after(a, kv), "dp", axis=0, tiled=True) for a in wq_far]
     go = [rows_at(grad_out, (win * group + lax.rem(r + group - s, group)) * rows, rows) for s in range(group)]
-
-    def grad_act(s, w):
-        return seq_out(lax.dot_general(seq_in(go[s]), w, (((1,), (1,)), ((), ())), preferred_element_type=F32).astype(BF16))
-
-    das = [[grad_act(s, down_weight)] for s in range(group)]
-
+    das = []
+
+    def grad_act(s):
+        das.append(seq_out(lax.dot_general(seq_in(go[s]), down_weight, (((1,), (1,)), ((), ())), preferred_element_type=F32).astype(BF16)))
+
+    def heads(w, b):
+        q = seq_out((jnp.dot(seq_in(n1), w, preferred_element_type=F32) + b.astype(F32)).astype(BF16))
+        att = seq_out(attn_fwd(q, keys, values_t, dcol, drow, seq, hd))
+        got = [rows_at(att, r * rows, rows)]
+        return got + [group_shift(rows_at(att, lax.rem(r + s, group) * rows, rows), s) for s in range(1, group)]
+
+    att_got = [heads(query_weight, query_bias)]
+    wo_z = spread_place(wo_got, 0)
+    wo = lax.all_gather(wo_z, "dp", axis=0, tiled=False)
+    up_far = [tp_shift(after(rows_at(up_weight, m * slab, slab), wo_z), t * group) for t in range(1, wins)]
+    upb_far = [tp_shift(vec(up_bias), t * group) for t in range(1, wins)]
+    for w, b in zip(wq_far, qb_far):
+        att_got.append(heads(w, b))
+    down_far = [tp_shift(arrive(rows_at(down_weight, m * uslab, uslab)), t * group) for t in range(1, wins)]
     att_own = jnp.zeros((rows, n * lq), BF16)
-    att_own = lax.dynamic_update_slice(att_own, rows_at(att, ti * rows, rows), (0, ti * lq))
-    for s in range(1, n):
-        att_own = lax.dynamic_update_slice(att_own, after(att_gots[s - 1], tok[0]), (0, tp_at(-s) * lq))
+    for t in range(wins):
+        if t == wins - 1:
+            for s in range(group):
+                grad_act(s)
+        for s in range(group):
+            col = lax.rem(win * group + lax.rem(r + group - s, group) + n - t * group, n) * lq
+            att_own = seq_out(lax.dynamic_update_slice(att_own, arrive(att_got[t][s]), (0, col)))
+    up_far = [lax.all_gather(after(a, att_own), "dp", axis=0, tiled=True) for a in up_far]
     x_own = rows_at(tokens, ti * rows, rows)
     h1, n2 = seq_out(proj_ln(att_own, wo, x_own, vec(out_bias), n2g, n2b))
 
     ns = [n2] + [group_shift(n2, s) for s in range(1, group)]
-    wq_z = spread(after(rows_at(query_weight, m * slab, slab), n2), 1)
-    wq = lax.all_gather(after(wq_z, *down_far), "dp", axis=0, tiled=True)
-    qb_all = jnp.zeros((n * lq,), BF16)
-    qb_all = lax.dynamic_update_slice(qb_all, query_bias, (ti * lq,))
-    for s in range(1, n):
-        qb_all = lax.dynamic_update_slice(qb_all, tp_shift(query_bias, s), (tp_at(-s) * lq,))
-
-    ups = [up_weight] + up_far
-    downs = [down_weight] + down_far
+    down_far = [lax.all_gather(after(b, h1), "dp", axis=0, tiled=True) for b in down_far]
+    ups, downs = [up_weight] + up_far, [down_weight] + down_far
     upbs = [vec(up_bias)] + upb_far
-    acts = [[None] * wins for _ in range(group)]
-    gbs = [[None] * wins for _ in range(group)]
+    units_of = [[None] * wins for _ in range(group)]
     gsums = [[None] * wins for _ in range(group)]
 
     def up(s, k):
-        acts[s][k], gbs[s][k], gsums[s][k] = seq_out(ffn_up(seq_in(ns[s]), ups[k], upbs[k], das[s][k]))
+        x = seq_in(ns[s])
+        res = ffn_up(x, ups[k], upbs[k], da=das[s]) if k == 0 else ffn_up(x, ups[k], upbs[k], go=go[s], down=downs[k])
+        units_of[s][k], gsums[s][k] = seq_out(res)
 
     def back_up(s):
-        out = None
-        for k in range(wins):
-            part = lax.dot_general(seq_in(gbs[s][k]) if k == 0 else gbs[s][k], ups[k], (((1,), (1,)), ((), ())), preferred_element_type=F32)
-            out = part if out is None else out + part
-        return seq_out(out.astype(BF16))
+        return seq_out(product([seq_in(units_of[s][0])] + units_of[s][1:], 1, ups, True))
 
     def down(s):
-        out = None
-        for k in range(wins):
-            part = jnp.dot(seq_in(acts[s][k]) if k == 0 else acts[s][k], downs[k], preferred_element_type=F32)
-            out = part if out is None else out + part
-        return seq_out(out.astype(BF16))
-
-    def grad_send(lefts, rights):
-        return perm(seq_out(grad_call(mv, ndp, [seq_in(lefts[0])] + lefts[1:], rights)), to_dp=lambda a: a ^ 1)
-
-    def grad_keep(lefts, rights, got):
-        sa, ka, sb, kb = seq_out(grad_call(mv, ndp, [seq_in(lefts[0])] + lefts[1:], rights, got))
-        res = []
-        for order, send, keep in zip(stage_orders((ndp // 2).bit_length() - 1), (sa, sb), (ka, kb)):
-            for b in order:
-                x = keep.astype(F32) + perm(send, to_dp=lambda a: a ^ (2 << b)).astype(F32)
-                x = x.astype(BF16)
-                half = x.shape[0] // 2
-                if half:
-                    send, keep = x[:half], x[half:]
-            res.append(x[0])
-        return jnp.concatenate(res, axis=1)
+        return seq_out(product([seq_in(units_of[s][0])] + units_of[s][1:], 0, downs, False))
+
+    class Grad:
+        def __init__(self, lefts, rights):
+            self.lefts = [l + [core_swap(arrive(a)) for a in l] for l in lefts]
+            self.rights = [[(a[None], 0) for a in x + [core_swap(arrive(a)) for a in x]] for x in rights]
+
+        def keep(self):
+            lefts = [[seq_in(self.lefts[0][0])] + self.lefts[0][1:]] + self.lefts[1:]
+            res = seq_out(grad_call(mv, ndp, lefts, self.rights))
+            self.orders = [list(o) for o in stage_orders((ndp // 2).bit_length() - 1)]
+            self.res = res
+
+        def go(self):
+            self.halves = [self.leave(h, arrive(self.res[2 * h]), self.res[2 * h + 1]) for h in range(2)]
+
+        def leave(self, h, send, keep):
+            b = self.orders[h].pop(0)
+            return keep, perm(send, to_dp=lambda a: a ^ (2 << b))
+
+        def stage(self):
+            nxt = []
+            for h in range(2):
+                keep, got = self.halves[h]
+                x = seq_out((keep.astype(F32) + arrive(got).astype(F32)).astype(BF16))
+                half = x.shape[1] // 2
+                nxt.append(self.leave(h, x[:, :half], x[:, half:]) if half else x[:, 0])
+            self.halves = nxt
+
+        def finish(self):
+            while self.orders[0]:
+                self.stage()
+            self.stage()
+            return jnp.concatenate(self.halves, axis=2)
+
+    go_swapped = [core_swap(after(g, n1)) for g in go]
 
     late = list(range(1, group)) + [0]
+    gn2_parts, sum_parts = [None] * group, [None] * group
+
     up(0, 0)
+    qb_got = [query_bias] + [tp_shift(after(query_bias, n2), s) for s in range(1, n)]
     for s in range(1, group):
         up(s, 0)
-    act_k = lambda k: [acts[s][k] for s in range(group)]
-    gb_k = lambda k: [gbs[s][k] for s in range(group)]
-    got_up, got_down, g_up, g_down = {}, {}, {}, {}
-    got_up[0] = grad_send(ns, gb_k(0))
-    got_down[0] = grad_send(go, act_k(0))
-    g_up[0] = grad_keep(ns, gb_k(0), got_up[0])
-    g_down[0] = grad_keep(go, act_k(0), got_down[0])
-    gn2_parts, sum_parts = [None] * group, [None] * group
+    qb_all = jnp.zeros((n * lq,), BF16)
+    for s in range(n):
+        qb_all = lax.dynamic_update_slice(qb_all, arrive(qb_got[s]), (tp_at(-s) * lq,))
+    qb_all = seq_out(qb_all)
+    wq_got = spread_send(after(rows_at(query_weight, m * slab, slab), *ns))
     for s in late:
         for k in range(1, wins):
-            das[s].append(grad_act(s, downs[k]))
             up(s, k)
+        if s == late[0]:
+            wq_z = spread_place(wq_got, 1)
+            wq = lax.all_gather(wq_z, "dp", axis=0, tiled=True)
         part = back_up(s)
         gn2_parts[s] = part if s == 0 else group_shift(part, -s)
     for s in late:
         part = down(s)
         sum_parts[s] = part if s == 0 else group_shift(after(part, gn2_parts[1]), -s)
-    for k in range(1, wins):
-        got_up[k] = grad_send(ns, gb_k(k))
-        got_down[k] = grad_send(go, act_k(k))
-    n1_own = rows_at(n1, ti * rows, rows)
+    ffn = []
+
+    def ffn_grad(k):
+        g = Grad([], [])
+        g.lefts = [ns + ns_swapped, go + go_swapped]
+        both = [units_of[s][k] for s in range(group)]
+        both = both + [core_swap(arrive(a)) for a in both]
+        g.rights = [[(a, 1) for a in both], [(a, 0) for a in both]]
+        ffn.append(g)
+
+    gh1, gm, gatt, sums2 = seq_out(norm2_back(gn2_parts, seq_in(h1), go[0], n2g, wo))
+    n1_own = rows_at(n1, r * rows, rows)
     q_own = seq_out((jnp.dot(seq_in(n1_own), wq, preferred_element_type=F32) + qb_all.astype(F32)).astype(BF16))
-
-    gh1, gm, gatt, sums2 = seq_out(norm2_back(gn2_parts, seq_in(h1), go[0], n2g, wo))
-    k_win = rows_at(keys, win * seq, seq)
-    v_win = rows_at(values, win * seq, seq)
-    row0 = r * rows
-    d_win = rows_at(dcol, win * seq, seq)
-    d_own = rows_at(dcol, ti * rows, rows).reshape(1, rows)
-    gq, gk, gv = seq_out(attn_bwd(row0.reshape(1), q_own, gatt, k_win, v_win, k_win.T, d_win, d_own, hd))
-    gkv_part = jnp.concatenate([gk, gv], axis=1)
-    gkv = rows_at(gkv_part, row0, rows)
-    got_kv = [
-        group_shift(rows_at(gkv_part, lax.rem(r + s, group) * rows, rows).astype(BF16), s) for s in range(1, group)
-    ]
-    for k in range(1, wins):
-        g_up[k] = grad_keep(ns, gb_k(k), got_up[k])
-    for got in got_kv:
-        gkv = gkv + after(got, tok[0]).astype(F32)
-    gkv = gkv.astype(BF16)
-    gt, sums1, small = seq_out(norm1_back(seq_in(gq), gkv, wq, keyval_weight, x_own, gh1, n1g))
-    grad_tokens = lax.all_gather(gt, "tp", axis=0, tiled=True)
-    for k in range(1, wins):
-        g_down[k] = grad_keep(go, act_k(k), got_down[k])
-
-    total = h1 + down_bias.astype(F32)
-    for sp in sum_parts:
-        total = total + sp.astype(F32)
-    output = lax.all_gather(total.astype(BF16), "tp", axis=0, tiled=True)
-
-    gqkv = jnp.concatenate([gq, gkv], axis=1)
-    got_out = grad_send([gm], [att_own])
-    got_qkv = grad_send([n1_own], [gqkv])
-    g_out = grad_keep([gm], [att_own], got_out)
-    g_qkv = grad_keep([n1_own], [gqkv], got_qkv)
-
-    g_upw, g_downw = g_up[0].astype(F32), g_down[0].astype(F32)
-    for t in range(1, wins):
-        g_upw = g_upw + tp_shift(g_up[t], -t * group).astype(F32)
-        g_downw = g_downw + tp_shift(g_down[t], -t * group).astype(F32)
-
-    def tp_scatter(x, cut):
-        out = cut(x, ti).astype(F32)
-        for s in range(1, n):
-            out = out + tp_shift(cut(x, tp_at(s)), s).astype(F32)
-        return out
-
-    take_cols = lambda x, i: lax.dynamic_slice_in_dim(x, i * lq, lq, axis=1)
-    g_outw = tp_scatter(g_out, take_cols).T
-    g_qw = tp_scatter(g_qkv[:, : n * lq], take_cols)
-    kv_rows = g_qkv.shape[0] // n
-    g_kvw = tp_scatter(g_qkv[:, n * lq :], lambda x, i: rows_at(x, i * kv_rows, kv_rows))
-
+    ns_swapped = [core_swap(arrive(x)) for x in ns]
     ub = jnp.zeros((n * units,), F32)
     for k in range(wins):
         part = sum(gsums[s][k] for s in range(group)).reshape(units)
         ub = lax.dynamic_update_slice(ub, part, (tp_at(-k * group) * units,))
+    out_g = Grad([[gm]], [[att_own]])
+    for k in range(wins):
+        ffn_grad(k)
+    row0 = r * rows
+    d_own = rows_at(dcol, row0, rows).reshape(1, rows)
+    keys_t = keys.T
+
+    gq, gk, gv = seq_out(attn_bwd(0, 1, row0.reshape(1), seq_in(q_own), gatt, keys, values, keys_t, dcol, d_own, hd))
+    gkv_part = jnp.concatenate([gk, gv], axis=1)
+    gkv = rows_at(gkv_part, row0, rows)
+    kv_got = [group_shift(rows_at(gkv_part, lax.rem(r + s, group) * rows, rows).astype(BF16), s) for s in range(1, group)]
+    total = seq_in(h1) + down_bias.astype(F32)
+    for sp in sum_parts:
+        total = total + sp.astype(F32)
+    total = seq_out(total.astype(BF16))
+    output = lax.all_gather(total, "tp", axis=0, tiled=True)
+    for got in kv_got:
+        gkv = gkv + arrive(got).astype(F32)
+    gkv = gkv.astype(BF16)
+    gt, sums1, small = seq_out(norm1_back(seq_in(gq), gkv, wq, keyval_weight, x_own, gh1, n1g))
+    qkv_g = Grad([[n1_own]], [[jnp.concatenate([gq, gkv], axis=1)]])
+    grad_tokens = lax.all_gather(gt, "tp", axis=0, tiled=True)
+
     pack = jnp.concatenate(
         [sums2[:4].reshape(-1), sums1[:3].reshape(-1), jnp.pad(small[0, hd:], (0, d - hd)), ub]
     )
-    step = 1
-    while step < ndp:
-        pack = pack + perm(pack, to_dp=lambda a: a ^ step)
-        step *= 2
-    step = 1
-    while step < n:
-        pack = pack + perm(pack, to_tp=lambda b: b ^ step)
-        step *= 2
+    swaps = [dict(to_dp=lambda a, s=1 << i: a ^ s) for i in range(ndp.bit_length() - 1)]
+    flying = None
+
+    def swap_small():
+        nonlocal pack, flying
+        if flying is not None:
+            pack = seq_out(pack + arrive(flying))
+            flying = None
+        if swaps:
+            flying = perm(pack, **swaps.pop(0))
+
+    swap_small()
+    swap_small()
+    out_g.keep()
+    swap_small()
+    for k in range(1, wins):
+        ffn[k].keep()
+    while swaps:
+        swap_small()
+    swap_small()
+    pack_got = [tp_shift(pack, s) for s in range(1, n)]
+    for k in range(1, wins):
+        ffn[k].go()
+    qkv_g.keep()
+    ffn[0].keep()
+    for k in range(1, wins):
+        ffn[k].stage()
+    out_g.go()
+    qkv_g.go()
+    far = [tp_shift(ffn[k].finish(), -k * group) for k in range(1, wins)]
+    ffn[0].go()
+    out_g.stage()
+    qkv_g.stage()
+    g_out = out_g.finish()[0]
+    g_qkv = qkv_g.finish()[0]
+
+    take_cols = lambda x, i: lax.dynamic_slice_in_dim(x, i * lq, lq, axis=1)
+    kv_rows = g_qkv.shape[0] // n
+    fr = g_qkv.shape[0]
+
+    def share(i):
+        kv_part = rows_at(g_qkv[:, n * lq :], i * kv_rows, kv_rows)
+        return [take_cols(g_out, i), take_cols(g_qkv, i), kv_part.reshape(-1, lq)]
+
+    mine = share(ti)
+    shares = [tp_shift(jnp.concatenate(share(tp_at(s)), axis=0), s) for s in range(1, n)]
+    output = seq_out(copied(arrive(output)))
+    ffn[0].stage()
+    f0 = ffn[0].finish()
+    g_upw, g_downw = f0[0].astype(F32), f0[1].astype(F32)
+    for got in far:
+        got = arrive(got).astype(F32)
+        g_upw = g_upw + got[0]
+        g_downw = g_downw + got[1]
+    g_upw = seq_out(g_upw)
+    g_downw = seq_out(g_downw.T).T
+    g_outw, g_qw, g_kvw = [x.astype(F32) for x in mine]
+    for got in shares:
+        got = arrive(got).astype(F32)
+        g_outw = g_outw + got[:fr]
+        g_qw = g_qw + got[fr : 2 * fr]
+        g_kvw = g_kvw + got[2 * fr :]
+    g_outw = seq_out(g_outw.T)
+    g_kvw = g_kvw.reshape(kv_rows, -1)
+    grad_tokens = copied(arrive(grad_tokens))
+    pack = lax.dynamic_update_slice(jnp.zeros((n, pack.shape[0]), F32), pack[None], (ti, 0))
+    for s in range(1, n):
+        pack = lax.dynamic_update_slice(pack, pack_got[s - 1][None], (tp_at(-s), 0))
+    pack = jnp.sum(pack, axis=0)
     piece = lambda row, at, size: lax.dynamic_slice_in_dim(pack, row * d + at, size)
     vs = d // ndp
     qs = lq // ndp

time: 1080 us -> 878 us (0.81)
  waiting for transfers between devices: 407 us -> 301 us
  matrix products: 124 us -> 43.3 us
  starting transfers between devices: 103 us -> 55.8 us
  Pallas kernels: 300 us -> 313 us
  local copies, waits for them, and re-layouts: 75.4 us -> 86.6 us
    ppermute x65 -> x58, waiting for transfers between devices: 399 us -> 300 us  [perm(): return lax.ppermute(x, ('dp', 'tp'), pairs)]
    dot_general x13 -> x4, matrix products: 109 us -> 29 us  [the longest x2 17.1 us: grad_act(): lax.dot_general(seq_in(go[s]), down_weight, (((1,), (1,)), ((), ())), pre...]
    ppermute x65 -> x58, starting transfers between devices: 102 us -> 55.3 us  [perm(): return lax.ppermute(x, ('dp', 'tp'), pairs)]
    pallas_call x17 -> x15, Pallas kernels: 196 us -> 217 us  [the longest x4 79.4 us: grad_call(): call(functools.partial(grad_kernel, count, pairs, places), (pairs, places...]
    unnamed x177 -> x116, local copies, waits for them, and re-layouts: 32.4 us -> 19.2 us
    convert_element_type x15 -> x25, other arithmetic: 15 us -> 27.8 us  [the longest x16 19.1 us: stage(): x = seq_out((keep.astype(F32) + arrive(got).astype(F32)).astype(BF16))]
    dynamic_update_slice x15 -> x20, local copies, waits for them, and re-layouts: 7.62 us -> 19.8 us  [the longest x3 7.98 us: per_device(): pack = lax.dynamic_update_slice(pack, pack_got[s - 1][None], (tp_at(-s), 0))]
  transfers between devices with their start and end apart: 71 -> 65, of which waited for: 28 -> 21; matrix products, arithmetic and copies ran while one was open for 20% -> 19% of each run, Pallas kernels for 28% -> 35%
where the time goes in v2:
time: 878 us; the launch traced here: 862 us
  Pallas kernels  313 us (36%)
  waiting for transfers between devices  301 us (34%)
  local copies, waits for them, and re-layouts  86.6 us (10%)
  starting transfers between devices  55.8 us (6%)
  other arithmetic  46.9 us (5%)
  matrix products  43.3 us (5%)
  between operations  15.5 us (2%)
    ppermute x58, waiting for transfers between devices, perm(): return lax.ppermute(x, ('dp', 'tp'), pairs)  300 us
    pallas_call x4, Pallas kernels, grad_call(): call(functools.partial(grad_kernel, count, pairs, places), (pairs, places...  79.4 us
    pallas_call x4, Pallas kernels, ffn_up(): call(functools.partial(up_kernel, ready), (u // bn,), [whole((r, d)), pl....  57.1 us
    pallas_call x4, Pallas kernels, product(): call(functools.partial(product_kernel, len(xs), nt), (n // bn,), [plane(x...  56.3 us
    ppermute x58, starting transfers between devices, perm(): return lax.ppermute(x, ('dp', 'tp'), pairs)  55.3 us
    pallas_call x1, Pallas kernels, attn_bwd(): call(functools.partial(attn_bwd_kernel, hd ** (-0.5), qb, reach), (heads,...  34.5 us
    pallas_call x2, Pallas kernels, attn_fwd(): call(functools.partial(attn_fwd_kernel, hd ** (-0.5), qb), (wins, heads),...  20.8 us
    unnamed x116, local copies, waits for them, and re-layouts  19.2 us
  transfers between devices with their start and end apart: 65, of which 21 were waited for; matrix products, arithmetic and copies ran while one was open for 19% of the time, Pallas kernels for 35%

profile of v2, /device:TPU:0, one launch (start us, length us, event | category | flops | bytes accessed | tf_op | source)
XLA Modules:
  0.0 861.7 jit_solution(5118629022431160846)
XLA Ops:
  8.8 4.1 collective-permute-start.3
  15.5 6.3 norm1.1
  21.8 4.4 fusion.29
  39.7 5.6 add_convert_fusion.15.q_ref
  46.2 10.4 %attn_fwd.2 = bf16[1024,512]{1,0:T(8,128)(2,1)} custom-call(bf16[1024,512]{1,0:T(8,128)(2,1)} %add_convert_fusion.15.q_ref, bf16[1024,128]{1,0:T(8,128)(2,1)} %copy.65.k_ref, bf16[128,1024]{1,0:T(8,128)(2,1)} %copy.66.vt_ref, s32[1024,1]{1,0:T(8,128)} %copy.67.dcol_ref, s32[1,1,1024]{2,1,0:T(1,128)} %get-tuple-element.345.drow_ref), custom_call_target="tpu_custom_call" | custom-call | flops 1342177280 | bytes 2621440 | tf_op jit(solution)/shard_map/attn_fwd/pallas_call | solution.py:116
  64.6 2.3 constant_dynamic-slice_fusion.4
  66.9 4.7 constant_dynamic-slice_fusion.8
  72.1 6.3 add_convert_fusion.14.q_ref
  78.4 10.4 %attn_fwd.3 = bf16[1024,512]{1,0:T(8,128)(2,1)} custom-call(bf16[1024,512]{1,0:T(8,128)(2,1)} %add_convert_fusion.14.q_ref, bf16[1024,128]{1,0:T(8,128)(2,1)} %copy.65.k_ref, bf16[128,1024]{1,0:T(8,128)(2,1)} %copy.66.vt_ref, s32[1024,1]{1,0:T(8,128)} %copy.67.dcol_ref, s32[1,1,1024]{2,1,0:T(1,128)} %get-tuple-element.345.drow_ref), custom_call_target="tpu_custom_call" | custom-call | flops 1342177280 | bytes 2621440 | tf_op jit(solution)/shard_map/attn_fwd/pallas_call | solution.py:116
  92.1 9.3 %convolution_convert_fusion.1.refs_0_ = bf16[512,2048]{1,0:T(8,128)(2,1)} fusion(bf16[512,2048]{1,0:T(8,128)(2,1)S(1)} %get-tuple-element.210.refs_0_.refs_3_.refs_4_, bf16[2048,2048]{1,0:T(8,128)(2,1)} %refs_2_.7), kind=kOutput, calls=%fused_computation.7 | convolution fusion | flops 4296015872 | bytes 12582912 | tf_op jit(solution)/shard_map/dot_general | solution.py:605
  102.7 7.8 convolution_convert_fusion.refs_0_
  111.3 17.7 %collective-permute-done.6 = bf16[512,512]{1,0:T(8,128)(2,1)S(1)} collective-permute-done((bf16[512,512]{1,0:T(8,128)(2,1)S(1)}, bf16[512,512]{1,0:T(8,128)(2,1)S(1)}, u32[]{:S(2)}, u32[]{:S(2)}) %collective-permute-start.6) | collective-permute-done | bytes 524320 | tf_op jit(solution)/shard_map/ppermute | solution.py:528
  133.4 3.2 constant_dynamic-slice_fusion.6.x_ref
  136.6 11.8 %proj_ln.1 = (f32[512,2048]{1,0:T(8,128)}, bf16[512,2048]{1,0:T(8,128)(2,1)}) custom-call(bf16[512,2048]{1,0:T(8,128)(2,1)} %constant_dynamic-update-slice_fusion.4.att_ref, bf16[8,2048,256]{2,1,0:T(8,128)(2,1)} %bitcast.85, bf16[512,2048]{1,0:T(8,128)(2,1)} %constant_dynamic-slice_fusion.6.x_ref, bf16[1,2048]{1,0:T(2,128)(2,1)} %reshape.122.ob_ref, ...), custom_call_target="tpu_custom_call" | custom-call | flops 4294967296 | bytes 18874368 | tf_op jit(solution)/shard_map/proj_ln/pallas_call | solution.py:151
  148.4 31.0 %collective-permute-done.14 = bf16[256,2048]{1,0:T(8,128)(2,1)S(1)} collective-permute-done((bf16[256,2048]{1,0:T(8,128)(2,1)S(1)}, bf16[256,2048]{1,0:T(8,128)(2,1)S(1)}, u32[]{:S(2)}, u32[]{:S(2)}) %collective-permute-start.14) | collective-permute-done | bytes 1048608 | tf_op jit(solution)/shard_map/ppermute | solution.py:528
  180.5 2.2 collective-permute-start.13
  185.7 11.9 %ffn_up.4 = (bf16[2,512,2048]{2,1,0:T(8,128)(2,1)}, f32[1,2048]{1,0:T(1,128)}) custom-call(bf16[512,2048]{1,0:T(8,128)(2,1)} %get-tuple-element.227.n_ref.refs_0_, bf16[2048,2048]{1,0:T(8,128)(2,1)} %refs_2_.5, bf16[1,2048]{1,0:T(2,128)(2,1)} %copy-done.41, bf16[512,2048]{1,0:T(8,128)(2,1)} %convolution_convert_fusion.1.refs_0_), custom_call_target="tpu_custom_call" | custom-call | flops 4294967296 | bytes 16777216 | tf_op jit(solution)/shard_map/ffn_up/pallas_call | solution.py:195
  197.6 30.9 %collective-permute-done.7.n_ref.refs_1_ = bf16[512,2048]{1,0:T(8,128)(2,1)S(1)} collective-permute-done((bf16[512,2048]{1,0:T(8,128)(2,1)}, bf16[512,2048]{1,0:T(8,128)(2,1)S(1)}, u32[]{:S(2)}, u32[]{:S(2)}) %collective-permute-start.7) | collective-permute-done | bytes 2097184 | tf_op jit(solution)/shard_map/ppermute | solution.py:528
  230.1 11.5 %ffn_up.5 = (bf16[2,512,2048]{2,1,0:T(8,128)(2,1)}, f32[1,2048]{1,0:T(1,128)}) custom-call(bf16[512,2048]{1,0:T(8,128)(2,1)} %copy-done.49, bf16[2048,2048]{1,0:T(8,128)(2,1)} %refs_2_.5, bf16[1,2048]{1,0:T(2,128)(2,1)} %copy-done.41, bf16[512,2048]{1,0:T(8,128)(2,1)} %convolution_convert_fusion.refs_0_), custom_call_target="tpu_custom_call" | custom-call | flops 4294967296 | bytes 16777216 | tf_op jit(solution)/shard_map/ffn_up/pallas_call | solution.py:195
  245.3 16.6 %ffn_up.6 = (bf16[2,512,2048]{2,1,0:T(8,128)(2,1)}, f32[1,2048]{1,0:T(1,128)}) custom-call(bf16[512,2048]{1,0:T(8,128)(2,1)} %copy-done.49, bf16[2048,2048]{1,0:T(8,128)(2,1)} %all-gather.11.cloned.1.call-done.w_ref.refs_3_, bf16[1,2048]{1,0:T(2,128)(2,1)} %copy-done.51, bf16[512,2048]{1,0:T(8,128)(2,1)} %get-tuple-element.211.refs_0_.refs_5_, ...), custom_call_target="tpu_custom_call" | custom-call | flops 8589934592 | bytes 16777216 | tf_op jit(solution)/shard_map/ffn_up/pallas_call | solution.py:195
  264.5 3.2 constant_dynamic-slice_fusion.5.refs_0_
  267.7 14.5 %product.4 = bf16[512,2048]{1,0:T(8,128)(2,1)} custom-call(bf16[2,512,2048]{2,1,0:T(8,128)(2,1)} %get-tuple-element.229.refs_0_.refs_9_.refs_13_, bf16[2,512,2048]{2,1,0:T(8,128)(2,1)} %get-tuple-element.213.refs_1_.refs_9_.refs_13_, bf16[2048,2048]{1,0:T(8,128)(2,1)} %refs_2_.5, bf16[2048,2048]{1,0:T(8,128)(2,1)} %all-gather.11.cloned.1.call-done.w_ref.refs_3_), custom_call_target="tpu_custom_call" | custom-call | flops 8589934592 | bytes 23068672 | tf_op jit(solution)/shard_map/product/pallas_call | solution.py:225
  283.6 17.1 %ffn_up.7 = (bf16[2,512,2048]{2,1,0:T(8,128)(2,1)}, f32[1,2048]{1,0:T(1,128)}) custom-call(bf16[512,2048]{1,0:T(8,128)(2,1)} %get-tuple-element.227.n_ref.refs_0_, bf16[2048,2048]{1,0:T(8,128)(2,1)} %all-gather.11.cloned.1.call-done.w_ref.refs_3_, bf16[1,2048]{1,0:T(2,128)(2,1)} %copy-done.51, bf16[512,2048]{1,0:T(8,128)(2,1)} %copy-done.3, ...), custom_call_target="tpu_custom_call" | custom-call | flops 8589934592 | bytes 16777216 | tf_op jit(solution)/shard_map/ffn_up/pallas_call | solution.py:195
  300.7 14.0 %product.5.refs_0_ = bf16[512,2048]{1,0:T(8,128)(2,1)} custom-call(bf16[2,512,2048]{2,1,0:T(8,128)(2,1)} %get-tuple-element.228.refs_0_.refs_8_.refs_12_, bf16[2,512,2048]{2,1,0:T(8,128)(2,1)} %get-tuple-element.212.refs_1_.refs_8_.refs_12_, bf16[2048,2048]{1,0:T(8,128)(2,1)} %refs_2_.5, bf16[2048,2048]{1,0:T(8,128)(2,1)} %all-gather.11.cloned.1.call-done.w_ref.refs_3_), custom_call_target="tpu_custom_call" | custom-call | flops 8589934592 | bytes 23068672 | tf_op jit(solution)/shard_map/product/pallas_call | solution.py:225
  314.7 13.9 %product.6 = bf16[512,2048]{1,0:T(8,128)(2,1)} custom-call(bf16[2,512,2048]{2,1,0:T(8,128)(2,1)} %get-tuple-element.229.refs_0_.refs_9_.refs_13_, bf16[2,512,2048]{2,1,0:T(8,128)(2,1)} %get-tuple-element.213.refs_1_.refs_9_.refs_13_, bf16[2048,2048]{1,0:T(8,128)(2,1)} %refs_2_.7, bf16[2048,2048]{1,0:T(8,128)(2,1)} %all-gather.13.cloned.1.call-done.refs_1_.refs_3_), custom_call_target="tpu_custom_call" | custom-call | flops 8589934592 | bytes 23068672 | tf_op jit(solution)/shard_map/product/pallas_call | solution.py:225
  328.7 13.8 %product.7 = bf16[512,2048]{1,0:T(8,128)(2,1)} custom-call(bf16[2,512,2048]{2,1,0:T(8,128)(2,1)} %get-tuple-element.228.refs_0_.refs_8_.refs_12_, bf16[2,512,2048]{2,1,0:T(8,128)(2,1)} %get-tuple-element.212.refs_1_.refs_8_.refs_12_, bf16[2048,2048]{1,0:T(8,128)(2,1)} %refs_2_.7, bf16[2048,2048]{1,0:T(8,128)(2,1)} %all-gather.13.cloned.1.call-done.refs_1_.refs_3_), custom_call_target="tpu_custom_call" | custom-call | flops 8589934592 | bytes 23068672 | tf_op jit(solution)/shard_map/product/pallas_call | solution.py:225
  343.8 14.6 %norm2_back.1 = (f32[512,2048]{1,0:T(8,128)}, bf16[512,2048]{1,0:T(8,128)(2,1)}, bf16[512,2048]{1,0:T(8,128)(2,1)}, f32[8,2048]{1,0:T(8,128)}) custom-call(bf16[512,2048]{1,0:T(8,128)(2,1)} %product.5.refs_0_, bf16[512,2048]{1,0:T(8,128)(2,1)} %copy-done.21, f32[512,2048]{1,0:T(8,128)} %get-tuple-element.186.refs_2_, bf16[512,2048]{1,0:T(8,128)(2,1)} %copy-done.3, ...), custom_call_target="tpu_custom_call" | custom-call | flops 4294967296 | bytes 29360128 | tf_op jit(solution)/shard_map/norm2_back/pallas_call | solution.py:275
  358.4 9.9 %add_convert_fusion.5.q_ref = bf16[512,2048]{1,0:T(8,128)(2,1)} fusion(bf16[512,2048]{1,0:T(8,128)(2,1)} %constant_dynamic-slice_fusion.5.refs_0_, bf16[2048,2048]{1,0:T(8,128)(2,1)} %all-gather.15.cloned.1.call-done.wq_ref, f32[2048]{0:T(1024)S(1)} %convert_element_type.244), kind=kOutput, calls=%fused_computation.5 | convolution fusion | flops 4297064448 | bytes 12591104 | tf_op jit(solution)/shard_map/dot_general | solution.py:721
  368.3 34.5 %attn_bwd.1 = (bf16[512,2048]{1,0:T(8,128)(2,1)}, f32[1024,128]{1,0:T(8,128)}, f32[1024,128]{1,0:T(8,128)}) custom-call(s32[1]{0:T(128)} %bitcast.5.row0_ref, bf16[512,2048]{1,0:T(8,128)(2,1)} %add_convert_fusion.5.q_ref, bf16[512,2048]{1,0:T(8,128)(2,1)} %get-tuple-element.184.go_ref, bf16[1024,128]{1,0:T(8,128)(2,1)} %copy.65.k_ref, ...), custom_call_target="tpu_custom_call" | custom-call | flops 8053063680 | bytes 8388608 | tf_op jit(solution)/shard_map/attn_bwd/pallas_call | solution.py:334
  402.8 4.1 add_convert_fusion.4
  411.7 4.2 collective-permute-done.19
  417.7 14.2 %norm1_back.1 = (bf16[512,2048]{1,0:T(8,128)(2,1)}, f32[8,2048]{1,0:T(8,128)}, f32[8,256]{1,0:T(8,128)}) custom-call(bf16[512,2048]{1,0:T(8,128)(2,1)} %get-tuple-element.189.gq_ref, bf16[512,256]{1,0:T(8,128)(2,1)} %add_convert_fusion.20.gkv_ref, bf16[2048,2048]{1,0:T(8,128)(2,1)} %all-gather.15.cloned.1.call-done.wq_ref, bf16[2048,256]{1,0:T(8,128)(2,1)} %wkv_ref.1, ...), custom_call_target="tpu_custom_call" | custom-call | flops 4831838208 | bytes 22020096 | tf_op jit(solution)/shard_map/norm1_back/pallas_call | solution.py:376
  437.1 2.6 collective-permute-done.21
  439.7 7.4 collective-permute-done.26.refs_3_
  447.6 8.5 collective-permute-done.23
  456.5 4.2 pad_maximum_fusion
  461.2 9.6 %weight_grad.4 = (bf16[1,2,256,1024]{3,2,1,0:T(8,128)(2,1)}, bf16[1,2,256,1024]{3,2,1,0:T(8,128)(2,1)}, bf16[1,2,256,1024]{3,2,1,0:T(8,128)(2,1)}, bf16[1,2,256,1024]{3,2,1,0:T(8,128)(2,1)}) custom-call(s32[1]{0:T(128)} %bitcast.7.m_ref, bf16[512,2048]{1,0:T(8,128)(2,1)} %get-tuple-element.203.refs_0_, bf16[512,2048]{1,0:T(8,128)(2,1)} %collective-permute-done.22.refs_1_, ...), custom_call_target="tpu_custom_call" | custom-call | flops 4294967296 | bytes 10485760 | tf_op jit(solution)/shard_map/weight_grad/pallas_call | solution.py:467
  472.5 29.6 %weight_grad.5 = (bf16[2,2,256,1024]{3,2,1,0:T(8,128)(2,1)}, bf16[2,2,256,1024]{3,2,1,0:T(8,128)(2,1)}, bf16[2,2,256,1024]{3,2,1,0:T(8,128)(2,1)}, bf16[2,2,256,1024]{3,2,1,0:T(8,128)(2,1)}) custom-call(s32[1]{0:T(128)} %bitcast.7.m_ref, bf16[512,2048]{1,0:T(8,128)(2,1)} %get-tuple-element.227.n_ref.refs_0_, bf16[512,2048]{1,0:T(8,128)(2,1)} %copy-done.49, ...), custom_call_target="tpu_custom_call" | custom-call | flops 17179869184 | bytes 33554432 | tf_op jit(solution)/shard_map/weight_grad/pallas_call | solution.py:467
  502.8 3.2 copy.76
  509.6 10.7 %weight_grad.6 = (bf16[1,2,256,1152]{3,2,1,0:T(8,128)(2,1)}, bf16[1,2,256,1152]{3,2,1,0:T(8,128)(2,1)}, bf16[1,2,256,1152]{3,2,1,0:T(8,128)(2,1)}, bf16[1,2,256,1152]{3,2,1,0:T(8,128)(2,1)}) custom-call(s32[1]{0:T(128)} %bitcast.7.m_ref, bf16[512,2048]{1,0:T(8,128)(2,1)} %constant_dynamic-slice_fusion.5.refs_0_, ...), custom_call_target="tpu_custom_call" | custom-call | flops 4831838208 | bytes 11534336 | tf_op jit(solution)/shard_map/weight_grad/pallas_call | solution.py:467
  520.3 29.6 %weight_grad.7 = (bf16[2,2,256,1024]{3,2,1,0:T(8,128)(2,1)}, bf16[2,2,256,1024]{3,2,1,0:T(8,128)(2,1)}, bf16[2,2,256,1024]{3,2,1,0:T(8,128)(2,1)}, bf16[2,2,256,1024]{3,2,1,0:T(8,128)(2,1)}) custom-call(s32[1]{0:T(128)} %bitcast.7.m_ref, bf16[512,2048]{1,0:T(8,128)(2,1)} %get-tuple-element.227.n_ref.refs_0_, bf16[512,2048]{1,0:T(8,128)(2,1)} %copy-done.49, ...), custom_call_target="tpu_custom_call" | custom-call | flops 17179869184 | bytes 33554432 | tf_op jit(solution)/shard_map/weight_grad/pallas_call | solution.py:467
  549.8 3.8 collective-permute-done.34
  554.9 2.6 add_convert_fusion.3
  567.3 7.0 collective-permute-done.55
  574.3 8.0 collective-permute-done.56
  583.1 2.9 dynamic_update_slice.84
  586.1 2.7 dynamic_update_slice.85
  588.7 2.7 dynamic_update_slice.86
  591.4 2.7 dynamic_update_slice.87
  603.9 7.8 collective-permute-done.40
  621.6 15.3 %collective-permute-done.38 = bf16[1,2,256,1152]{3,2,1,0:T(8,128)(2,1)S(1)} collective-permute-done((bf16[1,2,256,1152]{3,2,1,0:T(8,128)(2,1)}, bf16[1,2,256,1152]{3,2,1,0:T(8,128)(2,1)S(1)}, u32[]{:S(2)}, u32[]{:S(2)}) %collective-permute-start.38) | collective-permute-done | bytes 1179680 | tf_op jit(solution)/shard_map/ppermute | solution.py:528
  639.7 5.4 collective-permute-done.46
  649.8 51.7 %collective-permute-done.44 = bf16[1,1,256,1152]{3,2,1,0:T(8,128)(2,1)S(1)} collective-permute-done((bf16[1,1,256,1152]{3,2,1,0:T(8,128)(2,1)S(1)}, bf16[1,1,256,1152]{3,2,1,0:T(8,128)(2,1)S(1)}, u32[]{:S(2)}, u32[]{:S(2)}) %collective-permute-start.44) | collective-permute-done | bytes 589856 | tf_op jit(solution)/shard_map/ppermute | solution.py:528
  704.0 9.1 %copied.2 = bf16[2048,2048]{1,0:T(8,128)(2,1)} custom-call(bf16[2048,2048]{1,0:T(8,128)(2,1)} %all-gather.17.cloned.1.call-done.x_ref), custom_call_target="tpu_custom_call" | custom-call | bytes 16777216 | tf_op jit(solution)/shard_map/copied/pallas_call | solution.py:488
  713.1 2.6 add_convert_fusion.1
  718.5 2.5 add_convert_fusion
  729.7 10.8 %collective-permute-done.49 = bf16[2,1,256,1024]{3,2,0,1:T(8,128)(2,1)} collective-permute-done((bf16[2,1,256,1024]{3,2,0,1:T(8,128)(2,1)}, bf16[2,1,256,1024]{3,2,0,1:T(8,128)(2,1)}, u32[]{:S(2)}, u32[]{:S(2)}) %collective-permute-start.49) | collective-permute-done | bytes 1048608 | tf_op jit(solution)/shard_map/ppermute | solution.py:528
  743.6 2.2 collective-permute-done.51
  747.5 77.9 %collective-permute-done.52 = bf16[2,256,2048]{2,1,0:T(8,128)(2,1)} collective-permute-done((bf16[2,256,2048]{2,1,0:T(8,128)(2,1)}, bf16[2,256,2048]{2,1,0:T(8,128)(2,1)}, u32[]{:S(2)}, u32[]{:S(2)}) %collective-permute-start.52) | collective-permute-done | bytes 2097184 | tf_op jit(solution)/shard_map/ppermute | solution.py:528
  827.5 2.6 fusion
  830.1 2.9 copy.80
  834.2 3.1 collective-permute-done.53
  841.2 3.1 slice_add_fusion.2
  845.3 9.1 %copied.3 = bf16[2048,2048]{1,0:T(8,128)(2,1)} custom-call(bf16[2048,2048]{1,0:T(8,128)(2,1)} %all-gather.19.cloned.1.call-done.x_ref), custom_call_target="tpu_custom_call" | custom-call | bytes 16777216 | tf_op jit(solution)/shard_map/copied/pallas_call | solution.py:488
  (337 shorter events, 136.0 us)
Async XLA Ops:
  7.2 64.9 %all-gather.9.cloned.1.call-start = ((), (), s32[]{:S(2)}) async-start(), calls=%async_computation | async-start | bytes 2359296 | tf_op jit(solution)/shard_map/all_gather | solution.py:600
  8.8 17.4 %collective-permute-start.3 = (bf16[256,512]{1,0:T(8,128)(2,1)S(1)}, bf16[256,512]{1,0:T(8,128)(2,1)S(1)}, u32[]{:S(2)}, u32[]{:S(2)}) collective-permute-start(bf16[256,512]{1,0:T(8,128)(2,1)S(1)} %constant_dynamic-slice_fusion.12), channel_id=1, source_target_pairs={{0,2},{1,3},{2,0},{3,1},{4,6},{5,7},{6,4},{7,5},{8,10},{9,11},{10,... | collective-permute-start | bytes 786440 | tf_op jit(solution)/shard_map/ppermute | solution.py:528
  26.9 109.7 %all-gather.21.cloned.1.call-start = ((), (), s32[]{:S(2)}) async-start(), calls=%async_computation.6 | async-start | bytes 9437184 | tf_op jit(solution)/shard_map/all_gather | solution.py:615
  28.8 27.8 %collective-permute-start = (bf16[512,256]{1,0:T(8,128)(2,1)}, bf16[512,256]{1,0:T(8,128)(2,1)}, u32[]{:S(2)}, u32[]{:S(2)}) collective-permute-start(bf16[512,256]{1,0:T(8,128)(2,1)} %get-tuple-element.315), channel_id=1, source_target_pairs={{0,1},{1,2},{2,3},{3,0},{4,5},{5,6},{6,7},{7,4},{8,9},{9,10},{10,1... | collective-permute-start | bytes 786440 | tf_op jit(solution)/shard_map/ppermute | solution.py:528
  30.3 26.2 %collective-permute-start.1 = (bf16[512,256]{1,0:T(8,128)(2,1)}, bf16[512,256]{1,0:T(8,128)(2,1)}, u32[]{:S(2)}, u32[]{:S(2)}) collective-permute-start(bf16[512,256]{1,0:T(8,128)(2,1)} %get-tuple-element.315), channel_id=1, source_target_pairs={{0,2},{1,3},{2,0},{3,1},{4,6},{5,7},{6,4},{7,5},{8,10},{9,11},{10,... | collective-permute-start | bytes 786440 | tf_op jit(solution)/shard_map/ppermute | solution.py:528
  31.5 25.1 %collective-permute-start.2 = (bf16[512,256]{1,0:T(8,128)(2,1)}, bf16[512,256]{1,0:T(8,128)(2,1)}, u32[]{:S(2)}, u32[]{:S(2)}) collective-permute-start(bf16[512,256]{1,0:T(8,128)(2,1)} %get-tuple-element.315), channel_id=1, source_target_pairs={{0,3},{1,0},{2,1},{3,2},{4,7},{5,4},{6,5},{7,6},{8,11},{9,8},{10,9... | collective-permute-start | bytes 786440 | tf_op jit(solution)/shard_map/ppermute | solution.py:528
  60.6 184.1 %all-gather.11.cloned.1.call-start = ((), (), s32[]{:S(2)}) async-start(), calls=%async_computation.1 | async-start | bytes 9437184 | tf_op jit(solution)/shard_map/all_gather | solution.py:629
  60.8 10.7 %collective-permute-start.4 = (bf16[512]{0:T(512)(128)(2,1)S(1)}, bf16[512]{0:T(512)(128)(2,1)S(1)}, u32[]{:S(2)}, u32[]{:S(2)}) collective-permute-start(bf16[512]{0:T(512)(128)(2,1)S(1)} %copy-done.48), channel_id=1, source_target_pairs={{0,2},{1,3},{2,0},{3,1},{4,6},{5,7},{6,4},{7,5},{8,10},{9,11},{10,... | collective-permute-start | bytes 3080 | tf_op jit(solution)/shard_map/ppermute | solution.py:528
  63.6 27.6 %collective-permute-start.5 = (bf16[512,512]{1,0:T(8,128)(2,1)}, bf16[512,512]{1,0:T(8,128)(2,1)S(1)}, u32[]{:S(2)}, u32[]{:S(2)}) collective-permute-start(bf16[512,512]{1,0:T(8,128)(2,1)} %get-tuple-element.332), channel_id=1, source_target_pairs={{0,1},{1,0},{2,3},{3,2},{4,5},{5,4},{6,7},{7,6},{8,9},{9,8},{10,11... | collective-permute-start | bytes 1572872 | tf_op jit(solution)/shard_map/ppermute | solution.py:528
  71.6 58.2 %collective-permute-start.12 = (bf16[256,2048]{1,0:T(8,128)(2,1)}, bf16[256,2048]{1,0:T(8,128)(2,1)}, u32[]{:S(2)}, u32[]{:S(2)}) collective-permute-start(bf16[256,2048]{1,0:T(8,128)(2,1)} %constant_dynamic-slice_fusion.4), channel_id=1, source_target_pairs={{0,2},{1,3},{2,0},{3,1},{4,6},{5,7},{6,4},{7,5},{8,10},{9,11},{10,... | collective-permute-start | bytes 3145736 | tf_op jit(solution)/shard_map/ppermute | solution.py:528
  101.4 27.6 %collective-permute-start.6 = (bf16[512,512]{1,0:T(8,128)(2,1)S(1)}, bf16[512,512]{1,0:T(8,128)(2,1)S(1)}, u32[]{:S(2)}, u32[]{:S(2)}) collective-permute-start(bf16[512,512]{1,0:T(8,128)(2,1)S(1)} %get-tuple-element.330), channel_id=1, source_target_pairs={{0,1},{1,0},{2,3},{3,2},{4,5},{5,4},{6,7},{7,6},{8,9},{9,8},{10,11... | collective-permute-start | bytes 1572872 | tf_op jit(solution)/shard_map/ppermute | solution.py:528
  129.8 114.9 %all-gather.13.cloned.1.call-start = ((), (), s32[]{:S(2)}) async-start(), calls=%async_computation.2 | async-start | bytes 9437184 | tf_op jit(solution)/shard_map/all_gather | solution.py:634
  131.2 48.1 %collective-permute-start.14 = (bf16[256,2048]{1,0:T(8,128)(2,1)S(1)}, bf16[256,2048]{1,0:T(8,128)(2,1)S(1)}, u32[]{:S(2)}, u32[]{:S(2)}) collective-permute-start(bf16[256,2048]{1,0:T(8,128)(2,1)S(1)} %constant_dynamic-slice_fusion.3), channel_id=1, source_target_pairs={{0,2},{1,3},{2,0},{3,1},{4,6},{5,7},{6,4},{7,5},{8,10},{9,11},{10,... | collective-permute-start | bytes 3145736 | tf_op jit(solution)/shard_map/ppermute | solution.py:528
  180.4 178.0 %all-gather.15.cloned.1.call-start = ((), (), s32[]{:S(2)}) async-start(), calls=%async_computation.3 | async-start | bytes 9437184 | tf_op jit(solution)/shard_map/all_gather | solution.py:703
  180.4 48.1 %collective-permute-start.7 = (bf16[512,2048]{1,0:T(8,128)(2,1)}, bf16[512,2048]{1,0:T(8,128)(2,1)S(1)}, u32[]{:S(2)}, u32[]{:S(2)}) collective-permute-start(bf16[512,2048]{1,0:T(8,128)(2,1)} %get-tuple-element.227.n_ref.refs_0_), channel_id=1, source_target_pairs={{0,1},{1,0},{2,3},{3,2},{4,5},{5,4},{6,7},{7,6},{8,9},{9,8},{10,11... | collective-permute-start | bytes 6291464 | tf_op jit(solution)/shard_map/ppermute | solution.py:528
  180.5 64.2 %collective-permute-start.13 = (bf16[1,2048]{1,0:T(2,128)(2,1)S(1)}, bf16[1,2048]{1,0:T(2,128)(2,1)S(1)}, u32[]{:S(2)}, u32[]{:S(2)}) collective-permute-start(bf16[1,2048]{1,0:T(2,128)(2,1)S(1)} %reshape.126.b_ref), channel_id=1, source_target_pairs={{0,2},{1,3},{2,0},{3,1},{4,6},{5,7},{6,4},{7,5},{8,10},{9,11},{10,... | collective-permute-start | bytes 12296 | tf_op jit(solution)/shard_map/ppermute | solution.py:528
  182.8 59.0 %collective-permute-start.11 = (bf16[512]{0:T(512)(128)(2,1)S(1)}, bf16[512]{0:T(512)(128)(2,1)S(1)}, u32[]{:S(2)}, u32[]{:S(2)}) collective-permute-start(bf16[512]{0:T(512)(128)(2,1)S(1)} %copy-done.48), channel_id=1, source_target_pairs={{0,3},{1,0},{2,1},{3,2},{4,7},{5,4},{6,5},{7,6},{8,11},{9,8},{10,9... | collective-permute-start | bytes 3080 | tf_op jit(solution)/shard_map/ppermute | solution.py:528
  185.0 57.1 %collective-permute-start.10 = (bf16[512]{0:T(512)(128)(2,1)S(1)}, bf16[512]{0:T(512)(128)(2,1)S(1)}, u32[]{:S(2)}, u32[]{:S(2)}) collective-permute-start(bf16[512]{0:T(512)(128)(2,1)S(1)} %copy-done.48), channel_id=1, source_target_pairs={{0,2},{1,3},{2,0},{3,1},{4,6},{5,7},{6,4},{7,5},{8,10},{9,11},{10,... | collective-permute-start | bytes 3080 | tf_op jit(solution)/shard_map/ppermute | solution.py:528
  185.0 58.9 %collective-permute-start.9 = (bf16[512]{0:T(512)(128)(2,1)S(1)}, bf16[512]{0:T(512)(128)(2,1)S(1)}, u32[]{:S(2)}, u32[]{:S(2)}) collective-permute-start(bf16[512]{0:T(512)(128)(2,1)S(1)} %copy-done.48), channel_id=1, source_target_pairs={{0,1},{1,2},{2,3},{3,0},{4,5},{5,6},{6,7},{7,4},{8,9},{9,10},{10,1... | collective-permute-start | bytes 3080 | tf_op jit(solution)/shard_map/ppermute | solution.py:528
  228.5 33.4 %collective-permute-start.16 = (bf16[256,512]{1,0:T(8,128)(2,1)S(1)}, bf16[256,512]{1,0:T(8,128)(2,1)S(1)}, u32[]{:S(2)}, u32[]{:S(2)}) collective-permute-start(bf16[256,512]{1,0:T(8,128)(2,1)S(1)} %constant_dynamic-slice_fusion.12), channel_id=1, source_target_pairs={{0,3},{1,0},{2,1},{3,2},{4,7},{5,4},{6,5},{7,6},{8,11},{9,8},{10,9... | collective-permute-start | bytes 786440 | tf_op jit(solution)/shard_map/ppermute | solution.py:528
  241.8 20.1 %collective-permute-start.15 = (bf16[256,512]{1,0:T(8,128)(2,1)S(1)}, bf16[256,512]{1,0:T(8,128)(2,1)S(1)}, u32[]{:S(2)}, u32[]{:S(2)}) collective-permute-start(bf16[256,512]{1,0:T(8,128)(2,1)S(1)} %constant_dynamic-slice_fusion.12), channel_id=1, source_target_pairs={{0,2},{1,3},{2,0},{3,1},{4,6},{5,7},{6,4},{7,5},{8,10},{9,11},{10,... | collective-permute-start | bytes 786440 | tf_op jit(solution)/shard_map/ppermute | solution.py:528
  242.0 19.9 %collective-permute-start.8 = (bf16[256,512]{1,0:T(8,128)(2,1)S(1)}, bf16[256,512]{1,0:T(8,128)(2,1)S(1)}, u32[]{:S(2)}, u32[]{:S(2)}) collective-permute-start(bf16[256,512]{1,0:T(8,128)(2,1)S(1)} %constant_dynamic-slice_fusion.12), channel_id=1, source_target_pairs={{0,1},{1,2},{2,3},{3,0},{4,5},{5,6},{6,7},{7,4},{8,9},{9,10},{10,1... | collective-permute-start | bytes 786440 | tf_op jit(solution)/shard_map/ppermute | solution.py:528
  263.0 440.9 %all-gather.17.cloned.1.call-start = ((), (), s32[]{:S(2)}) async-start(), calls=%async_computation.4 | async-start | bytes 10485760 | tf_op jit(solution)/shard_map/all_gather | solution.py:742
  282.2 60.2 %collective-permute-start.17 = (bf16[512,2048]{1,0:T(8,128)(2,1)}, bf16[512,2048]{1,0:T(8,128)(2,1)S(1)}, u32[]{:S(2)}, u32[]{:S(2)}) collective-permute-start(bf16[512,2048]{1,0:T(8,128)(2,1)} %product.4), channel_id=1, source_target_pairs={{0,1},{1,0},{2,3},{3,2},{4,5},{5,4},{6,7},{7,6},{8,9},{9,8},{10,11... | collective-permute-start | bytes 6291464 | tf_op jit(solution)/shard_map/ppermute | solution.py:528
  342.5 60.3 %collective-permute-start.18 = (bf16[512,2048]{1,0:T(8,128)(2,1)}, bf16[512,2048]{1,0:T(8,128)(2,1)}, u32[]{:S(2)}, u32[]{:S(2)}) collective-permute-start(bf16[512,2048]{1,0:T(8,128)(2,1)} %product.6), channel_id=1, source_target_pairs={{0,1},{1,0},{2,3},{3,2},{4,5},{5,4},{6,7},{7,6},{8,9},{9,8},{10,11... | collective-permute-start | bytes 6291464 | tf_op jit(solution)/shard_map/ppermute | solution.py:528
  407.0 438.3 %all-gather.19.cloned.1.call-start = ((), (), s32[]{:S(2)}) async-start(), calls=%async_computation.5 | async-start | bytes 10485760 | tf_op jit(solution)/shard_map/all_gather | solution.py:748
  409.4 6.5 collective-permute-start.19
  410.3 26.3 %collective-permute-start.27 = (bf16[512,2048]{1,0:T(8,128)(2,1)S(1)}, bf16[512,2048]{1,0:T(8,128)(2,1)}, u32[]{:S(2)}, u32[]{:S(2)}) collective-permute-start(bf16[512,2048]{1,0:T(8,128)(2,1)S(1)} %copy-done.4), channel_id=1, source_target_pairs={{0,4},{1,5},{2,6},{3,7},{4,0},{5,1},{6,2},{7,3},{8,12},{9,13},{10,... | collective-permute-start | bytes 6291464 | tf_op jit(solution)/shard_map/ppermute | solution.py:528
  410.3 26.3 %collective-permute-start.28 = (bf16[512,2048]{1,0:T(8,128)(2,1)}, bf16[512,2048]{1,0:T(8,128)(2,1)}, u32[]{:S(2)}, u32[]{:S(2)}) collective-permute-start(bf16[512,2048]{1,0:T(8,128)(2,1)} %get-tuple-element.211.refs_0_.refs_5_), channel_id=1, source_target_pairs={{0,4},{1,5},{2,6},{3,7},{4,0},{5,1},{6,2},{7,3},{8,12},{9,13},{10,... | collective-permute-start | bytes 6291464 | tf_op jit(solution)/shard_map/ppermute | solution.py:528
  433.5 27.3 %collective-permute-start.30 = (bf16[2,512,2048]{2,1,0:T(8,128)(2,1)}, bf16[2,512,2048]{2,1,0:T(8,128)(2,1)}, u32[]{:S(2)}, u32[]{:S(2)}) collective-permute-start(bf16[2,512,2048]{2,1,0:T(8,128)(2,1)} %get-tuple-element.213.refs_1_.refs_9_.refs_13_), channel_id=1, source_target_pairs={{0,4},{1,5},{2,6},{3,7},{4,0},{5,1},{6,2},{7,3},{8,12},{9,13},{10,... | collective-permute-start | bytes 12582920 | tf_op jit(solution)/shard_map/ppermute | solution.py:528
  434.0 13.1 %collective-permute-start.26 = (bf16[512,2048]{1,0:T(8,128)(2,1)}, bf16[512,2048]{1,0:T(8,128)(2,1)}, u32[]{:S(2)}, u32[]{:S(2)}) collective-permute-start(bf16[512,2048]{1,0:T(8,128)(2,1)} %copy-done.49), channel_id=1, source_target_pairs={{0,4},{1,5},{2,6},{3,7},{4,0},{5,1},{6,2},{7,3},{8,12},{9,13},{10,... | collective-permute-start | bytes 6291464 | tf_op jit(solution)/shard_map/ppermute | solution.py:528
  434.8 4.9 collective-permute-start.21
  436.6 34.3 %collective-permute-start.29 = (bf16[2,512,2048]{2,1,0:T(8,128)(2,1)}, bf16[2,512,2048]{2,1,0:T(8,128)(2,1)}, u32[]{:S(2)}, u32[]{:S(2)}) collective-permute-start(bf16[2,512,2048]{2,1,0:T(8,128)(2,1)} %get-tuple-element.212.refs_1_.refs_8_.refs_12_), channel_id=1, source_target_pairs={{0,4},{1,5},{2,6},{3,7},{4,0},{5,1},{6,2},{7,3},{8,12},{9,13},{10,... | collective-permute-start | bytes 12582920 | tf_op jit(solution)/shard_map/ppermute | solution.py:528
  436.6 10.9 %collective-permute-start.25 = (bf16[512,2048]{1,0:T(8,128)(2,1)}, bf16[512,2048]{1,0:T(8,128)(2,1)S(1)}, u32[]{:S(2)}, u32[]{:S(2)}) collective-permute-start(bf16[512,2048]{1,0:T(8,128)(2,1)} %get-tuple-element.227.n_ref.refs_0_), channel_id=1, source_target_pairs={{0,4},{1,5},{2,6},{3,7},{4,0},{5,1},{6,2},{7,3},{8,12},{9,13},{10,... | collective-permute-start | bytes 6291464 | tf_op jit(solution)/shard_map/ppermute | solution.py:528
  439.7 16.4 %collective-permute-start.23 = (bf16[512,2048]{1,0:T(8,128)(2,1)}, bf16[512,2048]{1,0:T(8,128)(2,1)}, u32[]{:S(2)}, u32[]{:S(2)}) collective-permute-start(bf16[512,2048]{1,0:T(8,128)(2,1)} %constant_dynamic-update-slice_fusion.4.att_ref), channel_id=1, source_target_pairs={{0,4},{1,5},{2,6},{3,7},{4,0},{5,1},{6,2},{7,3},{8,12},{9,13},{10,... | collective-permute-start | bytes 6291464 | tf_op jit(solution)/shard_map/ppermute | solution.py:528
  447.1 13.6 %collective-permute-start.22 = (bf16[512,2048]{1,0:T(8,128)(2,1)}, bf16[512,2048]{1,0:T(8,128)(2,1)}, u32[]{:S(2)}, u32[]{:S(2)}) collective-permute-start(bf16[512,2048]{1,0:T(8,128)(2,1)} %get-tuple-element.203.refs_0_), channel_id=1, source_target_pairs={{0,4},{1,5},{2,6},{3,7},{4,0},{5,1},{6,2},{7,3},{8,12},{9,13},{10,... | collective-permute-start | bytes 6291464 | tf_op jit(solution)/shard_map/ppermute | solution.py:528
  447.5 72.8 %collective-permute-start.36 = (bf16[2,512,2048]{2,1,0:T(8,128)(2,1)}, bf16[2,512,2048]{2,1,0:T(8,128)(2,1)}, u32[]{:S(2)}, u32[]{:S(2)}) collective-permute-start(bf16[2,512,2048]{2,1,0:T(8,128)(2,1)} %get-tuple-element.229.refs_0_.refs_9_.refs_13_), channel_id=1, source_target_pairs={{0,4},{1,5},{2,6},{3,7},{4,0},{5,1},{6,2},{7,3},{8,12},{9,13},{10,... | collective-permute-start | bytes 12582920 | tf_op jit(solution)/shard_map/ppermute | solution.py:528
  456.1 64.1 %collective-permute-start.35 = (bf16[2,512,2048]{2,1,0:T(8,128)(2,1)}, bf16[2,512,2048]{2,1,0:T(8,128)(2,1)}, u32[]{:S(2)}, u32[]{:S(2)}) collective-permute-start(bf16[2,512,2048]{2,1,0:T(8,128)(2,1)} %get-tuple-element.228.refs_0_.refs_8_.refs_12_), channel_id=1, source_target_pairs={{0,4},{1,5},{2,6},{3,7},{4,0},{5,1},{6,2},{7,3},{8,12},{9,13},{10,... | collective-permute-start | bytes 12582920 | tf_op jit(solution)/shard_map/ppermute | solution.py:528
  460.7 48.9 %collective-permute-start.32 = (bf16[512,2304]{1,0:T(8,128)(2,1)}, bf16[512,2304]{1,0:T(8,128)(2,1)}, u32[]{:S(2)}, u32[]{:S(2)}) collective-permute-start(bf16[512,2304]{1,0:T(8,128)(2,1)} %get-tuple-element.218), channel_id=1, source_target_pairs={{0,4},{1,5},{2,6},{3,7},{4,0},{5,1},{6,2},{7,3},{8,12},{9,13},{10,... | collective-permute-start | bytes 7077896 | tf_op jit(solution)/shard_map/ppermute | solution.py:528
  460.8 48.1 %collective-permute-start.31 = (bf16[512,2048]{1,0:T(8,128)(2,1)}, bf16[512,2048]{1,0:T(8,128)(2,1)}, u32[]{:S(2)}, u32[]{:S(2)}) collective-permute-start(bf16[512,2048]{1,0:T(8,128)(2,1)} %constant_dynamic-slice_fusion.5.refs_0_), channel_id=1, source_target_pairs={{0,4},{1,5},{2,6},{3,7},{4,0},{5,1},{6,2},{7,3},{8,12},{9,13},{10,... | collective-permute-start | bytes 6291464 | tf_op jit(solution)/shard_map/ppermute | solution.py:528
  470.9 31.2 %collective-permute-start.24 = (f32[24576]{0:T(1024)S(1)}, f32[24576]{0:T(1024)S(1)}, u32[]{:S(2)}, u32[]{:S(2)}) collective-permute-start(f32[24576]{0:T(1024)S(1)} %add.425), channel_id=1, source_target_pairs={{0,16},{1,17},{2,18},{3,19},{4,20},{5,21},{6,22},{7,23},{8,24},{9,... | collective-permute-start | bytes 294920 | tf_op jit(solution)/shard_map/ppermute | solution.py:528
  506.0 47.6 %collective-permute-start.34 = (bf16[2,2,256,1024]{3,2,0,1:T(8,128)(2,1)}, bf16[2,2,256,1024]{3,2,0,1:T(8,128)(2,1)S(1)}, u32[]{:S(2)}, u32[]{:S(2)}) collective-permute-start(bf16[2,2,256,1024]{3,2,0,1:T(8,128)(2,1)} %copy.76), channel_id=1, source_target_pairs={{0,8},{1,9},{2,10},{3,11},{4,12},{5,13},{6,14},{7,15},{8,0},{9,1},... | collective-permute-start | bytes 6291464 | tf_op jit(solution)/shard_map/ppermute | solution.py:528
  509.0 50.0 %collective-permute-start.33 = (bf16[2,2,256,1024]{3,2,0,1:T(8,128)(2,1)}, bf16[2,2,256,1024]{3,2,0,1:T(8,128)(2,1)S(1)}, u32[]{:S(2)}, u32[]{:S(2)}) collective-permute-start(bf16[2,2,256,1024]{3,2,0,1:T(8,128)(2,1)} %copy.74), channel_id=1, source_target_pairs={{0,16},{1,17},{2,18},{3,19},{4,20},{5,21},{6,22},{7,23},{8,24},{9,... | collective-permute-start | bytes 6291464 | tf_op jit(solution)/shard_map/ppermute | solution.py:528
  558.6 42.0 %collective-permute-start.42 = (bf16[2,1,256,1024]{3,2,0,1:T(8,128)(2,1)}, bf16[2,1,256,1024]{3,2,0,1:T(8,128)(2,1)S(1)}, u32[]{:S(2)}, u32[]{:S(2)}) collective-permute-start(bf16[2,1,256,1024]{3,2,0,1:T(8,128)(2,1)} %slice.149), channel_id=1, source_target_pairs={{0,16},{1,17},{2,18},{3,19},{4,20},{5,21},{6,22},{7,23},{8,24},{9,... | collective-permute-start | bytes 3145736 | tf_op jit(solution)/shard_map/ppermute | solution.py:528
  562.8 39.4 %collective-permute-start.41 = (bf16[2,1,256,1024]{3,2,0,1:T(8,128)(2,1)}, bf16[2,1,256,1024]{3,2,0,1:T(8,128)(2,1)}, u32[]{:S(2)}, u32[]{:S(2)}) collective-permute-start(bf16[2,1,256,1024]{3,2,0,1:T(8,128)(2,1)} %slice.147), channel_id=1, source_target_pairs={{0,8},{1,9},{2,10},{3,11},{4,12},{5,13},{6,14},{7,15},{8,0},{9,1},... | collective-permute-start | bytes 3145736 | tf_op jit(solution)/shard_map/ppermute | solution.py:528
  564.3 47.4 %collective-permute-start.40 = (bf16[1,2,256,1024]{3,2,1,0:T(8,128)(2,1)}, bf16[1,2,256,1024]{3,2,1,0:T(8,128)(2,1)}, u32[]{:S(2)}, u32[]{:S(2)}) collective-permute-start(bf16[1,2,256,1024]{3,2,1,0:T(8,128)(2,1)} %get-tuple-element.240), channel_id=1, source_target_pairs={{0,8},{1,9},{2,10},{3,11},{4,12},{5,13},{6,14},{7,15},{8,0},{9,1},... | collective-permute-start | bytes 3145736 | tf_op jit(solution)/shard_map/ppermute | solution.py:528
  564.8 9.4 %collective-permute-start.55 = (f32[24576]{0:T(1024)}, f32[24576]{0:T(1024)}, u32[]{:S(2)}, u32[]{:S(2)}) collective-permute-start(f32[24576]{0:T(1024)} %add.426), channel_id=1, source_target_pairs={{0,1},{1,2},{2,3},{3,0},{4,5},{5,6},{6,7},{7,4},{8,9},{9,10},{10,1... | collective-permute-start | bytes 294920 | tf_op jit(solution)/shard_map/ppermute | solution.py:528
  566.1 16.3 %collective-permute-start.56 = (f32[24576]{0:T(1024)}, f32[24576]{0:T(1024)}, u32[]{:S(2)}, u32[]{:S(2)}) collective-permute-start(f32[24576]{0:T(1024)} %add.426), channel_id=1, source_target_pairs={{0,2},{1,3},{2,0},{3,1},{4,6},{5,7},{6,4},{7,5},{8,10},{9,11},{10,... | collective-permute-start | bytes 294920 | tf_op jit(solution)/shard_map/ppermute | solution.py:528
  574.3 17.1 %collective-permute-start.57 = (f32[24576]{0:T(1024)}, f32[24576]{0:T(1024)}, u32[]{:S(2)}, u32[]{:S(2)}) collective-permute-start(f32[24576]{0:T(1024)} %add.426), channel_id=1, source_target_pairs={{0,3},{1,0},{2,1},{3,2},{4,7},{5,4},{6,5},{7,6},{8,11},{9,8},{10,9... | collective-permute-start | bytes 294920 | tf_op jit(solution)/shard_map/ppermute | solution.py:528
  582.3 31.2 %collective-permute-start.39 = (bf16[1,2,256,1024]{3,2,1,0:T(8,128)(2,1)}, bf16[1,2,256,1024]{3,2,1,0:T(8,128)(2,1)}, u32[]{:S(2)}, u32[]{:S(2)}) collective-permute-start(bf16[1,2,256,1024]{3,2,1,0:T(8,128)(2,1)} %get-tuple-element.238), channel_id=1, source_target_pairs={{0,16},{1,17},{2,18},{3,19},{4,20},{5,21},{6,22},{7,23},{8,24},{9,... | collective-permute-start | bytes 3145736 | tf_op jit(solution)/shard_map/ppermute | solution.py:528
  599.1 37.8 %collective-permute-start.38 = (bf16[1,2,256,1152]{3,2,1,0:T(8,128)(2,1)}, bf16[1,2,256,1152]{3,2,1,0:T(8,128)(2,1)S(1)}, u32[]{:S(2)}, u32[]{:S(2)}) collective-permute-start(bf16[1,2,256,1152]{3,2,1,0:T(8,128)(2,1)} %get-tuple-element.235), channel_id=1, source_target_pairs={{0,8},{1,9},{2,10},{3,11},{4,12},{5,13},{6,14},{7,15},{8,0},{9,1},... | collective-permute-start | bytes 3538952 | tf_op jit(solution)/shard_map/ppermute | solution.py:528
  600.5 37.8 %collective-permute-start.37 = (bf16[1,2,256,1152]{3,2,1,0:T(8,128)(2,1)}, bf16[1,2,256,1152]{3,2,1,0:T(8,128)(2,1)S(1)}, u32[]{:S(2)}, u32[]{:S(2)}) collective-permute-start(bf16[1,2,256,1152]{3,2,1,0:T(8,128)(2,1)} %get-tuple-element.233), channel_id=1, source_target_pairs={{0,16},{1,17},{2,18},{3,19},{4,20},{5,21},{6,22},{7,23},{8,24},{9,... | collective-permute-start | bytes 3538952 | tf_op jit(solution)/shard_map/ppermute | solution.py:528
  613.5 31.6 %collective-permute-start.46 = (bf16[1,1,256,1024]{3,2,1,0:T(8,128)(2,1)S(1)}, bf16[1,1,256,1024]{3,2,1,0:T(8,128)(2,1)S(1)}, u32[]{:S(2)}, u32[]{:S(2)}) collective-permute-start(bf16[1,1,256,1024]{3,2,1,0:T(8,128)(2,1)S(1)} %slice.157), channel_id=1, source_target_pairs={{0,16},{1,17},{2,18},{3,19},{4,20},{5,21},{6,22},{7,23},{8,24},{9,... | collective-permute-start | bytes 1572872 | tf_op jit(solution)/shard_map/ppermute | solution.py:528
  616.5 31.6 %collective-permute-start.45 = (bf16[1,1,256,1024]{3,2,1,0:T(8,128)(2,1)S(1)}, bf16[1,1,256,1024]{3,2,1,0:T(8,128)(2,1)S(1)}, u32[]{:S(2)}, u32[]{:S(2)}) collective-permute-start(bf16[1,1,256,1024]{3,2,1,0:T(8,128)(2,1)S(1)} %slice.155), channel_id=1, source_target_pairs={{0,8},{1,9},{2,10},{3,11},{4,12},{5,13},{6,14},{7,15},{8,0},{9,1},... | collective-permute-start | bytes 1572872 | tf_op jit(solution)/shard_map/ppermute | solution.py:528
  619.5 93.6 %collective-permute-start.48 = (bf16[2,2,256,1024]{3,2,0,1:T(8,128)(2,1)}, bf16[2,2,256,1024]{3,2,0,1:T(8,128)(2,1)}, u32[]{:S(2)}, u32[]{:S(2)}) collective-permute-start(bf16[2,2,256,1024]{3,2,0,1:T(8,128)(2,1)} %copy.78), channel_id=1, source_target_pairs={{0,8},{1,9},{2,10},{3,11},{4,12},{5,13},{6,14},{7,15},{8,0},{9,1},... | collective-permute-start | bytes 6291464 | tf_op jit(solution)/shard_map/ppermute | solution.py:528
  636.9 80.8 %collective-permute-start.50 = (bf16[2,2,256,1024]{3,2,1,0:T(8,128)(2,1)}, bf16[2,2,256,1024]{3,2,1,0:T(8,128)(2,1)}, u32[]{:S(2)}, u32[]{:S(2)}) collective-permute-start(bf16[2,2,256,1024]{3,2,1,0:T(8,128)(2,1)} %get-tuple-element.257), channel_id=1, source_target_pairs={{0,16},{1,17},{2,18},{3,19},{4,20},{5,21},{6,22},{7,23},{8,24},{9,... | collective-permute-start | bytes 6291464 | tf_op jit(solution)/shard_map/ppermute | solution.py:528
  638.3 63.1 %collective-permute-start.44 = (bf16[1,1,256,1152]{3,2,1,0:T(8,128)(2,1)S(1)}, bf16[1,1,256,1152]{3,2,1,0:T(8,128)(2,1)S(1)}, u32[]{:S(2)}, u32[]{:S(2)}) collective-permute-start(bf16[1,1,256,1152]{3,2,1,0:T(8,128)(2,1)S(1)} %slice.153), channel_id=1, source_target_pairs={{0,16},{1,17},{2,18},{3,19},{4,20},{5,21},{6,22},{7,23},{8,24},{9,... | collective-permute-start | bytes 1769480 | tf_op jit(solution)/shard_map/ppermute | solution.py:528
  645.1 180.3 %collective-permute-start.52 = (bf16[2,256,2048]{2,1,0:T(8,128)(2,1)}, bf16[2,256,2048]{2,1,0:T(8,128)(2,1)}, u32[]{:S(2)}, u32[]{:S(2)}) collective-permute-start(bf16[2,256,2048]{2,1,0:T(8,128)(2,1)} %pad_maximum_fusion.1), channel_id=1, source_target_pairs={{0,2},{1,3},{2,0},{3,1},{4,6},{5,7},{6,4},{7,5},{8,10},{9,11},{10,... | collective-permute-start | bytes 6291464 | tf_op jit(solution)/shard_map/ppermute | solution.py:528
  648.1 55.6 %collective-permute-start.43 = (bf16[1,1,256,1152]{3,2,1,0:T(8,128)(2,1)S(1)}, bf16[1,1,256,1152]{3,2,1,0:T(8,128)(2,1)S(1)}, u32[]{:S(2)}, u32[]{:S(2)}) collective-permute-start(bf16[1,1,256,1152]{3,2,1,0:T(8,128)(2,1)S(1)} %slice.151), channel_id=1, source_target_pairs={{0,8},{1,9},{2,10},{3,11},{4,12},{5,13},{6,14},{7,15},{8,0},{9,1},... | collective-permute-start | bytes 1769480 | tf_op jit(solution)/shard_map/ppermute | solution.py:528
  716.8 23.6 %collective-permute-start.49 = (bf16[2,1,256,1024]{3,2,0,1:T(8,128)(2,1)}, bf16[2,1,256,1024]{3,2,0,1:T(8,128)(2,1)}, u32[]{:S(2)}, u32[]{:S(2)}) collective-permute-start(bf16[2,1,256,1024]{3,2,0,1:T(8,128)(2,1)} %slice.160), channel_id=1, source_target_pairs={{0,16},{1,17},{2,18},{3,19},{4,20},{5,21},{6,22},{7,23},{8,24},{9,... | collective-permute-start | bytes 3145736 | tf_op jit(solution)/shard_map/ppermute | solution.py:528
  722.2 23.6 %collective-permute-start.51 = (bf16[2,1,256,1024]{3,2,1,0:T(8,128)(2,1)}, bf16[2,1,256,1024]{3,2,1,0:T(8,128)(2,1)}, u32[]{:S(2)}, u32[]{:S(2)}) collective-permute-start(bf16[2,1,256,1024]{3,2,1,0:T(8,128)(2,1)} %slice.162), channel_id=1, source_target_pairs={{0,8},{1,9},{2,10},{3,11},{4,12},{5,13},{6,14},{7,15},{8,0},{9,1},... | collective-permute-start | bytes 3145736 | tf_op jit(solution)/shard_map/ppermute | solution.py:528
  725.5 107.5 %collective-permute-start.47 = (bf16[544,512]{1,0:T(8,128)(2,1)}, bf16[544,512]{1,0:T(8,128)(2,1)}, u32[]{:S(2)}, u32[]{:S(2)}) collective-permute-start(bf16[544,512]{1,0:T(8,128)(2,1)} %pad_maximum_fusion.4), channel_id=1, source_target_pairs={{0,1},{1,2},{2,3},{3,0},{4,5},{5,6},{6,7},{7,4},{8,9},{9,10},{10,1... | collective-permute-start | bytes 1671176 | tf_op jit(solution)/shard_map/ppermute | solution.py:528
  727.5 109.8 %collective-permute-start.53 = (bf16[544,512]{1,0:T(8,128)(2,1)}, bf16[544,512]{1,0:T(8,128)(2,1)}, u32[]{:S(2)}, u32[]{:S(2)}) collective-permute-start(bf16[544,512]{1,0:T(8,128)(2,1)} %pad_maximum_fusion.5), channel_id=1, source_target_pairs={{0,2},{1,3},{2,0},{3,1},{4,6},{5,7},{6,4},{7,5},{8,10},{9,11},{10,... | collective-permute-start | bytes 1671176 | tf_op jit(solution)/shard_map/ppermute | solution.py:528
  740.5 98.0 %collective-permute-start.54 = (bf16[544,512]{1,0:T(8,128)(2,1)}, bf16[544,512]{1,0:T(8,128)(2,1)S(1)}, u32[]{:S(2)}, u32[]{:S(2)}) collective-permute-start(bf16[544,512]{1,0:T(8,128)(2,1)} %pad_maximum_fusion.6), channel_id=1, source_target_pairs={{0,3},{1,0},{2,1},{3,2},{4,7},{5,4},{6,5},{7,6},{8,11},{9,8},{10,9... | collective-permute-start | bytes 1671176 | tf_op jit(solution)/shard_map/ppermute | solution.py:528
  (56 other events, 512.3 us)
Sparse Core Ops, SparseCore 0:
  27.1 27.6 all-gather.8
  60.7 54.3 all-gather.20
  130.0 54.3 all-gather.10
  186.2 54.3 all-gather.12
  263.1 54.0 all-gather.14
  407.1 148.3 all-gather.16
  557.1 259.3 all-gather.18

commit v3 on v2

--- a/solution.py
+++ b/solution.py
@@ -587,8 +587,12 @@
             full = lax.dynamic_update_slice(full, gots[s] if s == 0 else arrive(gots[s]), at)
         return seq_out(full)
 
-    wq_far = [tp_shift(rows_at(query_weight, m * slab, slab), t * group) for t in range(1, wins)]
-    qb_far = [tp_shift(query_bias, t * group) for t in range(1, wins)]
+    def with_bias(piece, bias):
+        return jnp.concatenate([piece, jnp.broadcast_to(bias.reshape(1, -1), (16, bias.shape[0]))], axis=0)
+
+    wq_slab = with_bias(rows_at(query_weight, m * slab, slab), query_bias)
+    wq_far = [tp_shift(wq_slab, t * group) for t in range(1, wins)]
+    qb_far = [a[slab] for a in wq_far]
     wo_got = spread_send(lax.dynamic_slice_in_dim(out_weight, m * slab, slab, axis=1))
     n1 = seq_out(layer_norm(win.reshape(1), tokens, n1g, n1b, seq))
     kv = seq_out(jnp.dot(n1, keyval_weight, preferred_element_type=F32))
@@ -597,7 +601,7 @@
     values_t = values.T
     dcol = rows_at(doc_ids, win, 1).reshape(seq, 1)
     drow = rows_at(doc_ids, win, 1).reshape(1, 1, seq)
-    wq_far = [lax.all_gather(after(a, kv), "dp", axis=0, tiled=True) for a in wq_far]
+    wq_far = [lax.all_gather(after(a[:slab], kv), "dp", axis=0, tiled=True) for a in wq_far]
     go = [rows_at(grad_out, (win * group + lax.rem(r + group - s, group)) * rows, rows) for s in range(group)]
     das = []
 
@@ -610,14 +614,16 @@
         got = [rows_at(att, r * rows, rows)]
         return got + [group_shift(rows_at(att, lax.rem(r + s, group) * rows, rows), s) for s in range(1, group)]
 
+    up_slab = with_bias(rows_at(up_weight, m * slab, slab), up_bias)
+    up_far = [tp_shift(after(up_slab, kv), t * group) for t in range(1, wins)]
     att_got = [heads(query_weight, query_bias)]
     wo_z = spread_place(wo_got, 0)
     wo = lax.all_gather(wo_z, "dp", axis=0, tiled=False)
-    up_far = [tp_shift(after(rows_at(up_weight, m * slab, slab), wo_z), t * group) for t in range(1, wins)]
-    upb_far = [tp_shift(vec(up_bias), t * group) for t in range(1, wins)]
+    down_far = [tp_shift(after(rows_at(down_weight, m * uslab, uslab), wo_z), t * group) for t in range(1, wins)]
     for w, b in zip(wq_far, qb_far):
         att_got.append(heads(w, b))
-    down_far = [tp_shift(arrive(rows_at(down_weight, m * uslab, uslab)), t * group) for t in range(1, wins)]
+    upb_far = [a[slab : slab + 1] for a in up_far]
+    up_far = [lax.all_gather(arrive(a)[:slab], "dp", axis=0, tiled=True) for a in up_far]
     att_own = jnp.zeros((rows, n * lq), BF16)
     for t in range(wins):
         if t == wins - 1:
@@ -626,7 +632,6 @@
         for s in range(group):
             col = lax.rem(win * group + lax.rem(r + group - s, group) + n - t * group, n) * lq
             att_own = seq_out(lax.dynamic_update_slice(att_own, arrive(att_got[t][s]), (0, col)))
-    up_far = [lax.all_gather(after(a, att_own), "dp", axis=0, tiled=True) for a in up_far]
     x_own = rows_at(tokens, ti * rows, rows)
     h1, n2 = seq_out(proj_ln(att_own, wo, x_own, vec(out_bias), n2g, n2b))
 
@@ -687,25 +692,21 @@
     gn2_parts, sum_parts = [None] * group, [None] * group
 
     up(0, 0)
-    qb_got = [query_bias] + [tp_shift(after(query_bias, n2), s) for s in range(1, n)]
     for s in range(1, group):
         up(s, 0)
-    qb_all = jnp.zeros((n * lq,), BF16)
-    for s in range(n):
-        qb_all = lax.dynamic_update_slice(qb_all, arrive(qb_got[s]), (tp_at(-s) * lq,))
-    qb_all = seq_out(qb_all)
-    wq_got = spread_send(after(rows_at(query_weight, m * slab, slab), *ns))
+    wq_got = spread_send(after(wq_slab, *ns))
     for s in late:
         for k in range(1, wins):
             up(s, k)
         if s == late[0]:
             wq_z = spread_place(wq_got, 1)
-            wq = lax.all_gather(wq_z, "dp", axis=0, tiled=True)
+            qb_all = wq_z[slab]
+            wq = lax.all_gather(wq_z[:slab], "dp", axis=0, tiled=True)
         part = back_up(s)
         gn2_parts[s] = part if s == 0 else group_shift(part, -s)
     for s in late:
         part = down(s)
-        sum_parts[s] = part if s == 0 else group_shift(after(part, gn2_parts[1]), -s)
+        sum_parts[s] = part if s == 0 else group_shift(part, -s)
     ffn = []
 
     def ffn_grad(k):
@@ -731,15 +732,24 @@
     d_own = rows_at(dcol, row0, rows).reshape(1, rows)
     keys_t = keys.T
 
-    gq, gk, gv = seq_out(attn_bwd(0, 1, row0.reshape(1), seq_in(q_own), gatt, keys, values, keys_t, dcol, d_own, hd))
-    gkv_part = jnp.concatenate([gk, gv], axis=1)
-    gkv = rows_at(gkv_part, row0, rows)
-    kv_got = [group_shift(rows_at(gkv_part, lax.rem(r + s, group) * rows, rows).astype(BF16), s) for s in range(1, group)]
+    def heads_back(part):
+        return seq_out(attn_bwd(part, 2, row0.reshape(1), seq_in(q_own), gatt, keys, values, keys_t, dcol, d_own, hd))
+
+    back = [heads_back(0)]
     total = seq_in(h1) + down_bias.astype(F32)
     for sp in sum_parts:
         total = total + sp.astype(F32)
     total = seq_out(total.astype(BF16))
     output = lax.all_gather(total, "tp", axis=0, tiled=True)
+    back.append(heads_back(1))
+    gq = jnp.concatenate([x[0] for x in back], axis=1)
+    gk, gv = back[0][1] + back[1][1], back[0][2] + back[1][2]
+    gkv_part = jnp.concatenate([gk, gv], axis=1)
+    gkv = rows_at(gkv_part, row0, rows)
+    kv_got = [group_shift(rows_at(gkv_part, lax.rem(r + s, group) * rows, rows).astype(BF16), s) for s in range(1, group)]
+    for k in range(1, wins):
+        ffn[k].keep()
+        ffn[k].go()
     for got in kv_got:
         gkv = gkv + arrive(got).astype(F32)
     gkv = gkv.astype(BF16)
@@ -762,29 +772,33 @@
             flying = perm(pack, **swaps.pop(0))
 
     swap_small()
-    swap_small()
     out_g.keep()
     swap_small()
     for k in range(1, wins):
-        ffn[k].keep()
+        ffn[k].stage()
+    ffn[0].keep()
+    swap_small()
+    far = [tp_shift(ffn[k].finish(), -k * group) for k in range(1, wins)]
+    qkv_g.keep()
     while swaps:
         swap_small()
     swap_small()
-    pack_got = [tp_shift(pack, s) for s in range(1, n)]
-    for k in range(1, wins):
-        ffn[k].go()
-    qkv_g.keep()
-    ffn[0].keep()
-    for k in range(1, wins):
-        ffn[k].stage()
+    pack_got = [pack] + [tp_shift(pack, s) for s in range(1, n)]
     out_g.go()
     qkv_g.go()
-    far = [tp_shift(ffn[k].finish(), -k * group) for k in range(1, wins)]
     ffn[0].go()
     out_g.stage()
     qkv_g.stage()
+    ffn[0].stage()
+    output = seq_out(copied(arrive(output)))
+    grad_tokens = seq_out(copied(arrive(grad_tokens)))
+    far_up, far_down = 0.0, 0.0
+    for got in far:
+        got = arrive(got).astype(F32)
+        far_up, far_down = seq_out([far_up + got[0], far_down + got[1]])
     g_out = out_g.finish()[0]
     g_qkv = qkv_g.finish()[0]
+    f0 = ffn[0].finish()
 
     take_cols = lambda x, i: lax.dynamic_slice_in_dim(x, i * lq, lq, axis=1)
     kv_rows = g_qkv.shape[0] // n
@@ -796,16 +810,8 @@
 
     mine = share(ti)
     shares = [tp_shift(jnp.concatenate(share(tp_at(s)), axis=0), s) for s in range(1, n)]
-    output = seq_out(copied(arrive(output)))
-    ffn[0].stage()
-    f0 = ffn[0].finish()
-    g_upw, g_downw = f0[0].astype(F32), f0[1].astype(F32)
-    for got in far:
-        got = arrive(got).astype(F32)
-        g_upw = g_upw + got[0]
-        g_downw = g_downw + got[1]
-    g_upw = seq_out(g_upw)
-    g_downw = seq_out(g_downw.T).T
+    g_upw = seq_out(f0[0].astype(F32) + far_up)
+    g_downw = seq_out((f0[1].astype(F32) + far_down).T).T
     g_outw, g_qw, g_kvw = [x.astype(F32) for x in mine]
     for got in shares:
         got = arrive(got).astype(F32)
@@ -814,11 +820,13 @@
         g_kvw = g_kvw + got[2 * fr :]
     g_outw = seq_out(g_outw.T)
     g_kvw = g_kvw.reshape(kv_rows, -1)
-    grad_tokens = copied(arrive(grad_tokens))
-    pack = lax.dynamic_update_slice(jnp.zeros((n, pack.shape[0]), F32), pack[None], (ti, 0))
-    for s in range(1, n):
-        pack = lax.dynamic_update_slice(pack, pack_got[s - 1][None], (tp_at(-s), 0))
-    pack = jnp.sum(pack, axis=0)
+    pack = jnp.zeros_like(pack)
+    for j in range(n):
+        part = jnp.zeros_like(pack)
+        for s in range(n):
+            part = part + jnp.where(tp_at(-s) == j, arrive(pack_got[s]), 0.0)
+        pack = pack + part
+    pack = seq_out(pack)
     piece = lambda row, at, size: lax.dynamic_slice_in_dim(pack, row * d + at, size)
     vs = d // ndp
     qs = lq // ndp

time: 878 us -> 868 us (0.989)
  local copies, waits for them, and re-layouts: 86.6 us -> 71.8 us
    dynamic_update_slice x8 -> x0, local copies, waits for them, and re-layouts: 11.7 us -> none  [the longest x3 7.98 us: per_device(): pack = lax.dynamic_update_slice(pack, pack_got[s - 1][None], (tp_at(-s), 0))]
    ppermute x58 -> x53, starting transfers between devices: 55.3 us -> 60.9 us  [perm(): return lax.ppermute(x, ('dp', 'tp'), pairs)]
    unnamed x116 -> x123, local copies, waits for them, and re-layouts: 19.2 us -> 14.7 us
    pallas_call x1 -> x2, Pallas kernels: 34.5 us -> 37.3 us  [attn_bwd(): call(functools.partial(attn_bwd_kernel, hd ** (-0.5), qb, reach), (heads,...]
    convert_element_type x16 -> x15, other arithmetic: 19.1 us -> 18.2 us  [stage(): x = seq_out((keep.astype(F32) + arrive(got).astype(F32)).astype(BF16))]
    ppermute x58 -> x53, waiting for transfers between devices: 300 us -> 300 us  [perm(): return lax.ppermute(x, ('dp', 'tp'), pairs)]
  transfers between devices with their start and end apart: 65 -> 60, of which waited for: 21 -> 17; matrix products, arithmetic and copies ran while one was open for 19% -> 17% of each run, Pallas kernels for 35% -> 37%
where the time goes in v3:
time: 868 us; the launch traced here: 856 us
  Pallas kernels  315 us (36%)
  waiting for transfers between devices  301 us (35%)
  local copies, waits for them, and re-layouts  71.8 us (8%)
  starting transfers between devices  61.6 us (7%)
  other arithmetic  49.9 us (6%)
  matrix products  41.8 us (5%)
  between operations  15.7 us (2%)
    ppermute x53, waiting for transfers between devices, perm(): return lax.ppermute(x, ('dp', 'tp'), pairs)  300 us
    pallas_call x4, Pallas kernels, grad_call(): call(functools.partial(grad_kernel, count, pairs, places), (pairs, places...  79.4 us
    ppermute x53, starting transfers between devices, perm(): return lax.ppermute(x, ('dp', 'tp'), pairs)  60.9 us
    pallas_call x4, Pallas kernels, ffn_up(): call(functools.partial(up_kernel, ready), (u // bn,), [whole((r, d)), pl....  56.6 us
    pallas_call x4, Pallas kernels, product(): call(functools.partial(product_kernel, len(xs), nt), (n // bn,), [plane(x...  56.4 us
    pallas_call x2, Pallas kernels, attn_bwd(): call(functools.partial(attn_bwd_kernel, hd ** (-0.5), qb, reach), (heads,...  37.3 us
    pallas_call x2, Pallas kernels, attn_fwd(): call(functools.partial(attn_fwd_kernel, hd ** (-0.5), qb), (wins, heads),...  20.8 us
    convert_element_type x15, other arithmetic, stage(): x = seq_out((keep.astype(F32) + arrive(got).astype(F32)).astype(BF16))  18.2 us
  transfers between devices with their start and end apart: 60, of which 17 were waited for; matrix products, arithmetic and copies ran while one was open for 17% of the time, Pallas kernels for 37%

profile of v3, /device:TPU:0, one launch (start us, length us, event | category | flops | bytes accessed | tf_op | source)
XLA Modules:
  0.0 856.0 jit_solution(16156651306144348578)
XLA Ops:
  9.5 4.1 collective-permute-start.3
  16.2 6.3 norm1.1
  22.5 4.4 fusion.35
  40.4 5.6 add_convert_fusion.15.q_ref
  46.9 10.4 %attn_fwd.2 = bf16[1024,512]{1,0:T(8,128)(2,1)} custom-call(bf16[1024,512]{1,0:T(8,128)(2,1)} %add_convert_fusion.15.q_ref, bf16[1024,128]{1,0:T(8,128)(2,1)} %copy.49.k_ref, bf16[128,1024]{1,0:T(8,128)(2,1)} %copy.50.vt_ref, s32[1024,1]{1,0:T(8,128)} %copy.51.dcol_ref, s32[1,1,1024]{2,1,0:T(1,128)} %get-tuple-element.331.drow_ref), custom_call_target="tpu_custom_call" | custom-call | flops 1342177280 | bytes 2621440 | tf_op jit(solution)/shard_map/attn_fwd/pallas_call | solution.py:116
  61.3 2.8 constant_dynamic-slice_fusion.3
  65.2 2.3 collective-permute-start.8
  68.2 6.8 add_convert_fusion.14.q_ref
  75.0 10.4 %attn_fwd.3 = bf16[1024,512]{1,0:T(8,128)(2,1)} custom-call(bf16[1024,512]{1,0:T(8,128)(2,1)} %add_convert_fusion.14.q_ref, bf16[1024,128]{1,0:T(8,128)(2,1)} %copy.49.k_ref, bf16[128,1024]{1,0:T(8,128)(2,1)} %copy.50.vt_ref, s32[1024,1]{1,0:T(8,128)} %copy.51.dcol_ref, s32[1,1,1024]{2,1,0:T(1,128)} %get-tuple-element.331.drow_ref), custom_call_target="tpu_custom_call" | custom-call | flops 1342177280 | bytes 2621440 | tf_op jit(solution)/shard_map/attn_fwd/pallas_call | solution.py:116
  85.4 30.4 %collective-permute-done.8 = bf16[272,2048]{1,0:T(8,128)(2,1)} collective-permute-done((bf16[272,2048]{1,0:T(8,128)(2,1)}, bf16[272,2048]{1,0:T(8,128)(2,1)}, u32[]{:S(2)}, u32[]{:S(2)}) %collective-permute-start.8) | collective-permute-done | bytes 1114144 | tf_op jit(solution)/shard_map/ppermute | solution.py:528
  115.8 2.3 slice.131
  119.3 3.2 constant_dynamic-slice_fusion.6.x_ref
  124.3 3.1 constant_dynamic-slice_fusion.8
  127.4 2.5 collective-permute-start.9
  132.3 2.4 collective-permute-done.4
  135.5 9.3 %convolution_convert_fusion.1.refs_0_ = bf16[512,2048]{1,0:T(8,128)(2,1)} fusion(bf16[512,2048]{1,0:T(8,128)(2,1)S(1)} %get-tuple-element.189.refs_0_.refs_3_.refs_4_, bf16[2048,2048]{1,0:T(8,128)(2,1)} %refs_2_.7), kind=kOutput, calls=%fused_computation.7 | convolution fusion | flops 4296015872 | bytes 12582912 | tf_op jit(solution)/shard_map/dot_general | solution.py:609
  145.0 5.8 convolution_convert_fusion.refs_0_
  151.7 11.9 %collective-permute-done.5 = bf16[512,512]{1,0:T(8,128)(2,1)S(1)} collective-permute-done((bf16[512,512]{1,0:T(8,128)(2,1)S(1)}, bf16[512,512]{1,0:T(8,128)(2,1)S(1)}, u32[]{:S(2)}, u32[]{:S(2)}) %collective-permute-start.5) | collective-permute-done | bytes 524320 | tf_op jit(solution)/shard_map/ppermute | solution.py:528
  164.4 11.3 %proj_ln.1 = (f32[512,2048]{1,0:T(8,128)}, bf16[512,2048]{1,0:T(8,128)(2,1)}) custom-call(bf16[512,2048]{1,0:T(8,128)(2,1)} %constant_dynamic-update-slice_fusion.4.att_ref, bf16[8,2048,256]{2,1,0:T(8,128)(2,1)} %bitcast.93, bf16[512,2048]{1,0:T(8,128)(2,1)} %constant_dynamic-slice_fusion.6.x_ref, bf16[1,2048]{1,0:T(2,128)(2,1)} %reshape.124.ob_ref, ...), custom_call_target="tpu_custom_call" | custom-call | flops 4294967296 | bytes 18874368 | tf_op jit(solution)/shard_map/proj_ln/pallas_call | solution.py:151
  175.8 2.5 collective-permute-start.6
  180.2 11.5 %ffn_up.4 = (bf16[2,512,2048]{2,1,0:T(8,128)(2,1)}, f32[1,2048]{1,0:T(1,128)}) custom-call(bf16[512,2048]{1,0:T(8,128)(2,1)} %get-tuple-element.221.n_ref.refs_0_, bf16[2048,2048]{1,0:T(8,128)(2,1)} %refs_2_.5, bf16[1,2048]{1,0:T(2,128)(2,1)} %reshape.128.b_ref, bf16[512,2048]{1,0:T(8,128)(2,1)} %convolution_convert_fusion.1.refs_0_), custom_call_target="tpu_custom_call" | custom-call | flops 4294967296 | bytes 16777216 | tf_op jit(solution)/shard_map/ffn_up/pallas_call | solution.py:195
  191.7 31.5 %collective-permute-done.6.n_ref.refs_1_ = bf16[512,2048]{1,0:T(8,128)(2,1)S(1)} collective-permute-done((bf16[512,2048]{1,0:T(8,128)(2,1)}, bf16[512,2048]{1,0:T(8,128)(2,1)S(1)}, u32[]{:S(2)}, u32[]{:S(2)}) %collective-permute-start.6) | collective-permute-done | bytes 2097184 | tf_op jit(solution)/shard_map/ppermute | solution.py:528
  223.1 6.3 collective-permute-start.11
  230.3 2.0 collective-permute-start.7
  232.4 11.5 %ffn_up.5 = (bf16[2,512,2048]{2,1,0:T(8,128)(2,1)}, f32[1,2048]{1,0:T(1,128)}) custom-call(bf16[512,2048]{1,0:T(8,128)(2,1)} %copy-done.53, bf16[2048,2048]{1,0:T(8,128)(2,1)} %refs_2_.5, bf16[1,2048]{1,0:T(2,128)(2,1)} %reshape.128.b_ref, bf16[512,2048]{1,0:T(8,128)(2,1)} %convolution_convert_fusion.refs_0_), custom_call_target="tpu_custom_call" | custom-call | flops 4294967296 | bytes 16777216 | tf_op jit(solution)/shard_map/ffn_up/pallas_call | solution.py:195
  244.1 16.6 %ffn_up.6 = (bf16[2,512,2048]{2,1,0:T(8,128)(2,1)}, f32[1,2048]{1,0:T(1,128)}) custom-call(bf16[512,2048]{1,0:T(8,128)(2,1)} %copy-done.53, bf16[2048,2048]{1,0:T(8,128)(2,1)} %all-gather.11.cloned.1.call-done.w_ref.refs_3_, bf16[1,2048]{1,0:T(2,128)(2,1)} %slice.172.b_ref, bf16[512,2048]{1,0:T(8,128)(2,1)} %copy-done.17, ...), custom_call_target="tpu_custom_call" | custom-call | flops 8589934592 | bytes 16777216 | tf_op jit(solution)/shard_map/ffn_up/pallas_call | solution.py:195
  263.7 3.2 constant_dynamic-slice_fusion.5.refs_0_
  266.9 14.7 %product.4 = bf16[512,2048]{1,0:T(8,128)(2,1)} custom-call(bf16[2,512,2048]{2,1,0:T(8,128)(2,1)} %get-tuple-element.223.refs_0_.refs_9_.refs_13_, bf16[2,512,2048]{2,1,0:T(8,128)(2,1)} %get-tuple-element.192.refs_1_.refs_9_.refs_13_, bf16[2048,2048]{1,0:T(8,128)(2,1)} %refs_2_.5, bf16[2048,2048]{1,0:T(8,128)(2,1)} %all-gather.11.cloned.1.call-done.w_ref.refs_3_), custom_call_target="tpu_custom_call" | custom-call | flops 8589934592 | bytes 23068672 | tf_op jit(solution)/shard_map/product/pallas_call | solution.py:225
  281.7 17.0 %ffn_up.7 = (bf16[2,512,2048]{2,1,0:T(8,128)(2,1)}, f32[1,2048]{1,0:T(1,128)}) custom-call(bf16[512,2048]{1,0:T(8,128)(2,1)} %get-tuple-element.221.n_ref.refs_0_, bf16[2048,2048]{1,0:T(8,128)(2,1)} %all-gather.11.cloned.1.call-done.w_ref.refs_3_, bf16[1,2048]{1,0:T(2,128)(2,1)} %slice.172.b_ref, bf16[512,2048]{1,0:T(8,128)(2,1)} %copy-done.3, ...), custom_call_target="tpu_custom_call" | custom-call | flops 8589934592 | bytes 16777216 | tf_op jit(solution)/shard_map/ffn_up/pallas_call | solution.py:195
  298.7 13.9 %product.5.refs_0_ = bf16[512,2048]{1,0:T(8,128)(2,1)} custom-call(bf16[2,512,2048]{2,1,0:T(8,128)(2,1)} %get-tuple-element.222.refs_0_.refs_8_.refs_12_, bf16[2,512,2048]{2,1,0:T(8,128)(2,1)} %get-tuple-element.191.refs_1_.refs_8_.refs_12_, bf16[2048,2048]{1,0:T(8,128)(2,1)} %refs_2_.5, bf16[2048,2048]{1,0:T(8,128)(2,1)} %all-gather.11.cloned.1.call-done.w_ref.refs_3_), custom_call_target="tpu_custom_call" | custom-call | flops 8589934592 | bytes 23068672 | tf_op jit(solution)/shard_map/product/pallas_call | solution.py:225
  312.6 14.0 %product.6 = bf16[512,2048]{1,0:T(8,128)(2,1)} custom-call(bf16[2,512,2048]{2,1,0:T(8,128)(2,1)} %get-tuple-element.223.refs_0_.refs_9_.refs_13_, bf16[2,512,2048]{2,1,0:T(8,128)(2,1)} %get-tuple-element.192.refs_1_.refs_9_.refs_13_, bf16[2048,2048]{1,0:T(8,128)(2,1)} %refs_2_.7, bf16[2048,2048]{1,0:T(8,128)(2,1)} %all-gather.13.cloned.1.call-done.refs_1_.refs_3_), custom_call_target="tpu_custom_call" | custom-call | flops 8589934592 | bytes 23068672 | tf_op jit(solution)/shard_map/product/pallas_call | solution.py:225
  328.4 13.8 %product.7 = bf16[512,2048]{1,0:T(8,128)(2,1)} custom-call(bf16[2,512,2048]{2,1,0:T(8,128)(2,1)} %get-tuple-element.222.refs_0_.refs_8_.refs_12_, bf16[2,512,2048]{2,1,0:T(8,128)(2,1)} %get-tuple-element.191.refs_1_.refs_8_.refs_12_, bf16[2048,2048]{1,0:T(8,128)(2,1)} %refs_2_.7, bf16[2048,2048]{1,0:T(8,128)(2,1)} %all-gather.13.cloned.1.call-done.refs_1_.refs_3_), custom_call_target="tpu_custom_call" | custom-call | flops 8589934592 | bytes 23068672 | tf_op jit(solution)/shard_map/product/pallas_call | solution.py:225
  343.7 14.6 %norm2_back.1 = (f32[512,2048]{1,0:T(8,128)}, bf16[512,2048]{1,0:T(8,128)(2,1)}, bf16[512,2048]{1,0:T(8,128)(2,1)}, f32[8,2048]{1,0:T(8,128)}) custom-call(bf16[512,2048]{1,0:T(8,128)(2,1)} %product.5.refs_0_, bf16[512,2048]{1,0:T(8,128)(2,1)} %copy-done.22, f32[512,2048]{1,0:T(8,128)} %get-tuple-element.183.refs_2_, bf16[512,2048]{1,0:T(8,128)(2,1)} %copy-done.3, ...), custom_call_target="tpu_custom_call" | custom-call | flops 4294967296 | bytes 29360128 | tf_op jit(solution)/shard_map/norm2_back/pallas_call | solution.py:275
  358.3 9.9 %add_convert_fusion.5.q_ref = bf16[512,2048]{1,0:T(8,128)(2,1)} fusion(bf16[512,2048]{1,0:T(8,128)(2,1)} %constant_dynamic-slice_fusion.5.refs_0_, bf16[2048,2048]{1,0:T(8,128)(2,1)} %all-gather.15.cloned.1.call-done.wq_ref, f32[2048]{0:T(1024)S(1)} %bitcast.109), kind=kOutput, calls=%fused_computation.5 | convolution fusion | flops 4297064448 | bytes 12591104 | tf_op jit(solution)/shard_map/dot_general | solution.py:722
  368.2 18.6 %attn_bwd.2 = (bf16[512,1024]{1,0:T(8,128)(2,1)}, f32[1024,128]{1,0:T(8,128)}, f32[1024,128]{1,0:T(8,128)}) custom-call(s32[1]{0:T(128)} %bitcast.6.row0_ref, bf16[512,2048]{1,0:T(8,128)(2,1)} %add_convert_fusion.5.q_ref, bf16[512,2048]{1,0:T(8,128)(2,1)} %get-tuple-element.181.go_ref, bf16[1024,128]{1,0:T(8,128)(2,1)} %copy.49.k_ref, ...), custom_call_target="tpu_custom_call" | custom-call | flops 4026531840 | bytes 5242880 | tf_op jit(solution)/shard_map/attn_bwd/pallas_call | solution.py:334
  386.9 4.1 add_convert_fusion.4
  393.6 6.1 collective-permute-done.16.refs_6_
  402.1 18.7 %attn_bwd.3 = (bf16[512,1024]{1,0:T(8,128)(2,1)}, f32[1024,128]{1,0:T(8,128)}, f32[1024,128]{1,0:T(8,128)}) custom-call(s32[1]{0:T(128)} %bitcast.6.row0_ref, bf16[512,2048]{1,0:T(8,128)(2,1)} %add_convert_fusion.5.q_ref, bf16[512,2048]{1,0:T(8,128)(2,1)} %get-tuple-element.181.go_ref, bf16[1024,128]{1,0:T(8,128)(2,1)} %copy.49.k_ref, ...), custom_call_target="tpu_custom_call" | custom-call | flops 4026531840 | bytes 5242880 | tf_op jit(solution)/shard_map/attn_bwd/pallas_call | solution.py:334
  425.9 29.6 %weight_grad.4 = (bf16[2,2,256,1024]{3,2,1,0:T(8,128)(2,1)}, bf16[2,2,256,1024]{3,2,1,0:T(8,128)(2,1)}, bf16[2,2,256,1024]{3,2,1,0:T(8,128)(2,1)}, bf16[2,2,256,1024]{3,2,1,0:T(8,128)(2,1)}) custom-call(s32[1]{0:T(128)} %bitcast.9.m_ref, bf16[512,2048]{1,0:T(8,128)(2,1)} %get-tuple-element.221.n_ref.refs_0_, bf16[512,2048]{1,0:T(8,128)(2,1)} %copy-done.53, ...), custom_call_target="tpu_custom_call" | custom-call | flops 17179869184 | bytes 33554432 | tf_op jit(solution)/shard_map/weight_grad/pallas_call | solution.py:467
  456.1 3.1 copy.62
  461.4 14.0 %norm1_back.1 = (bf16[512,2048]{1,0:T(8,128)(2,1)}, f32[8,2048]{1,0:T(8,128)}, f32[8,256]{1,0:T(8,128)}) custom-call(bf16[512,2048]{1,0:T(8,128)(2,1)} %pad_maximum_fusion.1.gq_ref, bf16[512,256]{1,0:T(8,128)(2,1)} %fusion.9.gkv_ref, bf16[2048,2048]{1,0:T(8,128)(2,1)} %all-gather.15.cloned.1.call-done.wq_ref, bf16[2048,256]{1,0:T(8,128)(2,1)} %wkv_ref.1, ...), custom_call_target="tpu_custom_call" | custom-call | flops 4831838208 | bytes 22020096 | tf_op jit(solution)/shard_map/norm1_back/pallas_call | solution.py:376
  476.3 3.1 copy.60
  483.2 9.8 %weight_grad.5 = (bf16[1,2,256,1024]{3,2,1,0:T(8,128)(2,1)}, bf16[1,2,256,1024]{3,2,1,0:T(8,128)(2,1)}, bf16[1,2,256,1024]{3,2,1,0:T(8,128)(2,1)}, bf16[1,2,256,1024]{3,2,1,0:T(8,128)(2,1)}) custom-call(s32[1]{0:T(128)} %bitcast.9.m_ref, bf16[512,2048]{1,0:T(8,128)(2,1)} %get-tuple-element.215.refs_0_, bf16[512,2048]{1,0:T(8,128)(2,1)} %collective-permute-done.24.refs_1_, ...), custom_call_target="tpu_custom_call" | custom-call | flops 4294967296 | bytes 10485760 | tf_op jit(solution)/shard_map/weight_grad/pallas_call | solution.py:467
  493.5 13.3 %collective-permute-done.21 = bf16[2,2,256,1024]{3,2,0,1:T(8,128)(2,1)} collective-permute-done((bf16[2,2,256,1024]{3,2,0,1:T(8,128)(2,1)}, bf16[2,2,256,1024]{3,2,0,1:T(8,128)(2,1)}, u32[]{:S(2)}, u32[]{:S(2)}) %collective-permute-start.21) | collective-permute-done | bytes 2097184 | tf_op jit(solution)/shard_map/ppermute | solution.py:528
  506.8 2.7 add_convert_fusion.3
  509.5 18.0 %collective-permute-done.20 = bf16[2,2,256,1024]{3,2,0,1:T(8,128)(2,1)} collective-permute-done((bf16[2,2,256,1024]{3,2,0,1:T(8,128)(2,1)}, bf16[2,2,256,1024]{3,2,0,1:T(8,128)(2,1)}, u32[]{:S(2)}, u32[]{:S(2)}) %collective-permute-start.20) | collective-permute-done | bytes 2097184 | tf_op jit(solution)/shard_map/ppermute | solution.py:528
  528.1 2.5 add_convert_fusion.2
  534.8 29.5 %weight_grad.6 = (bf16[2,2,256,1024]{3,2,1,0:T(8,128)(2,1)}, bf16[2,2,256,1024]{3,2,1,0:T(8,128)(2,1)}, bf16[2,2,256,1024]{3,2,1,0:T(8,128)(2,1)}, bf16[2,2,256,1024]{3,2,1,0:T(8,128)(2,1)}) custom-call(s32[1]{0:T(128)} %bitcast.9.m_ref, bf16[512,2048]{1,0:T(8,128)(2,1)} %get-tuple-element.221.n_ref.refs_0_, bf16[512,2048]{1,0:T(8,128)(2,1)} %copy-done.53, ...), custom_call_target="tpu_custom_call" | custom-call | flops 17179869184 | bytes 33554432 | tf_op jit(solution)/shard_map/weight_grad/pallas_call | solution.py:467
  568.1 10.5 %weight_grad.7 = (bf16[1,2,256,1152]{3,2,1,0:T(8,128)(2,1)}, bf16[1,2,256,1152]{3,2,1,0:T(8,128)(2,1)}, bf16[1,2,256,1152]{3,2,1,0:T(8,128)(2,1)}, bf16[1,2,256,1152]{3,2,1,0:T(8,128)(2,1)}) custom-call(s32[1]{0:T(128)} %bitcast.9.m_ref, bf16[512,2048]{1,0:T(8,128)(2,1)} %constant_dynamic-slice_fusion.5.refs_0_, ...), custom_call_target="tpu_custom_call" | custom-call | flops 4831838208 | bytes 11534336 | tf_op jit(solution)/shard_map/weight_grad/pallas_call | solution.py:467
  582.9 2.0 collective-permute-start.50
  588.6 17.1 %collective-permute-done.39 = bf16[1,2,256,1024]{3,2,1,0:T(8,128)(2,1)} collective-permute-done((bf16[1,2,256,1024]{3,2,1,0:T(8,128)(2,1)}, bf16[1,2,256,1024]{3,2,1,0:T(8,128)(2,1)}, u32[]{:S(2)}, u32[]{:S(2)}) %collective-permute-start.39) | collective-permute-done | bytes 1048608 | tf_op jit(solution)/shard_map/ppermute | solution.py:528
  611.6 19.4 %collective-permute-done.37 = bf16[1,2,256,1152]{3,2,1,0:T(8,128)(2,1)} collective-permute-done((bf16[1,2,256,1152]{3,2,1,0:T(8,128)(2,1)}, bf16[1,2,256,1152]{3,2,1,0:T(8,128)(2,1)}, u32[]{:S(2)}, u32[]{:S(2)}) %collective-permute-start.37) | collective-permute-done | bytes 1179680 | tf_op jit(solution)/shard_map/ppermute | solution.py:528
  635.2 49.5 %collective-permute-done.40 = bf16[1,1,256,1024]{3,2,1,0:T(8,128)(2,1)S(1)} collective-permute-done((bf16[1,1,256,1024]{3,2,1,0:T(8,128)(2,1)S(1)}, bf16[1,1,256,1024]{3,2,1,0:T(8,128)(2,1)S(1)}, u32[]{:S(2)}, u32[]{:S(2)}) %collective-permute-start.40) | collective-permute-done | bytes 524320 | tf_op jit(solution)/shard_map/ppermute | solution.py:528
  689.6 7.0 collective-permute-done.43
  711.1 11.5 %collective-permute-done.46 = bf16[2,1,256,1024]{3,2,0,1:T(8,128)(2,1)} collective-permute-done((bf16[2,1,256,1024]{3,2,0,1:T(8,128)(2,1)}, bf16[2,1,256,1024]{3,2,0,1:T(8,128)(2,1)}, u32[]{:S(2)}, u32[]{:S(2)}) %collective-permute-start.46) | collective-permute-done | bytes 1048608 | tf_op jit(solution)/shard_map/ppermute | solution.py:528
  722.6 2.0 collective-permute-start.45
  730.0 9.0 %copied.2 = bf16[2048,2048]{1,0:T(8,128)(2,1)} custom-call(bf16[2048,2048]{1,0:T(8,128)(2,1)} %all-gather.17.cloned.1.call-done.x_ref), custom_call_target="tpu_custom_call" | custom-call | bytes 16777216 | tf_op jit(solution)/shard_map/copied/pallas_call | solution.py:488
  739.0 9.0 %copied.3 = bf16[2048,2048]{1,0:T(8,128)(2,1)} custom-call(bf16[2048,2048]{1,0:T(8,128)(2,1)} %all-gather.19.cloned.1.call-done.x_ref), custom_call_target="tpu_custom_call" | custom-call | bytes 16777216 | tf_op jit(solution)/shard_map/copied/pallas_call | solution.py:488
  748.0 67.6 %collective-permute-done.41 = bf16[2,256,2048]{2,1,0:T(8,128)(2,1)} collective-permute-done((bf16[2,256,2048]{2,1,0:T(8,128)(2,1)}, bf16[2,256,2048]{2,1,0:T(8,128)(2,1)}, u32[]{:S(2)}, u32[]{:S(2)}) %collective-permute-start.41) | collective-permute-done | bytes 2097184 | tf_op jit(solution)/shard_map/ppermute | solution.py:528
  815.6 2.1 convert_element_type.282
  821.6 6.1 collective-permute-done.48
  830.4 7.9 collective-permute-done.49
  840.1 2.2 copy.65
  842.2 2.9 copy.66
  (336 shorter events, 123.4 us)
Async XLA Ops:
  7.2 61.0 %all-gather.9.cloned.1.call-start = ((), (), s32[]{:S(2)}) async-start(), calls=%async_computation | async-start | bytes 2359296 | tf_op jit(solution)/shard_map/all_gather | solution.py:604
  9.5 17.4 %collective-permute-start.3 = (bf16[272,512]{1,0:T(8,128)(2,1)S(1)}, bf16[272,512]{1,0:T(8,128)(2,1)S(1)}, u32[]{:S(2)}, u32[]{:S(2)}) collective-permute-start(bf16[272,512]{1,0:T(8,128)(2,1)S(1)} %pad_maximum_fusion.9), channel_id=1, source_target_pairs={{0,2},{1,3},{2,0},{3,1},{4,6},{5,7},{6,4},{7,5},{8,10},{9,11},{10,... | collective-permute-start | bytes 835592 | tf_op jit(solution)/shard_map/ppermute | solution.py:528
  27.7 136.8 %all-gather.21.cloned.1.call-start = ((), (), s32[]{:S(2)}) async-start(), calls=%async_computation.6 | async-start | bytes 9437184 | tf_op jit(solution)/shard_map/all_gather | solution.py:621
  29.5 27.8 %collective-permute-start = (bf16[512,256]{1,0:T(8,128)(2,1)}, bf16[512,256]{1,0:T(8,128)(2,1)}, u32[]{:S(2)}, u32[]{:S(2)}) collective-permute-start(bf16[512,256]{1,0:T(8,128)(2,1)} %get-tuple-element.303), channel_id=1, source_target_pairs={{0,1},{1,2},{2,3},{3,0},{4,5},{5,6},{6,7},{7,4},{8,9},{9,10},{10,1... | collective-permute-start | bytes 786440 | tf_op jit(solution)/shard_map/ppermute | solution.py:528
  31.1 26.2 %collective-permute-start.1 = (bf16[512,256]{1,0:T(8,128)(2,1)}, bf16[512,256]{1,0:T(8,128)(2,1)}, u32[]{:S(2)}, u32[]{:S(2)}) collective-permute-start(bf16[512,256]{1,0:T(8,128)(2,1)} %get-tuple-element.303), channel_id=1, source_target_pairs={{0,2},{1,3},{2,0},{3,1},{4,6},{5,7},{6,4},{7,5},{8,10},{9,11},{10,... | collective-permute-start | bytes 786440 | tf_op jit(solution)/shard_map/ppermute | solution.py:528
  33.0 24.4 %collective-permute-start.2 = (bf16[512,256]{1,0:T(8,128)(2,1)}, bf16[512,256]{1,0:T(8,128)(2,1)}, u32[]{:S(2)}, u32[]{:S(2)}) collective-permute-start(bf16[512,256]{1,0:T(8,128)(2,1)} %get-tuple-element.303), channel_id=1, source_target_pairs={{0,3},{1,0},{2,1},{3,2},{4,7},{5,4},{6,5},{7,6},{8,11},{9,8},{10,9... | collective-permute-start | bytes 786440 | tf_op jit(solution)/shard_map/ppermute | solution.py:528
  61.3 182.8 %all-gather.11.cloned.1.call-start = ((), (), s32[]{:S(2)}) async-start(), calls=%async_computation.1 | async-start | bytes 9437184 | tf_op jit(solution)/shard_map/all_gather | solution.py:626
  65.2 50.6 %collective-permute-start.8 = (bf16[272,2048]{1,0:T(8,128)(2,1)}, bf16[272,2048]{1,0:T(8,128)(2,1)}, u32[]{:S(2)}, u32[]{:S(2)}) collective-permute-start(bf16[272,2048]{1,0:T(8,128)(2,1)} %pad_maximum_fusion.4), channel_id=1, source_target_pairs={{0,2},{1,3},{2,0},{3,1},{4,6},{5,7},{6,4},{7,5},{8,10},{9,11},{10,... | collective-permute-start | bytes 3342344 | tf_op jit(solution)/shard_map/ppermute | solution.py:528
  85.4 32.9 %copy-start.32 = (bf16[1024,512]{1,0:T(8,128)(2,1)S(1)}, bf16[1024,512]{1,0:T(8,128)(2,1)}, u32[]{:S(2)}) copy-start(bf16[1024,512]{1,0:T(8,128)(2,1)} %attn_fwd.2) | copy-start | bytes 3145732
  118.1 126.0 %all-gather.13.cloned.1.call-start = ((), (), s32[]{:S(2)}) async-start(), calls=%async_computation.2 | async-start | bytes 9437184 | tf_op jit(solution)/shard_map/all_gather | solution.py:639
  119.2 15.5 %collective-permute-start.4 = (bf16[512,512]{1,0:T(8,128)(2,1)}, bf16[512,512]{1,0:T(8,128)(2,1)S(1)}, u32[]{:S(2)}, u32[]{:S(2)}) collective-permute-start(bf16[512,512]{1,0:T(8,128)(2,1)} %get-tuple-element.318), channel_id=1, source_target_pairs={{0,1},{1,0},{2,3},{3,2},{4,5},{5,4},{6,7},{7,6},{8,9},{9,8},{10,11... | collective-permute-start | bytes 1572872 | tf_op jit(solution)/shard_map/ppermute | solution.py:528
  127.4 48.3 %collective-permute-start.9 = (bf16[256,2048]{1,0:T(8,128)(2,1)}, bf16[256,2048]{1,0:T(8,128)(2,1)}, u32[]{:S(2)}, u32[]{:S(2)}) collective-permute-start(bf16[256,2048]{1,0:T(8,128)(2,1)} %get-tuple-element.165), channel_id=1, source_target_pairs={{0,2},{1,3},{2,0},{3,1},{4,6},{5,7},{6,4},{7,5},{8,10},{9,11},{10,... | collective-permute-start | bytes 3145736 | tf_op jit(solution)/shard_map/ppermute | solution.py:528
  144.9 18.7 %collective-permute-start.5 = (bf16[512,512]{1,0:T(8,128)(2,1)S(1)}, bf16[512,512]{1,0:T(8,128)(2,1)S(1)}, u32[]{:S(2)}, u32[]{:S(2)}) collective-permute-start(bf16[512,512]{1,0:T(8,128)(2,1)S(1)} %get-tuple-element.316), channel_id=1, source_target_pairs={{0,1},{1,0},{2,3},{3,2},{4,5},{5,4},{6,7},{7,6},{8,9},{9,8},{10,11... | collective-permute-start | bytes 1572872 | tf_op jit(solution)/shard_map/ppermute | solution.py:528
  175.7 182.6 %all-gather.15.cloned.1.call-start = ((), (), s32[]{:S(2)}) async-start(), calls=%async_computation.3 | async-start | bytes 9437184 | tf_op jit(solution)/shard_map/all_gather | solution.py:704
  175.8 47.4 %collective-permute-start.6 = (bf16[512,2048]{1,0:T(8,128)(2,1)}, bf16[512,2048]{1,0:T(8,128)(2,1)S(1)}, u32[]{:S(2)}, u32[]{:S(2)}) collective-permute-start(bf16[512,2048]{1,0:T(8,128)(2,1)} %get-tuple-element.221.n_ref.refs_0_), channel_id=1, source_target_pairs={{0,1},{1,0},{2,3},{3,2},{4,5},{5,4},{6,7},{7,6},{8,9},{9,8},{10,11... | collective-permute-start | bytes 6291464 | tf_op jit(solution)/shard_map/ppermute | solution.py:528
  223.1 37.6 %collective-permute-start.11 = (bf16[272,512]{1,0:T(8,128)(2,1)S(1)}, bf16[272,512]{1,0:T(8,128)(2,1)S(1)}, u32[]{:S(2)}, u32[]{:S(2)}) collective-permute-start(bf16[272,512]{1,0:T(8,128)(2,1)S(1)} %pad_maximum_fusion.9), channel_id=1, source_target_pairs={{0,3},{1,0},{2,1},{3,2},{4,7},{5,4},{6,5},{7,6},{8,11},{9,8},{10,9... | collective-permute-start | bytes 835592 | tf_op jit(solution)/shard_map/ppermute | solution.py:528
  229.4 31.3 %collective-permute-start.10 = (bf16[272,512]{1,0:T(8,128)(2,1)S(1)}, bf16[272,512]{1,0:T(8,128)(2,1)S(1)}, u32[]{:S(2)}, u32[]{:S(2)}) collective-permute-start(bf16[272,512]{1,0:T(8,128)(2,1)S(1)} %pad_maximum_fusion.9), channel_id=1, source_target_pairs={{0,2},{1,3},{2,0},{3,1},{4,6},{5,7},{6,4},{7,5},{8,10},{9,11},{10,... | collective-permute-start | bytes 835592 | tf_op jit(solution)/shard_map/ppermute | solution.py:528
  230.3 30.4 %collective-permute-start.7 = (bf16[272,512]{1,0:T(8,128)(2,1)S(1)}, bf16[272,512]{1,0:T(8,128)(2,1)S(1)}, u32[]{:S(2)}, u32[]{:S(2)}) collective-permute-start(bf16[272,512]{1,0:T(8,128)(2,1)S(1)} %pad_maximum_fusion.9), channel_id=1, source_target_pairs={{0,1},{1,2},{2,3},{3,0},{4,5},{5,6},{6,7},{7,4},{8,9},{9,10},{10,1... | collective-permute-start | bytes 835592 | tf_op jit(solution)/shard_map/ppermute | solution.py:528
  262.0 468.1 %all-gather.17.cloned.1.call-start = ((), (), s32[]{:S(2)}) async-start(), calls=%async_computation.4 | async-start | bytes 10485760 | tf_op jit(solution)/shard_map/all_gather | solution.py:743
  281.5 60.7 %collective-permute-start.12 = (bf16[512,2048]{1,0:T(8,128)(2,1)}, bf16[512,2048]{1,0:T(8,128)(2,1)S(1)}, u32[]{:S(2)}, u32[]{:S(2)}) collective-permute-start(bf16[512,2048]{1,0:T(8,128)(2,1)} %product.4), channel_id=1, source_target_pairs={{0,1},{1,0},{2,3},{3,2},{4,5},{5,4},{6,7},{7,6},{8,9},{9,8},{10,11... | collective-permute-start | bytes 6291464 | tf_op jit(solution)/shard_map/ppermute | solution.py:528
  326.6 60.3 %collective-permute-start.13 = (bf16[512,2048]{1,0:T(8,128)(2,1)}, bf16[512,2048]{1,0:T(8,128)(2,1)}, u32[]{:S(2)}, u32[]{:S(2)}) collective-permute-start(bf16[512,2048]{1,0:T(8,128)(2,1)} %product.6), channel_id=1, source_target_pairs={{0,1},{1,0},{2,3},{3,2},{4,5},{5,4},{6,7},{7,6},{8,9},{9,8},{10,11... | collective-permute-start | bytes 6291464 | tf_op jit(solution)/shard_map/ppermute | solution.py:528
  391.0 348.0 %all-gather.19.cloned.1.call-start = ((), (), s32[]{:S(2)}) async-start(), calls=%async_computation.5 | async-start | bytes 10485760 | tf_op jit(solution)/shard_map/all_gather | solution.py:758
  392.6 7.1 collective-permute-start.16
  392.6 32.8 %collective-permute-start.19 = (bf16[2,512,2048]{2,1,0:T(8,128)(2,1)}, bf16[2,512,2048]{2,1,0:T(8,128)(2,1)}, u32[]{:S(2)}, u32[]{:S(2)}) collective-permute-start(bf16[2,512,2048]{2,1,0:T(8,128)(2,1)} %get-tuple-element.192.refs_1_.refs_9_.refs_13_), channel_id=1, source_target_pairs={{0,4},{1,5},{2,6},{3,7},{4,0},{5,1},{6,2},{7,3},{8,12},{9,13},{10,... | collective-permute-start | bytes 12582920 | tf_op jit(solution)/shard_map/ppermute | solution.py:528
  393.1 32.6 %collective-permute-start.18 = (bf16[2,512,2048]{2,1,0:T(8,128)(2,1)}, bf16[2,512,2048]{2,1,0:T(8,128)(2,1)}, u32[]{:S(2)}, u32[]{:S(2)}) collective-permute-start(bf16[2,512,2048]{2,1,0:T(8,128)(2,1)} %get-tuple-element.191.refs_1_.refs_8_.refs_12_), channel_id=1, source_target_pairs={{0,4},{1,5},{2,6},{3,7},{4,0},{5,1},{6,2},{7,3},{8,12},{9,13},{10,... | collective-permute-start | bytes 12582920 | tf_op jit(solution)/shard_map/ppermute | solution.py:528
  393.1 31.7 %collective-permute-start.17 = (bf16[512,2048]{1,0:T(8,128)(2,1)}, bf16[512,2048]{1,0:T(8,128)(2,1)}, u32[]{:S(2)}, u32[]{:S(2)}) collective-permute-start(bf16[512,2048]{1,0:T(8,128)(2,1)} %copy-done.17), channel_id=1, source_target_pairs={{0,4},{1,5},{2,6},{3,7},{4,0},{5,1},{6,2},{7,3},{8,12},{9,13},{10,... | collective-permute-start | bytes 6291464 | tf_op jit(solution)/shard_map/ppermute | solution.py:528
  393.6 31.3 %collective-permute-start.15 = (bf16[512,2048]{1,0:T(8,128)(2,1)}, bf16[512,2048]{1,0:T(8,128)(2,1)}, u32[]{:S(2)}, u32[]{:S(2)}) collective-permute-start(bf16[512,2048]{1,0:T(8,128)(2,1)} %copy-done.53), channel_id=1, source_target_pairs={{0,4},{1,5},{2,6},{3,7},{4,0},{5,1},{6,2},{7,3},{8,12},{9,13},{10,... | collective-permute-start | bytes 6291464 | tf_op jit(solution)/shard_map/ppermute | solution.py:528
  401.1 24.1 %collective-permute-start.14 = (bf16[512,2048]{1,0:T(8,128)(2,1)}, bf16[512,2048]{1,0:T(8,128)(2,1)}, u32[]{:S(2)}, u32[]{:S(2)}) collective-permute-start(bf16[512,2048]{1,0:T(8,128)(2,1)} %get-tuple-element.221.n_ref.refs_0_), channel_id=1, source_target_pairs={{0,4},{1,5},{2,6},{3,7},{4,0},{5,1},{6,2},{7,3},{8,12},{9,13},{10,... | collective-permute-start | bytes 6291464 | tf_op jit(solution)/shard_map/ppermute | solution.py:528
  424.7 31.3 %collective-permute-start.22 = (bf16[512,256]{1,0:T(8,128)(2,1)S(1)}, bf16[512,256]{1,0:T(8,128)(2,1)S(1)}, u32[]{:S(2)}, u32[]{:S(2)}) collective-permute-start(bf16[512,256]{1,0:T(8,128)(2,1)S(1)} %fusion.6), channel_id=1, source_target_pairs={{0,1},{1,0},{2,3},{3,2},{4,5},{5,4},{6,7},{7,6},{8,9},{9,8},{10,11... | collective-permute-start | bytes 786440 | tf_op jit(solution)/shard_map/ppermute | solution.py:528
  424.8 107.0 %collective-permute-start.27 = (bf16[2,512,2048]{2,1,0:T(8,128)(2,1)}, bf16[2,512,2048]{2,1,0:T(8,128)(2,1)}, u32[]{:S(2)}, u32[]{:S(2)}) collective-permute-start(bf16[2,512,2048]{2,1,0:T(8,128)(2,1)} %get-tuple-element.223.refs_0_.refs_9_.refs_13_), channel_id=1, source_target_pairs={{0,4},{1,5},{2,6},{3,7},{4,0},{5,1},{6,2},{7,3},{8,12},{9,13},{10,... | collective-permute-start | bytes 12582920 | tf_op jit(solution)/shard_map/ppermute | solution.py:528
  425.2 108.2 %collective-permute-start.26 = (bf16[2,512,2048]{2,1,0:T(8,128)(2,1)}, bf16[2,512,2048]{2,1,0:T(8,128)(2,1)}, u32[]{:S(2)}, u32[]{:S(2)}) collective-permute-start(bf16[2,512,2048]{2,1,0:T(8,128)(2,1)} %get-tuple-element.222.refs_0_.refs_8_.refs_12_), channel_id=1, source_target_pairs={{0,4},{1,5},{2,6},{3,7},{4,0},{5,1},{6,2},{7,3},{8,12},{9,13},{10,... | collective-permute-start | bytes 12582920 | tf_op jit(solution)/shard_map/ppermute | solution.py:528
  425.4 54.8 %collective-permute-start.24 = (bf16[512,2048]{1,0:T(8,128)(2,1)}, bf16[512,2048]{1,0:T(8,128)(2,1)}, u32[]{:S(2)}, u32[]{:S(2)}) collective-permute-start(bf16[512,2048]{1,0:T(8,128)(2,1)} %get-tuple-element.215.refs_0_), channel_id=1, source_target_pairs={{0,4},{1,5},{2,6},{3,7},{4,0},{5,1},{6,2},{7,3},{8,12},{9,13},{10,... | collective-permute-start | bytes 6291464 | tf_op jit(solution)/shard_map/ppermute | solution.py:528
  425.7 57.5 %collective-permute-start.25 = (bf16[512,2048]{1,0:T(8,128)(2,1)}, bf16[512,2048]{1,0:T(8,128)(2,1)}, u32[]{:S(2)}, u32[]{:S(2)}) collective-permute-start(bf16[512,2048]{1,0:T(8,128)(2,1)} %constant_dynamic-update-slice_fusion.4.att_ref), channel_id=1, source_target_pairs={{0,4},{1,5},{2,6},{3,7},{4,0},{5,1},{6,2},{7,3},{8,12},{9,13},{10,... | collective-permute-start | bytes 6291464 | tf_op jit(solution)/shard_map/ppermute | solution.py:528
  459.2 47.6 %collective-permute-start.21 = (bf16[2,2,256,1024]{3,2,0,1:T(8,128)(2,1)}, bf16[2,2,256,1024]{3,2,0,1:T(8,128)(2,1)}, u32[]{:S(2)}, u32[]{:S(2)}) collective-permute-start(bf16[2,2,256,1024]{3,2,0,1:T(8,128)(2,1)} %copy.62), channel_id=1, source_target_pairs={{0,8},{1,9},{2,10},{3,11},{4,12},{5,13},{6,14},{7,15},{8,0},{9,1},... | collective-permute-start | bytes 6291464 | tf_op jit(solution)/shard_map/ppermute | solution.py:528
  480.1 47.4 %collective-permute-start.20 = (bf16[2,2,256,1024]{3,2,0,1:T(8,128)(2,1)}, bf16[2,2,256,1024]{3,2,0,1:T(8,128)(2,1)}, u32[]{:S(2)}, u32[]{:S(2)}) collective-permute-start(bf16[2,2,256,1024]{3,2,0,1:T(8,128)(2,1)} %copy.60), channel_id=1, source_target_pairs={{0,16},{1,17},{2,18},{3,19},{4,20},{5,21},{6,22},{7,23},{8,24},{9,... | collective-permute-start | bytes 6291464 | tf_op jit(solution)/shard_map/ppermute | solution.py:528
  483.2 9.8 %collective-permute-start.23 = (f32[24576]{0:T(1024)S(1)}, f32[24576]{0:T(1024)S(1)}, u32[]{:S(2)}, u32[]{:S(2)}) collective-permute-start(f32[24576]{0:T(1024)S(1)} %fusion.28), channel_id=1, source_target_pairs={{0,4},{1,5},{2,6},{3,7},{4,0},{5,1},{6,2},{7,3},{8,12},{9,13},{10,... | collective-permute-start | bytes 294920 | tf_op jit(solution)/shard_map/ppermute | solution.py:528
  483.2 23.6 %copy-start.21 = (bf16[2,2,256,1024]{3,2,1,0:T(8,128)(2,1)S(1)}, bf16[2,2,256,1024]{3,2,1,0:T(8,128)(2,1)}, u32[]{:S(2)}) copy-start(bf16[2,2,256,1024]{3,2,1,0:T(8,128)(2,1)} %get-tuple-element.197) | copy-start | bytes 6291460
  493.0 75.1 %collective-permute-start.33 = (bf16[512,2304]{1,0:T(8,128)(2,1)S(1)}, bf16[512,2304]{1,0:T(8,128)(2,1)}, u32[]{:S(2)}, u32[]{:S(2)}) collective-permute-start(bf16[512,2304]{1,0:T(8,128)(2,1)S(1)} %get-tuple-element.232), channel_id=1, source_target_pairs={{0,4},{1,5},{2,6},{3,7},{4,0},{5,1},{6,2},{7,3},{8,12},{9,13},{10,... | collective-permute-start | bytes 7077896 | tf_op jit(solution)/shard_map/ppermute | solution.py:528
  506.8 61.3 %collective-permute-start.32 = (bf16[512,2048]{1,0:T(8,128)(2,1)}, bf16[512,2048]{1,0:T(8,128)(2,1)}, u32[]{:S(2)}, u32[]{:S(2)}) collective-permute-start(bf16[512,2048]{1,0:T(8,128)(2,1)} %constant_dynamic-slice_fusion.5.refs_0_), channel_id=1, source_target_pairs={{0,4},{1,5},{2,6},{3,7},{4,0},{5,1},{6,2},{7,3},{8,12},{9,13},{10,... | collective-permute-start | bytes 6291464 | tf_op jit(solution)/shard_map/ppermute | solution.py:528
  527.5 36.7 %collective-permute-start.28 = (f32[24576]{0:T(1024)S(1)}, f32[24576]{0:T(1024)S(1)}, u32[]{:S(2)}, u32[]{:S(2)}) collective-permute-start(f32[24576]{0:T(1024)S(1)} %fusion.32), channel_id=1, source_target_pairs={{0,8},{1,9},{2,10},{3,11},{4,12},{5,13},{6,14},{7,15},{8,0},{9,1},... | collective-permute-start | bytes 294920 | tf_op jit(solution)/shard_map/ppermute | solution.py:528
  531.8 33.0 %collective-permute-start.31 = (bf16[2,1,256,1024]{3,2,0,1:T(8,128)(2,1)S(1)}, bf16[2,1,256,1024]{3,2,0,1:T(8,128)(2,1)}, u32[]{:S(2)}, u32[]{:S(2)}) collective-permute-start(bf16[2,1,256,1024]{3,2,0,1:T(8,128)(2,1)S(1)} %slice.178), channel_id=1, source_target_pairs={{0,16},{1,17},{2,18},{3,19},{4,20},{5,21},{6,22},{7,23},{8,24},{9,... | collective-permute-start | bytes 3145736 | tf_op jit(solution)/shard_map/ppermute | solution.py:528
  533.3 33.1 %collective-permute-start.30 = (bf16[2,1,256,1024]{3,2,0,1:T(8,128)(2,1)}, bf16[2,1,256,1024]{3,2,0,1:T(8,128)(2,1)}, u32[]{:S(2)}, u32[]{:S(2)}) collective-permute-start(bf16[2,1,256,1024]{3,2,0,1:T(8,128)(2,1)} %slice.176), channel_id=1, source_target_pairs={{0,8},{1,9},{2,10},{3,11},{4,12},{5,13},{6,14},{7,15},{8,0},{9,1},... | collective-permute-start | bytes 3145736 | tf_op jit(solution)/shard_map/ppermute | solution.py:528
  564.3 14.4 %collective-permute-start.29 = (f32[24576]{0:T(1024)S(1)}, f32[24576]{0:T(1024)S(1)}, u32[]{:S(2)}, u32[]{:S(2)}) collective-permute-start(f32[24576]{0:T(1024)S(1)} %add.480), channel_id=1, source_target_pairs={{0,16},{1,17},{2,18},{3,19},{4,20},{5,21},{6,22},{7,23},{8,24},{9,... | collective-permute-start | bytes 294920 | tf_op jit(solution)/shard_map/ppermute | solution.py:528
  579.3 26.4 %collective-permute-start.39 = (bf16[1,2,256,1024]{3,2,1,0:T(8,128)(2,1)}, bf16[1,2,256,1024]{3,2,1,0:T(8,128)(2,1)}, u32[]{:S(2)}, u32[]{:S(2)}) collective-permute-start(bf16[1,2,256,1024]{3,2,1,0:T(8,128)(2,1)} %get-tuple-element.247), channel_id=1, source_target_pairs={{0,8},{1,9},{2,10},{3,11},{4,12},{5,13},{6,14},{7,15},{8,0},{9,1},... | collective-permute-start | bytes 3145736 | tf_op jit(solution)/shard_map/ppermute | solution.py:528
  579.9 28.2 %collective-permute-start.38 = (bf16[1,2,256,1024]{3,2,1,0:T(8,128)(2,1)}, bf16[1,2,256,1024]{3,2,1,0:T(8,128)(2,1)}, u32[]{:S(2)}, u32[]{:S(2)}) collective-permute-start(bf16[1,2,256,1024]{3,2,1,0:T(8,128)(2,1)} %get-tuple-element.245), channel_id=1, source_target_pairs={{0,16},{1,17},{2,18},{3,19},{4,20},{5,21},{6,22},{7,23},{8,24},{9,... | collective-permute-start | bytes 3145736 | tf_op jit(solution)/shard_map/ppermute | solution.py:528
  581.4 49.5 %collective-permute-start.37 = (bf16[1,2,256,1152]{3,2,1,0:T(8,128)(2,1)}, bf16[1,2,256,1152]{3,2,1,0:T(8,128)(2,1)}, u32[]{:S(2)}, u32[]{:S(2)}) collective-permute-start(bf16[1,2,256,1152]{3,2,1,0:T(8,128)(2,1)} %get-tuple-element.242), channel_id=1, source_target_pairs={{0,8},{1,9},{2,10},{3,11},{4,12},{5,13},{6,14},{7,15},{8,0},{9,1},... | collective-permute-start | bytes 3538952 | tf_op jit(solution)/shard_map/ppermute | solution.py:528
  582.9 262.9 %collective-permute-start.50 = (f32[24576]{0:T(1024)}, f32[24576]{0:T(1024)}, u32[]{:S(2)}, u32[]{:S(2)}) collective-permute-start(f32[24576]{0:T(1024)} %add.483), channel_id=1, source_target_pairs={{0,1},{1,2},{2,3},{3,0},{4,5},{5,6},{6,7},{7,4},{8,9},{9,10},{10,1... | collective-permute-start | bytes 294920 | tf_op jit(solution)/shard_map/ppermute | solution.py:528
  584.8 49.3 %collective-permute-start.36 = (bf16[1,2,256,1152]{3,2,1,0:T(8,128)(2,1)}, bf16[1,2,256,1152]{3,2,1,0:T(8,128)(2,1)S(1)}, u32[]{:S(2)}, u32[]{:S(2)}) collective-permute-start(bf16[1,2,256,1152]{3,2,1,0:T(8,128)(2,1)} %get-tuple-element.240), channel_id=1, source_target_pairs={{0,16},{1,17},{2,18},{3,19},{4,20},{5,21},{6,22},{7,23},{8,24},{9,... | collective-permute-start | bytes 3538952 | tf_op jit(solution)/shard_map/ppermute | solution.py:528
  605.7 94.2 %collective-permute-start.35 = (bf16[2,2,256,1024]{3,2,0,1:T(8,128)(2,1)S(1)}, bf16[2,2,256,1024]{3,2,0,1:T(8,128)(2,1)S(1)}, u32[]{:S(2)}, u32[]{:S(2)}) collective-permute-start(bf16[2,2,256,1024]{3,2,0,1:T(8,128)(2,1)S(1)} %copy.64), channel_id=1, source_target_pairs={{0,8},{1,9},{2,10},{3,11},{4,12},{5,13},{6,14},{7,15},{8,0},{9,1},... | collective-permute-start | bytes 6291464 | tf_op jit(solution)/shard_map/ppermute | solution.py:528
  608.3 95.4 %collective-permute-start.34 = (bf16[2,2,256,1024]{3,2,1,0:T(8,128)(2,1)S(1)}, bf16[2,2,256,1024]{3,2,1,0:T(8,128)(2,1)S(1)}, u32[]{:S(2)}, u32[]{:S(2)}) collective-permute-start(bf16[2,2,256,1024]{3,2,1,0:T(8,128)(2,1)S(1)} %copy-done.54), channel_id=1, source_target_pairs={{0,16},{1,17},{2,18},{3,19},{4,20},{5,21},{6,22},{7,23},{8,24},{9,... | collective-permute-start | bytes 6291464 | tf_op jit(solution)/shard_map/ppermute | solution.py:528
  611.5 23.3 %copy-start.26 = (bf16[1,2,256,1152]{3,2,1,0:T(8,128)(2,1)S(1)}, bf16[1,2,256,1152]{3,2,1,0:T(8,128)(2,1)}, u32[]{:S(2)}) copy-start(bf16[1,2,256,1152]{3,2,1,0:T(8,128)(2,1)} %get-tuple-element.238) | copy-start | bytes 3538948
  631.0 53.7 %collective-permute-start.40 = (bf16[1,1,256,1024]{3,2,1,0:T(8,128)(2,1)S(1)}, bf16[1,1,256,1024]{3,2,1,0:T(8,128)(2,1)S(1)}, u32[]{:S(2)}, u32[]{:S(2)}) collective-permute-start(bf16[1,1,256,1024]{3,2,1,0:T(8,128)(2,1)S(1)} %slice.180), channel_id=1, source_target_pairs={{0,16},{1,17},{2,18},{3,19},{4,20},{5,21},{6,22},{7,23},{8,24},{9,... | collective-permute-start | bytes 1572872 | tf_op jit(solution)/shard_map/ppermute | solution.py:528
  634.1 52.4 %collective-permute-start.42 = (bf16[1,1,256,1024]{3,2,1,0:T(8,128)(2,1)S(1)}, bf16[1,1,256,1024]{3,2,1,0:T(8,128)(2,1)S(1)}, u32[]{:S(2)}, u32[]{:S(2)}) collective-permute-start(bf16[1,1,256,1024]{3,2,1,0:T(8,128)(2,1)S(1)} %slice.183), channel_id=1, source_target_pairs={{0,8},{1,9},{2,10},{3,11},{4,12},{5,13},{6,14},{7,15},{8,0},{9,1},... | collective-permute-start | bytes 1572872 | tf_op jit(solution)/shard_map/ppermute | solution.py:528
  684.7 11.8 %collective-permute-start.43 = (bf16[1,1,256,1152]{3,2,1,0:T(8,128)(2,1)S(1)}, bf16[1,1,256,1152]{3,2,1,0:T(8,128)(2,1)S(1)}, u32[]{:S(2)}, u32[]{:S(2)}) collective-permute-start(bf16[1,1,256,1152]{3,2,1,0:T(8,128)(2,1)S(1)} %slice.185), channel_id=1, source_target_pairs={{0,16},{1,17},{2,18},{3,19},{4,20},{5,21},{6,22},{7,23},{8,24},{9,... | collective-permute-start | bytes 1769480 | tf_op jit(solution)/shard_map/ppermute | solution.py:528
  686.6 12.0 %collective-permute-start.44 = (bf16[1,1,256,1152]{3,2,1,0:T(8,128)(2,1)S(1)}, bf16[1,1,256,1152]{3,2,1,0:T(8,128)(2,1)S(1)}, u32[]{:S(2)}, u32[]{:S(2)}) collective-permute-start(bf16[1,1,256,1152]{3,2,1,0:T(8,128)(2,1)S(1)} %slice.187), channel_id=1, source_target_pairs={{0,8},{1,9},{2,10},{3,11},{4,12},{5,13},{6,14},{7,15},{8,0},{9,1},... | collective-permute-start | bytes 1769480 | tf_op jit(solution)/shard_map/ppermute | solution.py:528
  696.6 149.2 %collective-permute-start.51 = (f32[24576]{0:T(1024)}, f32[24576]{0:T(1024)}, u32[]{:S(2)}, u32[]{:S(2)}) collective-permute-start(f32[24576]{0:T(1024)} %add.483), channel_id=1, source_target_pairs={{0,2},{1,3},{2,0},{3,1},{4,6},{5,7},{6,4},{7,5},{8,10},{9,11},{10,... | collective-permute-start | bytes 294920 | tf_op jit(solution)/shard_map/ppermute | solution.py:528
  698.5 117.1 %collective-permute-start.41 = (bf16[2,256,2048]{2,1,0:T(8,128)(2,1)}, bf16[2,256,2048]{2,1,0:T(8,128)(2,1)}, u32[]{:S(2)}, u32[]{:S(2)}) collective-permute-start(bf16[2,256,2048]{2,1,0:T(8,128)(2,1)} %pad_maximum_fusion.2), channel_id=1, source_target_pairs={{0,2},{1,3},{2,0},{3,1},{4,6},{5,7},{6,4},{7,5},{8,10},{9,11},{10,... | collective-permute-start | bytes 6291464 | tf_op jit(solution)/shard_map/ppermute | solution.py:528
  702.0 20.6 %collective-permute-start.46 = (bf16[2,1,256,1024]{3,2,0,1:T(8,128)(2,1)}, bf16[2,1,256,1024]{3,2,0,1:T(8,128)(2,1)}, u32[]{:S(2)}, u32[]{:S(2)}) collective-permute-start(bf16[2,1,256,1024]{3,2,0,1:T(8,128)(2,1)} %slice.190), channel_id=1, source_target_pairs={{0,16},{1,17},{2,18},{3,19},{4,20},{5,21},{6,22},{7,23},{8,24},{9,... | collective-permute-start | bytes 3145736 | tf_op jit(solution)/shard_map/ppermute | solution.py:528
  705.8 20.6 %collective-permute-start.47 = (bf16[2,1,256,1024]{3,2,1,0:T(8,128)(2,1)}, bf16[2,1,256,1024]{3,2,1,0:T(8,128)(2,1)}, u32[]{:S(2)}, u32[]{:S(2)}) collective-permute-start(bf16[2,1,256,1024]{3,2,1,0:T(8,128)(2,1)} %slice.192), channel_id=1, source_target_pairs={{0,8},{1,9},{2,10},{3,11},{4,12},{5,13},{6,14},{7,15},{8,0},{9,1},... | collective-permute-start | bytes 3145736 | tf_op jit(solution)/shard_map/ppermute | solution.py:528
  722.6 96.7 %collective-permute-start.45 = (bf16[544,512]{1,0:T(8,128)(2,1)}, bf16[544,512]{1,0:T(8,128)(2,1)}, u32[]{:S(2)}, u32[]{:S(2)}) collective-permute-start(bf16[544,512]{1,0:T(8,128)(2,1)} %pad_maximum_fusion.6), channel_id=1, source_target_pairs={{0,1},{1,2},{2,3},{3,0},{4,5},{5,6},{6,7},{7,4},{8,9},{9,10},{10,1... | collective-permute-start | bytes 1671176 | tf_op jit(solution)/shard_map/ppermute | solution.py:528
  726.4 101.2 %collective-permute-start.48 = (bf16[544,512]{1,0:T(8,128)(2,1)}, bf16[544,512]{1,0:T(8,128)(2,1)}, u32[]{:S(2)}, u32[]{:S(2)}) collective-permute-start(bf16[544,512]{1,0:T(8,128)(2,1)} %pad_maximum_fusion.7), channel_id=1, source_target_pairs={{0,2},{1,3},{2,0},{3,1},{4,6},{5,7},{6,4},{7,5},{8,10},{9,11},{10,... | collective-permute-start | bytes 1671176 | tf_op jit(solution)/shard_map/ppermute | solution.py:528
  739.0 76.7 %copy-start.35 = (bf16[544,512]{1,0:T(8,128)(2,1)S(1)}, bf16[544,512]{1,0:T(8,128)(2,1)}, u32[]{:S(2)}) copy-start(bf16[544,512]{1,0:T(8,128)(2,1)} %pad_maximum_fusion.8) | copy-start | bytes 1671172
  815.6 22.7 %collective-permute-start.49 = (bf16[544,512]{1,0:T(8,128)(2,1)S(1)}, bf16[544,512]{1,0:T(8,128)(2,1)S(1)}, u32[]{:S(2)}, u32[]{:S(2)}) collective-permute-start(bf16[544,512]{1,0:T(8,128)(2,1)S(1)} %copy-done.35), channel_id=1, source_target_pairs={{0,3},{1,0},{2,1},{3,2},{4,7},{5,4},{6,5},{7,6},{8,11},{9,8},{10,9... | collective-permute-start | bytes 1671176 | tf_op jit(solution)/shard_map/ppermute | solution.py:528
  819.4 26.4 %collective-permute-start.52 = (f32[24576]{0:T(1024)}, f32[24576]{0:T(1024)S(1)}, u32[]{:S(2)}, u32[]{:S(2)}) collective-permute-start(f32[24576]{0:T(1024)} %add.483), channel_id=1, source_target_pairs={{0,3},{1,0},{2,1},{3,2},{4,7},{5,4},{6,5},{7,6},{8,11},{9,8},{10,9... | collective-permute-start | bytes 294920 | tf_op jit(solution)/shard_map/ppermute | solution.py:528
  (55 other events, 440.8 us)
Sparse Core Ops, SparseCore 0:
  27.8 28.4 all-gather.8
  61.4 54.2 all-gather.20
  118.2 53.8 all-gather.10
  175.8 66.8 all-gather.12
  262.1 53.7 all-gather.14
  391.1 151.7 all-gather.16
  544.5 152.3 all-gather.18

commit v4 on v3

--- a/solution.py
+++ b/solution.py
@@ -790,12 +790,6 @@
     out_g.stage()
     qkv_g.stage()
     ffn[0].stage()
-    output = seq_out(copied(arrive(output)))
-    grad_tokens = seq_out(copied(arrive(grad_tokens)))
-    far_up, far_down = 0.0, 0.0
-    for got in far:
-        got = arrive(got).astype(F32)
-        far_up, far_down = seq_out([far_up + got[0], far_down + got[1]])
     g_out = out_g.finish()[0]
     g_qkv = qkv_g.finish()[0]
     f0 = ffn[0].finish()
@@ -810,8 +804,15 @@
 
     mine = share(ti)
     shares = [tp_shift(jnp.concatenate(share(tp_at(s)), axis=0), s) for s in range(1, n)]
-    g_upw = seq_out(f0[0].astype(F32) + far_up)
-    g_downw = seq_out((f0[1].astype(F32) + far_down).T).T
+    output = seq_out(copied(arrive(output)))
+    grad_tokens = seq_out(copied(arrive(grad_tokens)))
+    g_upw, g_downw = f0[0].astype(F32), f0[1].astype(F32)
+    for got in far:
+        got = arrive(got).astype(F32)
+        g_upw = g_upw + got[0]
+        g_downw = g_downw + got[1]
+    g_upw = seq_out(g_upw)
+    g_downw = seq_out(g_downw.T).T
     g_outw, g_qw, g_kvw = [x.astype(F32) for x in mine]
     for got in shares:
         got = arrive(got).astype(F32)

time: 868 us -> 865 us (level)
    all_gather x1, waiting for transfers between devices: 0.01 us -> 44.7 us  [per_device(): grad_tokens = lax.all_gather(gt, 'tp', axis=0, tiled=True)]
    ppermute x53, waiting for transfers between devices: 300 us -> 259 us  [perm(): return lax.ppermute(x, ('dp', 'tp'), pairs)]
    convert_element_type x15 -> x16, other arithmetic: 18.2 us -> 21.8 us  [stage(): x = seq_out((keep.astype(F32) + arrive(got).astype(F32)).astype(BF16))]
  transfers between devices with their start and end apart: 60 -> 60, of which waited for: 17 -> 20; matrix products, arithmetic and copies ran while one was open for 17% -> 17% of each run, Pallas kernels for 37% -> 37%
where the time goes in v4:
time: 865 us; the launch traced here: 855 us
  Pallas kernels  315 us (36%)
  waiting for transfers between devices  304 us (35%)
  local copies, waits for them, and re-layouts  71 us (8%)
  starting transfers between devices  60.1 us (7%)
  other arithmetic  48 us (6%)
  matrix products  41.8 us (5%)
  between operations  15.6 us (2%)
    ppermute x53, waiting for transfers between devices, perm(): return lax.ppermute(x, ('dp', 'tp'), pairs)  259 us
    pallas_call x4, Pallas kernels, grad_call(): call(functools.partial(grad_kernel, count, pairs, places), (pairs, places...  79.6 us
    ppermute x53, starting transfers between devices, perm(): return lax.ppermute(x, ('dp', 'tp'), pairs)  59.5 us
    pallas_call x4, Pallas kernels, ffn_up(): call(functools.partial(up_kernel, ready), (u // bn,), [whole((r, d)), pl....  56.7 us
    pallas_call x4, Pallas kernels, product(): call(functools.partial(product_kernel, len(xs), nt), (n // bn,), [plane(x...  56.4 us
    all_gather x1, waiting for transfers between devices, per_device(): grad_tokens = lax.all_gather(gt, 'tp', axis=0, tiled=True)  44.7 us
    pallas_call x2, Pallas kernels, attn_bwd(): call(functools.partial(attn_bwd_kernel, hd ** (-0.5), qb, reach), (heads,...  37.3 us
    convert_element_type x16, other arithmetic, stage(): x = seq_out((keep.astype(F32) + arrive(got).astype(F32)).astype(BF16))  21.8 us
  transfers between devices with their start and end apart: 60, of which 20 were waited for; matrix products, arithmetic and copies ran while one was open for 17% of the time, Pallas kernels for 37%

profile of v4, /device:TPU:0, one launch (start us, length us, event | category | flops | bytes accessed | tf_op | source)
XLA Modules:
  0.0 855.1 jit_solution(4017417539748800787)
XLA Ops:
  9.5 4.1 collective-permute-start.3
  16.2 6.3 norm1.1
  22.5 4.4 fusion.34
  40.4 5.6 add_convert_fusion.15.q_ref
  46.9 10.4 %attn_fwd.2 = bf16[1024,512]{1,0:T(8,128)(2,1)} custom-call(bf16[1024,512]{1,0:T(8,128)(2,1)} %add_convert_fusion.15.q_ref, bf16[1024,128]{1,0:T(8,128)(2,1)} %copy.49.k_ref, bf16[128,1024]{1,0:T(8,128)(2,1)} %copy.50.vt_ref, s32[1024,1]{1,0:T(8,128)} %copy.51.dcol_ref, s32[1,1,1024]{2,1,0:T(1,128)} %get-tuple-element.333.drow_ref), custom_call_target="tpu_custom_call" | custom-call | flops 1342177280 | bytes 2621440 | tf_op jit(solution)/shard_map/attn_fwd/pallas_call | solution.py:116
  61.3 2.8 constant_dynamic-slice_fusion.3
  68.2 6.8 add_convert_fusion.14.q_ref
  75.0 10.4 %attn_fwd.3 = bf16[1024,512]{1,0:T(8,128)(2,1)} custom-call(bf16[1024,512]{1,0:T(8,128)(2,1)} %add_convert_fusion.14.q_ref, bf16[1024,128]{1,0:T(8,128)(2,1)} %copy.49.k_ref, bf16[128,1024]{1,0:T(8,128)(2,1)} %copy.50.vt_ref, s32[1024,1]{1,0:T(8,128)} %copy.51.dcol_ref, s32[1,1,1024]{2,1,0:T(1,128)} %get-tuple-element.333.drow_ref), custom_call_target="tpu_custom_call" | custom-call | flops 1342177280 | bytes 2621440 | tf_op jit(solution)/shard_map/attn_fwd/pallas_call | solution.py:116
  85.4 30.4 %collective-permute-done.8 = bf16[272,2048]{1,0:T(8,128)(2,1)} collective-permute-done((bf16[272,2048]{1,0:T(8,128)(2,1)}, bf16[272,2048]{1,0:T(8,128)(2,1)}, u32[]{:S(2)}, u32[]{:S(2)}) %collective-permute-start.8) | collective-permute-done | bytes 1114144 | tf_op jit(solution)/shard_map/ppermute | solution.py:528
  115.8 2.3 slice.131
  119.3 3.2 constant_dynamic-slice_fusion.6.x_ref
  124.3 3.1 constant_dynamic-slice_fusion.8
  127.5 2.5 collective-permute-start.9
  132.3 2.4 collective-permute-done.4
  135.6 9.3 %convolution_convert_fusion.1.refs_0_ = bf16[512,2048]{1,0:T(8,128)(2,1)} fusion(bf16[512,2048]{1,0:T(8,128)(2,1)S(1)} %get-tuple-element.189.refs_0_.refs_3_.refs_4_, bf16[2048,2048]{1,0:T(8,128)(2,1)} %refs_2_.7), kind=kOutput, calls=%fused_computation.7 | convolution fusion | flops 4296015872 | bytes 12582912 | tf_op jit(solution)/shard_map/dot_general | solution.py:609
  145.0 5.8 convolution_convert_fusion.refs_0_
  151.7 12.0 %collective-permute-done.5 = bf16[512,512]{1,0:T(8,128)(2,1)S(1)} collective-permute-done((bf16[512,512]{1,0:T(8,128)(2,1)S(1)}, bf16[512,512]{1,0:T(8,128)(2,1)S(1)}, u32[]{:S(2)}, u32[]{:S(2)}) %collective-permute-start.5) | collective-permute-done | bytes 524320 | tf_op jit(solution)/shard_map/ppermute | solution.py:528
  164.5 11.2 %proj_ln.1 = (f32[512,2048]{1,0:T(8,128)}, bf16[512,2048]{1,0:T(8,128)(2,1)}) custom-call(bf16[512,2048]{1,0:T(8,128)(2,1)} %constant_dynamic-update-slice_fusion.4.att_ref, bf16[8,2048,256]{2,1,0:T(8,128)(2,1)} %bitcast.83, bf16[512,2048]{1,0:T(8,128)(2,1)} %constant_dynamic-slice_fusion.6.x_ref, bf16[1,2048]{1,0:T(2,128)(2,1)} %reshape.124.ob_ref, ...), custom_call_target="tpu_custom_call" | custom-call | flops 4294967296 | bytes 18874368 | tf_op jit(solution)/shard_map/proj_ln/pallas_call | solution.py:151
  175.8 2.5 collective-permute-start.6
  180.2 11.5 %ffn_up.4 = (bf16[2,512,2048]{2,1,0:T(8,128)(2,1)}, f32[1,2048]{1,0:T(1,128)}) custom-call(bf16[512,2048]{1,0:T(8,128)(2,1)} %get-tuple-element.221.n_ref.refs_0_, bf16[2048,2048]{1,0:T(8,128)(2,1)} %refs_2_.5, bf16[1,2048]{1,0:T(2,128)(2,1)} %reshape.128.b_ref, bf16[512,2048]{1,0:T(8,128)(2,1)} %convolution_convert_fusion.1.refs_0_), custom_call_target="tpu_custom_call" | custom-call | flops 4294967296 | bytes 16777216 | tf_op jit(solution)/shard_map/ffn_up/pallas_call | solution.py:195
  191.8 31.4 %collective-permute-done.6.n_ref.refs_1_ = bf16[512,2048]{1,0:T(8,128)(2,1)S(1)} collective-permute-done((bf16[512,2048]{1,0:T(8,128)(2,1)}, bf16[512,2048]{1,0:T(8,128)(2,1)S(1)}, u32[]{:S(2)}, u32[]{:S(2)}) %collective-permute-start.6) | collective-permute-done | bytes 2097184 | tf_op jit(solution)/shard_map/ppermute | solution.py:528
  223.2 6.3 collective-permute-start.11
  232.4 11.5 %ffn_up.5 = (bf16[2,512,2048]{2,1,0:T(8,128)(2,1)}, f32[1,2048]{1,0:T(1,128)}) custom-call(bf16[512,2048]{1,0:T(8,128)(2,1)} %copy-done.47, bf16[2048,2048]{1,0:T(8,128)(2,1)} %refs_2_.5, bf16[1,2048]{1,0:T(2,128)(2,1)} %reshape.128.b_ref, bf16[512,2048]{1,0:T(8,128)(2,1)} %convolution_convert_fusion.refs_0_), custom_call_target="tpu_custom_call" | custom-call | flops 4294967296 | bytes 16777216 | tf_op jit(solution)/shard_map/ffn_up/pallas_call | solution.py:195
  244.1 16.5 %ffn_up.6 = (bf16[2,512,2048]{2,1,0:T(8,128)(2,1)}, f32[1,2048]{1,0:T(1,128)}) custom-call(bf16[512,2048]{1,0:T(8,128)(2,1)} %copy-done.47, bf16[2048,2048]{1,0:T(8,128)(2,1)} %all-gather.11.cloned.1.call-done.w_ref.refs_3_, bf16[1,2048]{1,0:T(2,128)(2,1)} %slice.172.b_ref, bf16[512,2048]{1,0:T(8,128)(2,1)} %copy-done.15, ...), custom_call_target="tpu_custom_call" | custom-call | flops 8589934592 | bytes 16777216 | tf_op jit(solution)/shard_map/ffn_up/pallas_call | solution.py:195
  263.6 3.2 constant_dynamic-slice_fusion.5.refs_0_
  266.8 14.7 %product.4 = bf16[512,2048]{1,0:T(8,128)(2,1)} custom-call(bf16[2,512,2048]{2,1,0:T(8,128)(2,1)} %get-tuple-element.223.refs_0_.refs_9_.refs_13_, bf16[2,512,2048]{2,1,0:T(8,128)(2,1)} %get-tuple-element.192.refs_1_.refs_9_.refs_13_, bf16[2048,2048]{1,0:T(8,128)(2,1)} %refs_2_.5, bf16[2048,2048]{1,0:T(8,128)(2,1)} %all-gather.11.cloned.1.call-done.w_ref.refs_3_), custom_call_target="tpu_custom_call" | custom-call | flops 8589934592 | bytes 23068672 | tf_op jit(solution)/shard_map/product/pallas_call | solution.py:225
  281.7 17.1 %ffn_up.7 = (bf16[2,512,2048]{2,1,0:T(8,128)(2,1)}, f32[1,2048]{1,0:T(1,128)}) custom-call(bf16[512,2048]{1,0:T(8,128)(2,1)} %get-tuple-element.221.n_ref.refs_0_, bf16[2048,2048]{1,0:T(8,128)(2,1)} %all-gather.11.cloned.1.call-done.w_ref.refs_3_, bf16[1,2048]{1,0:T(2,128)(2,1)} %slice.172.b_ref, bf16[512,2048]{1,0:T(8,128)(2,1)} %copy-done.3, ...), custom_call_target="tpu_custom_call" | custom-call | flops 8589934592 | bytes 16777216 | tf_op jit(solution)/shard_map/ffn_up/pallas_call | solution.py:195
  298.8 14.0 %product.5.refs_0_ = bf16[512,2048]{1,0:T(8,128)(2,1)} custom-call(bf16[2,512,2048]{2,1,0:T(8,128)(2,1)} %get-tuple-element.222.refs_0_.refs_8_.refs_12_, bf16[2,512,2048]{2,1,0:T(8,128)(2,1)} %get-tuple-element.191.refs_1_.refs_8_.refs_12_, bf16[2048,2048]{1,0:T(8,128)(2,1)} %refs_2_.5, bf16[2048,2048]{1,0:T(8,128)(2,1)} %all-gather.11.cloned.1.call-done.w_ref.refs_3_), custom_call_target="tpu_custom_call" | custom-call | flops 8589934592 | bytes 23068672 | tf_op jit(solution)/shard_map/product/pallas_call | solution.py:225
  312.7 14.0 %product.6 = bf16[512,2048]{1,0:T(8,128)(2,1)} custom-call(bf16[2,512,2048]{2,1,0:T(8,128)(2,1)} %get-tuple-element.223.refs_0_.refs_9_.refs_13_, bf16[2,512,2048]{2,1,0:T(8,128)(2,1)} %get-tuple-element.192.refs_1_.refs_9_.refs_13_, bf16[2048,2048]{1,0:T(8,128)(2,1)} %refs_2_.7, bf16[2048,2048]{1,0:T(8,128)(2,1)} %all-gather.13.cloned.1.call-done.refs_1_.refs_3_), custom_call_target="tpu_custom_call" | custom-call | flops 8589934592 | bytes 23068672 | tf_op jit(solution)/shard_map/product/pallas_call | solution.py:225
  328.6 13.8 %product.7 = bf16[512,2048]{1,0:T(8,128)(2,1)} custom-call(bf16[2,512,2048]{2,1,0:T(8,128)(2,1)} %get-tuple-element.222.refs_0_.refs_8_.refs_12_, bf16[2,512,2048]{2,1,0:T(8,128)(2,1)} %get-tuple-element.191.refs_1_.refs_8_.refs_12_, bf16[2048,2048]{1,0:T(8,128)(2,1)} %refs_2_.7, bf16[2048,2048]{1,0:T(8,128)(2,1)} %all-gather.13.cloned.1.call-done.refs_1_.refs_3_), custom_call_target="tpu_custom_call" | custom-call | flops 8589934592 | bytes 23068672 | tf_op jit(solution)/shard_map/product/pallas_call | solution.py:225
  343.8 14.7 %norm2_back.1 = (f32[512,2048]{1,0:T(8,128)}, bf16[512,2048]{1,0:T(8,128)(2,1)}, bf16[512,2048]{1,0:T(8,128)(2,1)}, f32[8,2048]{1,0:T(8,128)}) custom-call(bf16[512,2048]{1,0:T(8,128)(2,1)} %product.5.refs_0_, bf16[512,2048]{1,0:T(8,128)(2,1)} %copy-done.20, f32[512,2048]{1,0:T(8,128)} %get-tuple-element.183.refs_2_, bf16[512,2048]{1,0:T(8,128)(2,1)} %copy-done.3, ...), custom_call_target="tpu_custom_call" | custom-call | flops 4294967296 | bytes 29360128 | tf_op jit(solution)/shard_map/norm2_back/pallas_call | solution.py:275
  358.4 9.9 %add_convert_fusion.5.q_ref = bf16[512,2048]{1,0:T(8,128)(2,1)} fusion(bf16[512,2048]{1,0:T(8,128)(2,1)} %constant_dynamic-slice_fusion.5.refs_0_, bf16[2048,2048]{1,0:T(8,128)(2,1)} %all-gather.15.cloned.1.call-done.wq_ref, f32[2048]{0:T(1024)S(1)} %bitcast.101), kind=kOutput, calls=%fused_computation.5 | convolution fusion | flops 4297064448 | bytes 12591104 | tf_op jit(solution)/shard_map/dot_general | solution.py:722
  368.4 18.6 %attn_bwd.2 = (bf16[512,1024]{1,0:T(8,128)(2,1)}, f32[1024,128]{1,0:T(8,128)}, f32[1024,128]{1,0:T(8,128)}) custom-call(s32[1]{0:T(128)} %bitcast.6.row0_ref, bf16[512,2048]{1,0:T(8,128)(2,1)} %add_convert_fusion.5.q_ref, bf16[512,2048]{1,0:T(8,128)(2,1)} %get-tuple-element.181.go_ref, bf16[1024,128]{1,0:T(8,128)(2,1)} %copy.49.k_ref, ...), custom_call_target="tpu_custom_call" | custom-call | flops 4026531840 | bytes 5242880 | tf_op jit(solution)/shard_map/attn_bwd/pallas_call | solution.py:334
  387.0 4.1 add_convert_fusion.4
  393.7 6.1 collective-permute-done.16.refs_6_
  402.2 18.7 %attn_bwd.3 = (bf16[512,1024]{1,0:T(8,128)(2,1)}, f32[1024,128]{1,0:T(8,128)}, f32[1024,128]{1,0:T(8,128)}) custom-call(s32[1]{0:T(128)} %bitcast.6.row0_ref, bf16[512,2048]{1,0:T(8,128)(2,1)} %add_convert_fusion.5.q_ref, bf16[512,2048]{1,0:T(8,128)(2,1)} %get-tuple-element.181.go_ref, bf16[1024,128]{1,0:T(8,128)(2,1)} %copy.49.k_ref, ...), custom_call_target="tpu_custom_call" | custom-call | flops 4026531840 | bytes 5242880 | tf_op jit(solution)/shard_map/attn_bwd/pallas_call | solution.py:334
  426.0 29.6 %weight_grad.4 = (bf16[2,2,256,1024]{3,2,1,0:T(8,128)(2,1)}, bf16[2,2,256,1024]{3,2,1,0:T(8,128)(2,1)}, bf16[2,2,256,1024]{3,2,1,0:T(8,128)(2,1)}, bf16[2,2,256,1024]{3,2,1,0:T(8,128)(2,1)}) custom-call(s32[1]{0:T(128)} %bitcast.9.m_ref, bf16[512,2048]{1,0:T(8,128)(2,1)} %get-tuple-element.221.n_ref.refs_0_, bf16[512,2048]{1,0:T(8,128)(2,1)} %copy-done.47, ...), custom_call_target="tpu_custom_call" | custom-call | flops 17179869184 | bytes 33554432 | tf_op jit(solution)/shard_map/weight_grad/pallas_call | solution.py:467
  456.2 3.1 copy.62
  461.5 14.1 %norm1_back.1 = (bf16[512,2048]{1,0:T(8,128)(2,1)}, f32[8,2048]{1,0:T(8,128)}, f32[8,256]{1,0:T(8,128)}) custom-call(bf16[512,2048]{1,0:T(8,128)(2,1)} %pad_maximum_fusion.1.gq_ref, bf16[512,256]{1,0:T(8,128)(2,1)} %fusion.8.gkv_ref, bf16[2048,2048]{1,0:T(8,128)(2,1)} %all-gather.15.cloned.1.call-done.wq_ref, bf16[2048,256]{1,0:T(8,128)(2,1)} %wkv_ref.1, ...), custom_call_target="tpu_custom_call" | custom-call | flops 4831838208 | bytes 22020096 | tf_op jit(solution)/shard_map/norm1_back/pallas_call | solution.py:376
  476.5 3.1 copy.60
  483.3 9.8 %weight_grad.5 = (bf16[1,2,256,1024]{3,2,1,0:T(8,128)(2,1)}, bf16[1,2,256,1024]{3,2,1,0:T(8,128)(2,1)}, bf16[1,2,256,1024]{3,2,1,0:T(8,128)(2,1)}, bf16[1,2,256,1024]{3,2,1,0:T(8,128)(2,1)}) custom-call(s32[1]{0:T(128)} %bitcast.9.m_ref, bf16[512,2048]{1,0:T(8,128)(2,1)} %get-tuple-element.215.refs_0_, bf16[512,2048]{1,0:T(8,128)(2,1)} %collective-permute-done.24.refs_1_, ...), custom_call_target="tpu_custom_call" | custom-call | flops 4294967296 | bytes 10485760 | tf_op jit(solution)/shard_map/weight_grad/pallas_call | solution.py:467
  493.6 13.2 %collective-permute-done.21 = bf16[2,2,256,1024]{3,2,0,1:T(8,128)(2,1)} collective-permute-done((bf16[2,2,256,1024]{3,2,0,1:T(8,128)(2,1)}, bf16[2,2,256,1024]{3,2,0,1:T(8,128)(2,1)}, u32[]{:S(2)}, u32[]{:S(2)}) %collective-permute-start.21) | collective-permute-done | bytes 2097184 | tf_op jit(solution)/shard_map/ppermute | solution.py:528
  506.8 2.7 add_convert_fusion.3
  509.6 18.0 %collective-permute-done.20 = bf16[2,2,256,1024]{3,2,0,1:T(8,128)(2,1)} collective-permute-done((bf16[2,2,256,1024]{3,2,0,1:T(8,128)(2,1)}, bf16[2,2,256,1024]{3,2,0,1:T(8,128)(2,1)}, u32[]{:S(2)}, u32[]{:S(2)}) %collective-permute-start.20) | collective-permute-done | bytes 2097184 | tf_op jit(solution)/shard_map/ppermute | solution.py:528
  528.2 2.5 add_convert_fusion.2
  534.8 29.5 %weight_grad.6 = (bf16[2,2,256,1024]{3,2,1,0:T(8,128)(2,1)}, bf16[2,2,256,1024]{3,2,1,0:T(8,128)(2,1)}, bf16[2,2,256,1024]{3,2,1,0:T(8,128)(2,1)}, bf16[2,2,256,1024]{3,2,1,0:T(8,128)(2,1)}) custom-call(s32[1]{0:T(128)} %bitcast.9.m_ref, bf16[512,2048]{1,0:T(8,128)(2,1)} %get-tuple-element.221.n_ref.refs_0_, bf16[512,2048]{1,0:T(8,128)(2,1)} %copy-done.47, ...), custom_call_target="tpu_custom_call" | custom-call | flops 17179869184 | bytes 33554432 | tf_op jit(solution)/shard_map/weight_grad/pallas_call | solution.py:467
  568.2 10.7 %weight_grad.7 = (bf16[1,2,256,1152]{3,2,1,0:T(8,128)(2,1)}, bf16[1,2,256,1152]{3,2,1,0:T(8,128)(2,1)}, bf16[1,2,256,1152]{3,2,1,0:T(8,128)(2,1)}, bf16[1,2,256,1152]{3,2,1,0:T(8,128)(2,1)}) custom-call(s32[1]{0:T(128)} %bitcast.9.m_ref, bf16[512,2048]{1,0:T(8,128)(2,1)} %constant_dynamic-slice_fusion.5.refs_0_, ...), custom_call_target="tpu_custom_call" | custom-call | flops 4831838208 | bytes 11534336 | tf_op jit(solution)/shard_map/weight_grad/pallas_call | solution.py:467
  587.1 18.4 %collective-permute-done.39 = bf16[1,2,256,1024]{3,2,1,0:T(8,128)(2,1)} collective-permute-done((bf16[1,2,256,1024]{3,2,1,0:T(8,128)(2,1)}, bf16[1,2,256,1024]{3,2,1,0:T(8,128)(2,1)}, u32[]{:S(2)}, u32[]{:S(2)}) %collective-permute-start.39) | collective-permute-done | bytes 1048608 | tf_op jit(solution)/shard_map/ppermute | solution.py:528
  612.4 18.4 %collective-permute-done.37 = bf16[1,2,256,1152]{3,2,1,0:T(8,128)(2,1)} collective-permute-done((bf16[1,2,256,1152]{3,2,1,0:T(8,128)(2,1)}, bf16[1,2,256,1152]{3,2,1,0:T(8,128)(2,1)}, u32[]{:S(2)}, u32[]{:S(2)}) %collective-permute-start.37) | collective-permute-done | bytes 1179680 | tf_op jit(solution)/shard_map/ppermute | solution.py:528
  635.8 36.9 %collective-permute-done.35 = bf16[2,2,256,1024]{3,2,0,1:T(8,128)(2,1)S(1)} collective-permute-done((bf16[2,2,256,1024]{3,2,0,1:T(8,128)(2,1)S(1)}, bf16[2,2,256,1024]{3,2,0,1:T(8,128)(2,1)S(1)}, u32[]{:S(2)}, u32[]{:S(2)}) %collective-permute-start.35) | collective-permute-done | bytes 2097184 | tf_op jit(solution)/shard_map/ppermute | solution.py:528
  678.7 8.8 %collective-permute-done.45 = bf16[1,1,256,1024]{3,2,1,0:T(8,128)(2,1)S(1)} collective-permute-done((bf16[1,1,256,1024]{3,2,1,0:T(8,128)(2,1)S(1)}, bf16[1,1,256,1024]{3,2,1,0:T(8,128)(2,1)S(1)}, u32[]{:S(2)}, u32[]{:S(2)}) %collective-permute-start.45) | collective-permute-done | bytes 524320 | tf_op jit(solution)/shard_map/ppermute | solution.py:528
  693.2 3.5 collective-permute-done.43
  696.8 4.3 collective-permute-done.42
  707.3 11.4 %collective-permute-done.41 = bf16[2,1,256,1024]{3,2,0,1:T(8,128)(2,1)} collective-permute-done((bf16[2,1,256,1024]{3,2,0,1:T(8,128)(2,1)}, bf16[2,1,256,1024]{3,2,0,1:T(8,128)(2,1)}, u32[]{:S(2)}, u32[]{:S(2)}) %collective-permute-start.41) | collective-permute-done | bytes 1048608 | tf_op jit(solution)/shard_map/ppermute | solution.py:528
  720.7 2.6 add_convert_fusion.9
  724.0 2.6 add_convert_fusion.8
  726.6 8.9 %copied.2 = bf16[2048,2048]{1,0:T(8,128)(2,1)} custom-call(bf16[2048,2048]{1,0:T(8,128)(2,1)} %all-gather.17.cloned.1.call-done.x_ref), custom_call_target="tpu_custom_call" | custom-call | bytes 16777216 | tf_op jit(solution)/shard_map/copied/pallas_call | solution.py:488
  735.5 44.7 %all-gather.19.cloned.1.call-done.x_ref = bf16[2048,2048]{1,0:T(8,128)(2,1)} async-done(((bf16[512,2048]{1,0:T(8,128)(2,1)}), bf16[2048,2048]{1,0:T(8,128)(2,1)}) %all-gather.19.cloned.1.call-update) | async-done | bytes 8388624 | tf_op jit(solution)/shard_map/all_gather | solution.py:758
  780.2 8.9 %copied.3 = bf16[2048,2048]{1,0:T(8,128)(2,1)} custom-call(bf16[2048,2048]{1,0:T(8,128)(2,1)} %all-gather.19.cloned.1.call-done.x_ref), custom_call_target="tpu_custom_call" | custom-call | bytes 16777216 | tf_op jit(solution)/shard_map/copied/pallas_call | solution.py:488
  789.2 26.7 %collective-permute-done.47 = bf16[2,256,2048]{2,1,0:T(8,128)(2,1)} collective-permute-done((bf16[2,256,2048]{2,1,0:T(8,128)(2,1)}, bf16[2,256,2048]{2,1,0:T(8,128)(2,1)}, u32[]{:S(2)}, u32[]{:S(2)}) %collective-permute-start.47) | collective-permute-done | bytes 2097184 | tf_op jit(solution)/shard_map/ppermute | solution.py:528
  818.0 2.6 fusion
  822.8 5.1 collective-permute-done.48
  829.0 9.4 %collective-permute-done.49 = bf16[544,512]{1,0:T(8,128)(2,1)S(1)} collective-permute-done((bf16[544,512]{1,0:T(8,128)(2,1)S(1)}, bf16[544,512]{1,0:T(8,128)(2,1)S(1)}, u32[]{:S(2)}, u32[]{:S(2)}) %collective-permute-start.49) | collective-permute-done | bytes 557088 | tf_op jit(solution)/shard_map/ppermute | solution.py:528
  842.3 2.9 copy.66
  (323 shorter events, 125.8 us)
Async XLA Ops:
  7.2 61.0 %all-gather.9.cloned.1.call-start = ((), (), s32[]{:S(2)}) async-start(), calls=%async_computation | async-start | bytes 2359296 | tf_op jit(solution)/shard_map/all_gather | solution.py:604
  9.5 17.4 %collective-permute-start.3 = (bf16[272,512]{1,0:T(8,128)(2,1)S(1)}, bf16[272,512]{1,0:T(8,128)(2,1)S(1)}, u32[]{:S(2)}, u32[]{:S(2)}) collective-permute-start(bf16[272,512]{1,0:T(8,128)(2,1)S(1)} %pad_maximum_fusion.9), channel_id=1, source_target_pairs={{0,2},{1,3},{2,0},{3,1},{4,6},{5,7},{6,4},{7,5},{8,10},{9,11},{10,... | collective-permute-start | bytes 835592 | tf_op jit(solution)/shard_map/ppermute | solution.py:528
  27.6 136.8 %all-gather.21.cloned.1.call-start = ((), (), s32[]{:S(2)}) async-start(), calls=%async_computation.6 | async-start | bytes 9437184 | tf_op jit(solution)/shard_map/all_gather | solution.py:621
  29.5 27.8 %collective-permute-start = (bf16[512,256]{1,0:T(8,128)(2,1)}, bf16[512,256]{1,0:T(8,128)(2,1)}, u32[]{:S(2)}, u32[]{:S(2)}) collective-permute-start(bf16[512,256]{1,0:T(8,128)(2,1)} %get-tuple-element.303), channel_id=1, source_target_pairs={{0,1},{1,2},{2,3},{3,0},{4,5},{5,6},{6,7},{7,4},{8,9},{9,10},{10,1... | collective-permute-start | bytes 786440 | tf_op jit(solution)/shard_map/ppermute | solution.py:528
  31.1 26.3 %collective-permute-start.1 = (bf16[512,256]{1,0:T(8,128)(2,1)}, bf16[512,256]{1,0:T(8,128)(2,1)}, u32[]{:S(2)}, u32[]{:S(2)}) collective-permute-start(bf16[512,256]{1,0:T(8,128)(2,1)} %get-tuple-element.303), channel_id=1, source_target_pairs={{0,2},{1,3},{2,0},{3,1},{4,6},{5,7},{6,4},{7,5},{8,10},{9,11},{10,... | collective-permute-start | bytes 786440 | tf_op jit(solution)/shard_map/ppermute | solution.py:528
  33.0 24.4 %collective-permute-start.2 = (bf16[512,256]{1,0:T(8,128)(2,1)}, bf16[512,256]{1,0:T(8,128)(2,1)}, u32[]{:S(2)}, u32[]{:S(2)}) collective-permute-start(bf16[512,256]{1,0:T(8,128)(2,1)} %get-tuple-element.303), channel_id=1, source_target_pairs={{0,3},{1,0},{2,1},{3,2},{4,7},{5,4},{6,5},{7,6},{8,11},{9,8},{10,9... | collective-permute-start | bytes 786440 | tf_op jit(solution)/shard_map/ppermute | solution.py:528
  61.3 182.8 %all-gather.11.cloned.1.call-start = ((), (), s32[]{:S(2)}) async-start(), calls=%async_computation.1 | async-start | bytes 9437184 | tf_op jit(solution)/shard_map/all_gather | solution.py:626
  65.3 50.6 %collective-permute-start.8 = (bf16[272,2048]{1,0:T(8,128)(2,1)}, bf16[272,2048]{1,0:T(8,128)(2,1)}, u32[]{:S(2)}, u32[]{:S(2)}) collective-permute-start(bf16[272,2048]{1,0:T(8,128)(2,1)} %pad_maximum_fusion.4), channel_id=1, source_target_pairs={{0,2},{1,3},{2,0},{3,1},{4,6},{5,7},{6,4},{7,5},{8,10},{9,11},{10,... | collective-permute-start | bytes 3342344 | tf_op jit(solution)/shard_map/ppermute | solution.py:528
  85.4 33.0 %copy-start.30 = (bf16[1024,512]{1,0:T(8,128)(2,1)S(1)}, bf16[1024,512]{1,0:T(8,128)(2,1)}, u32[]{:S(2)}) copy-start(bf16[1024,512]{1,0:T(8,128)(2,1)} %attn_fwd.2) | copy-start | bytes 3145732
  118.2 125.9 %all-gather.13.cloned.1.call-start = ((), (), s32[]{:S(2)}) async-start(), calls=%async_computation.2 | async-start | bytes 9437184 | tf_op jit(solution)/shard_map/all_gather | solution.py:639
  119.3 15.4 %collective-permute-start.4 = (bf16[512,512]{1,0:T(8,128)(2,1)}, bf16[512,512]{1,0:T(8,128)(2,1)S(1)}, u32[]{:S(2)}, u32[]{:S(2)}) collective-permute-start(bf16[512,512]{1,0:T(8,128)(2,1)} %get-tuple-element.320), channel_id=1, source_target_pairs={{0,1},{1,0},{2,3},{3,2},{4,5},{5,4},{6,7},{7,6},{8,9},{9,8},{10,11... | collective-permute-start | bytes 1572872 | tf_op jit(solution)/shard_map/ppermute | solution.py:528
  127.5 48.3 %collective-permute-start.9 = (bf16[256,2048]{1,0:T(8,128)(2,1)}, bf16[256,2048]{1,0:T(8,128)(2,1)}, u32[]{:S(2)}, u32[]{:S(2)}) collective-permute-start(bf16[256,2048]{1,0:T(8,128)(2,1)} %get-tuple-element.165), channel_id=1, source_target_pairs={{0,2},{1,3},{2,0},{3,1},{4,6},{5,7},{6,4},{7,5},{8,10},{9,11},{10,... | collective-permute-start | bytes 3145736 | tf_op jit(solution)/shard_map/ppermute | solution.py:528
  144.9 18.7 %collective-permute-start.5 = (bf16[512,512]{1,0:T(8,128)(2,1)S(1)}, bf16[512,512]{1,0:T(8,128)(2,1)S(1)}, u32[]{:S(2)}, u32[]{:S(2)}) collective-permute-start(bf16[512,512]{1,0:T(8,128)(2,1)S(1)} %get-tuple-element.318), channel_id=1, source_target_pairs={{0,1},{1,0},{2,3},{3,2},{4,5},{5,4},{6,7},{7,6},{8,9},{9,8},{10,11... | collective-permute-start | bytes 1572872 | tf_op jit(solution)/shard_map/ppermute | solution.py:528
  175.8 182.7 %all-gather.15.cloned.1.call-start = ((), (), s32[]{:S(2)}) async-start(), calls=%async_computation.3 | async-start | bytes 9437184 | tf_op jit(solution)/shard_map/all_gather | solution.py:704
  175.8 47.4 %collective-permute-start.6 = (bf16[512,2048]{1,0:T(8,128)(2,1)}, bf16[512,2048]{1,0:T(8,128)(2,1)S(1)}, u32[]{:S(2)}, u32[]{:S(2)}) collective-permute-start(bf16[512,2048]{1,0:T(8,128)(2,1)} %get-tuple-element.221.n_ref.refs_0_), channel_id=1, source_target_pairs={{0,1},{1,0},{2,3},{3,2},{4,5},{5,4},{6,7},{7,6},{8,9},{9,8},{10,11... | collective-permute-start | bytes 6291464 | tf_op jit(solution)/shard_map/ppermute | solution.py:528
  223.2 37.5 %collective-permute-start.11 = (bf16[272,512]{1,0:T(8,128)(2,1)S(1)}, bf16[272,512]{1,0:T(8,128)(2,1)S(1)}, u32[]{:S(2)}, u32[]{:S(2)}) collective-permute-start(bf16[272,512]{1,0:T(8,128)(2,1)S(1)} %pad_maximum_fusion.9), channel_id=1, source_target_pairs={{0,3},{1,0},{2,1},{3,2},{4,7},{5,4},{6,5},{7,6},{8,11},{9,8},{10,9... | collective-permute-start | bytes 835592 | tf_op jit(solution)/shard_map/ppermute | solution.py:528
  229.5 31.2 %collective-permute-start.10 = (bf16[272,512]{1,0:T(8,128)(2,1)S(1)}, bf16[272,512]{1,0:T(8,128)(2,1)S(1)}, u32[]{:S(2)}, u32[]{:S(2)}) collective-permute-start(bf16[272,512]{1,0:T(8,128)(2,1)S(1)} %pad_maximum_fusion.9), channel_id=1, source_target_pairs={{0,2},{1,3},{2,0},{3,1},{4,6},{5,7},{6,4},{7,5},{8,10},{9,11},{10,... | collective-permute-start | bytes 835592 | tf_op jit(solution)/shard_map/ppermute | solution.py:528
  230.4 30.3 %collective-permute-start.7 = (bf16[272,512]{1,0:T(8,128)(2,1)S(1)}, bf16[272,512]{1,0:T(8,128)(2,1)S(1)}, u32[]{:S(2)}, u32[]{:S(2)}) collective-permute-start(bf16[272,512]{1,0:T(8,128)(2,1)S(1)} %pad_maximum_fusion.9), channel_id=1, source_target_pairs={{0,1},{1,2},{2,3},{3,0},{4,5},{5,6},{6,7},{7,4},{8,9},{9,10},{10,1... | collective-permute-start | bytes 835592 | tf_op jit(solution)/shard_map/ppermute | solution.py:528
  261.9 464.6 %all-gather.17.cloned.1.call-start = ((), (), s32[]{:S(2)}) async-start(), calls=%async_computation.4 | async-start | bytes 10485760 | tf_op jit(solution)/shard_map/all_gather | solution.py:743
  281.5 60.9 %collective-permute-start.12 = (bf16[512,2048]{1,0:T(8,128)(2,1)}, bf16[512,2048]{1,0:T(8,128)(2,1)S(1)}, u32[]{:S(2)}, u32[]{:S(2)}) collective-permute-start(bf16[512,2048]{1,0:T(8,128)(2,1)} %product.4), channel_id=1, source_target_pairs={{0,1},{1,0},{2,3},{3,2},{4,5},{5,4},{6,7},{7,6},{8,9},{9,8},{10,11... | collective-permute-start | bytes 6291464 | tf_op jit(solution)/shard_map/ppermute | solution.py:528
  326.7 60.3 %collective-permute-start.13 = (bf16[512,2048]{1,0:T(8,128)(2,1)}, bf16[512,2048]{1,0:T(8,128)(2,1)}, u32[]{:S(2)}, u32[]{:S(2)}) collective-permute-start(bf16[512,2048]{1,0:T(8,128)(2,1)} %product.6), channel_id=1, source_target_pairs={{0,1},{1,0},{2,3},{3,2},{4,5},{5,4},{6,7},{7,6},{8,9},{9,8},{10,11... | collective-permute-start | bytes 6291464 | tf_op jit(solution)/shard_map/ppermute | solution.py:528
  391.1 389.1 %all-gather.19.cloned.1.call-start = ((), (), s32[]{:S(2)}) async-start(), calls=%async_computation.5 | async-start | bytes 10485760 | tf_op jit(solution)/shard_map/all_gather | solution.py:758
  392.7 7.1 collective-permute-start.16
  392.7 32.8 %collective-permute-start.19 = (bf16[2,512,2048]{2,1,0:T(8,128)(2,1)}, bf16[2,512,2048]{2,1,0:T(8,128)(2,1)}, u32[]{:S(2)}, u32[]{:S(2)}) collective-permute-start(bf16[2,512,2048]{2,1,0:T(8,128)(2,1)} %get-tuple-element.192.refs_1_.refs_9_.refs_13_), channel_id=1, source_target_pairs={{0,4},{1,5},{2,6},{3,7},{4,0},{5,1},{6,2},{7,3},{8,12},{9,13},{10,... | collective-permute-start | bytes 12582920 | tf_op jit(solution)/shard_map/ppermute | solution.py:528
  393.2 32.6 %collective-permute-start.18 = (bf16[2,512,2048]{2,1,0:T(8,128)(2,1)}, bf16[2,512,2048]{2,1,0:T(8,128)(2,1)}, u32[]{:S(2)}, u32[]{:S(2)}) collective-permute-start(bf16[2,512,2048]{2,1,0:T(8,128)(2,1)} %get-tuple-element.191.refs_1_.refs_8_.refs_12_), channel_id=1, source_target_pairs={{0,4},{1,5},{2,6},{3,7},{4,0},{5,1},{6,2},{7,3},{8,12},{9,13},{10,... | collective-permute-start | bytes 12582920 | tf_op jit(solution)/shard_map/ppermute | solution.py:528
  393.2 31.6 %collective-permute-start.17 = (bf16[512,2048]{1,0:T(8,128)(2,1)}, bf16[512,2048]{1,0:T(8,128)(2,1)}, u32[]{:S(2)}, u32[]{:S(2)}) collective-permute-start(bf16[512,2048]{1,0:T(8,128)(2,1)} %copy-done.15), channel_id=1, source_target_pairs={{0,4},{1,5},{2,6},{3,7},{4,0},{5,1},{6,2},{7,3},{8,12},{9,13},{10,... | collective-permute-start | bytes 6291464 | tf_op jit(solution)/shard_map/ppermute | solution.py:528
  393.7 31.2 %collective-permute-start.15 = (bf16[512,2048]{1,0:T(8,128)(2,1)}, bf16[512,2048]{1,0:T(8,128)(2,1)}, u32[]{:S(2)}, u32[]{:S(2)}) collective-permute-start(bf16[512,2048]{1,0:T(8,128)(2,1)} %copy-done.47), channel_id=1, source_target_pairs={{0,4},{1,5},{2,6},{3,7},{4,0},{5,1},{6,2},{7,3},{8,12},{9,13},{10,... | collective-permute-start | bytes 6291464 | tf_op jit(solution)/shard_map/ppermute | solution.py:528
  401.2 24.1 %collective-permute-start.14 = (bf16[512,2048]{1,0:T(8,128)(2,1)}, bf16[512,2048]{1,0:T(8,128)(2,1)}, u32[]{:S(2)}, u32[]{:S(2)}) collective-permute-start(bf16[512,2048]{1,0:T(8,128)(2,1)} %get-tuple-element.221.n_ref.refs_0_), channel_id=1, source_target_pairs={{0,4},{1,5},{2,6},{3,7},{4,0},{5,1},{6,2},{7,3},{8,12},{9,13},{10,... | collective-permute-start | bytes 6291464 | tf_op jit(solution)/shard_map/ppermute | solution.py:528
  424.8 31.4 %collective-permute-start.22 = (bf16[512,256]{1,0:T(8,128)(2,1)S(1)}, bf16[512,256]{1,0:T(8,128)(2,1)S(1)}, u32[]{:S(2)}, u32[]{:S(2)}) collective-permute-start(bf16[512,256]{1,0:T(8,128)(2,1)S(1)} %fusion.5), channel_id=1, source_target_pairs={{0,1},{1,0},{2,3},{3,2},{4,5},{5,4},{6,7},{7,6},{8,9},{9,8},{10,11... | collective-permute-start | bytes 786440 | tf_op jit(solution)/shard_map/ppermute | solution.py:528
  424.9 107.0 %collective-permute-start.27 = (bf16[2,512,2048]{2,1,0:T(8,128)(2,1)}, bf16[2,512,2048]{2,1,0:T(8,128)(2,1)}, u32[]{:S(2)}, u32[]{:S(2)}) collective-permute-start(bf16[2,512,2048]{2,1,0:T(8,128)(2,1)} %get-tuple-element.223.refs_0_.refs_9_.refs_13_), channel_id=1, source_target_pairs={{0,4},{1,5},{2,6},{3,7},{4,0},{5,1},{6,2},{7,3},{8,12},{9,13},{10,... | collective-permute-start | bytes 12582920 | tf_op jit(solution)/shard_map/ppermute | solution.py:528
  425.3 108.1 %collective-permute-start.26 = (bf16[2,512,2048]{2,1,0:T(8,128)(2,1)}, bf16[2,512,2048]{2,1,0:T(8,128)(2,1)}, u32[]{:S(2)}, u32[]{:S(2)}) collective-permute-start(bf16[2,512,2048]{2,1,0:T(8,128)(2,1)} %get-tuple-element.222.refs_0_.refs_8_.refs_12_), channel_id=1, source_target_pairs={{0,4},{1,5},{2,6},{3,7},{4,0},{5,1},{6,2},{7,3},{8,12},{9,13},{10,... | collective-permute-start | bytes 12582920 | tf_op jit(solution)/shard_map/ppermute | solution.py:528
  425.4 54.8 %collective-permute-start.24 = (bf16[512,2048]{1,0:T(8,128)(2,1)}, bf16[512,2048]{1,0:T(8,128)(2,1)}, u32[]{:S(2)}, u32[]{:S(2)}) collective-permute-start(bf16[512,2048]{1,0:T(8,128)(2,1)} %get-tuple-element.215.refs_0_), channel_id=1, source_target_pairs={{0,4},{1,5},{2,6},{3,7},{4,0},{5,1},{6,2},{7,3},{8,12},{9,13},{10,... | collective-permute-start | bytes 6291464 | tf_op jit(solution)/shard_map/ppermute | solution.py:528
  425.8 57.5 %collective-permute-start.25 = (bf16[512,2048]{1,0:T(8,128)(2,1)}, bf16[512,2048]{1,0:T(8,128)(2,1)}, u32[]{:S(2)}, u32[]{:S(2)}) collective-permute-start(bf16[512,2048]{1,0:T(8,128)(2,1)} %constant_dynamic-update-slice_fusion.4.att_ref), channel_id=1, source_target_pairs={{0,4},{1,5},{2,6},{3,7},{4,0},{5,1},{6,2},{7,3},{8,12},{9,13},{10,... | collective-permute-start | bytes 6291464 | tf_op jit(solution)/shard_map/ppermute | solution.py:528
  459.3 47.6 %collective-permute-start.21 = (bf16[2,2,256,1024]{3,2,0,1:T(8,128)(2,1)}, bf16[2,2,256,1024]{3,2,0,1:T(8,128)(2,1)}, u32[]{:S(2)}, u32[]{:S(2)}) collective-permute-start(bf16[2,2,256,1024]{3,2,0,1:T(8,128)(2,1)} %copy.62), channel_id=1, source_target_pairs={{0,8},{1,9},{2,10},{3,11},{4,12},{5,13},{6,14},{7,15},{8,0},{9,1},... | collective-permute-start | bytes 6291464 | tf_op jit(solution)/shard_map/ppermute | solution.py:528
  480.3 47.3 %collective-permute-start.20 = (bf16[2,2,256,1024]{3,2,0,1:T(8,128)(2,1)}, bf16[2,2,256,1024]{3,2,0,1:T(8,128)(2,1)}, u32[]{:S(2)}, u32[]{:S(2)}) collective-permute-start(bf16[2,2,256,1024]{3,2,0,1:T(8,128)(2,1)} %copy.60), channel_id=1, source_target_pairs={{0,16},{1,17},{2,18},{3,19},{4,20},{5,21},{6,22},{7,23},{8,24},{9,... | collective-permute-start | bytes 6291464 | tf_op jit(solution)/shard_map/ppermute | solution.py:528
  483.3 9.8 %collective-permute-start.23 = (f32[24576]{0:T(1024)S(1)}, f32[24576]{0:T(1024)S(1)}, u32[]{:S(2)}, u32[]{:S(2)}) collective-permute-start(f32[24576]{0:T(1024)S(1)} %fusion.27), channel_id=1, source_target_pairs={{0,4},{1,5},{2,6},{3,7},{4,0},{5,1},{6,2},{7,3},{8,12},{9,13},{10,... | collective-permute-start | bytes 294920 | tf_op jit(solution)/shard_map/ppermute | solution.py:528
  493.1 75.1 %collective-permute-start.33 = (bf16[512,2304]{1,0:T(8,128)(2,1)S(1)}, bf16[512,2304]{1,0:T(8,128)(2,1)}, u32[]{:S(2)}, u32[]{:S(2)}) collective-permute-start(bf16[512,2304]{1,0:T(8,128)(2,1)S(1)} %get-tuple-element.232), channel_id=1, source_target_pairs={{0,4},{1,5},{2,6},{3,7},{4,0},{5,1},{6,2},{7,3},{8,12},{9,13},{10,... | collective-permute-start | bytes 7077896 | tf_op jit(solution)/shard_map/ppermute | solution.py:528
  506.8 61.4 %collective-permute-start.32 = (bf16[512,2048]{1,0:T(8,128)(2,1)}, bf16[512,2048]{1,0:T(8,128)(2,1)}, u32[]{:S(2)}, u32[]{:S(2)}) collective-permute-start(bf16[512,2048]{1,0:T(8,128)(2,1)} %constant_dynamic-slice_fusion.5.refs_0_), channel_id=1, source_target_pairs={{0,4},{1,5},{2,6},{3,7},{4,0},{5,1},{6,2},{7,3},{8,12},{9,13},{10,... | collective-permute-start | bytes 6291464 | tf_op jit(solution)/shard_map/ppermute | solution.py:528
  527.6 36.7 %collective-permute-start.28 = (f32[24576]{0:T(1024)S(1)}, f32[24576]{0:T(1024)S(1)}, u32[]{:S(2)}, u32[]{:S(2)}) collective-permute-start(f32[24576]{0:T(1024)S(1)} %fusion.31), channel_id=1, source_target_pairs={{0,8},{1,9},{2,10},{3,11},{4,12},{5,13},{6,14},{7,15},{8,0},{9,1},... | collective-permute-start | bytes 294920 | tf_op jit(solution)/shard_map/ppermute | solution.py:528
  531.9 33.0 %collective-permute-start.31 = (bf16[2,1,256,1024]{3,2,0,1:T(8,128)(2,1)S(1)}, bf16[2,1,256,1024]{3,2,0,1:T(8,128)(2,1)}, u32[]{:S(2)}, u32[]{:S(2)}) collective-permute-start(bf16[2,1,256,1024]{3,2,0,1:T(8,128)(2,1)S(1)} %slice.178), channel_id=1, source_target_pairs={{0,16},{1,17},{2,18},{3,19},{4,20},{5,21},{6,22},{7,23},{8,24},{9,... | collective-permute-start | bytes 3145736 | tf_op jit(solution)/shard_map/ppermute | solution.py:528
  533.3 33.2 %collective-permute-start.30 = (bf16[2,1,256,1024]{3,2,0,1:T(8,128)(2,1)}, bf16[2,1,256,1024]{3,2,0,1:T(8,128)(2,1)}, u32[]{:S(2)}, u32[]{:S(2)}) collective-permute-start(bf16[2,1,256,1024]{3,2,0,1:T(8,128)(2,1)} %slice.176), channel_id=1, source_target_pairs={{0,8},{1,9},{2,10},{3,11},{4,12},{5,13},{6,14},{7,15},{8,0},{9,1},... | collective-permute-start | bytes 3145736 | tf_op jit(solution)/shard_map/ppermute | solution.py:528
  564.3 14.6 %collective-permute-start.29 = (f32[24576]{0:T(1024)S(1)}, f32[24576]{0:T(1024)S(1)}, u32[]{:S(2)}, u32[]{:S(2)}) collective-permute-start(f32[24576]{0:T(1024)S(1)} %add.483), channel_id=1, source_target_pairs={{0,16},{1,17},{2,18},{3,19},{4,20},{5,21},{6,22},{7,23},{8,24},{9,... | collective-permute-start | bytes 294920 | tf_op jit(solution)/shard_map/ppermute | solution.py:528
  579.0 26.5 %collective-permute-start.39 = (bf16[1,2,256,1024]{3,2,1,0:T(8,128)(2,1)}, bf16[1,2,256,1024]{3,2,1,0:T(8,128)(2,1)}, u32[]{:S(2)}, u32[]{:S(2)}) collective-permute-start(bf16[1,2,256,1024]{3,2,1,0:T(8,128)(2,1)} %get-tuple-element.247), channel_id=1, source_target_pairs={{0,8},{1,9},{2,10},{3,11},{4,12},{5,13},{6,14},{7,15},{8,0},{9,1},... | collective-permute-start | bytes 3145736 | tf_op jit(solution)/shard_map/ppermute | solution.py:528
  579.7 29.1 %collective-permute-start.38 = (bf16[1,2,256,1024]{3,2,1,0:T(8,128)(2,1)}, bf16[1,2,256,1024]{3,2,1,0:T(8,128)(2,1)}, u32[]{:S(2)}, u32[]{:S(2)}) collective-permute-start(bf16[1,2,256,1024]{3,2,1,0:T(8,128)(2,1)} %get-tuple-element.245), channel_id=1, source_target_pairs={{0,16},{1,17},{2,18},{3,19},{4,20},{5,21},{6,22},{7,23},{8,24},{9,... | collective-permute-start | bytes 3145736 | tf_op jit(solution)/shard_map/ppermute | solution.py:528
  581.1 49.6 %collective-permute-start.37 = (bf16[1,2,256,1152]{3,2,1,0:T(8,128)(2,1)}, bf16[1,2,256,1152]{3,2,1,0:T(8,128)(2,1)}, u32[]{:S(2)}, u32[]{:S(2)}) collective-permute-start(bf16[1,2,256,1152]{3,2,1,0:T(8,128)(2,1)} %get-tuple-element.242), channel_id=1, source_target_pairs={{0,8},{1,9},{2,10},{3,11},{4,12},{5,13},{6,14},{7,15},{8,0},{9,1},... | collective-permute-start | bytes 3538952 | tf_op jit(solution)/shard_map/ppermute | solution.py:528
  582.6 51.6 %collective-permute-start.36 = (bf16[1,2,256,1152]{3,2,1,0:T(8,128)(2,1)}, bf16[1,2,256,1152]{3,2,1,0:T(8,128)(2,1)S(1)}, u32[]{:S(2)}, u32[]{:S(2)}) collective-permute-start(bf16[1,2,256,1152]{3,2,1,0:T(8,128)(2,1)} %get-tuple-element.240), channel_id=1, source_target_pairs={{0,16},{1,17},{2,18},{3,19},{4,20},{5,21},{6,22},{7,23},{8,24},{9,... | collective-permute-start | bytes 3538952 | tf_op jit(solution)/shard_map/ppermute | solution.py:528
  584.9 87.8 %collective-permute-start.35 = (bf16[2,2,256,1024]{3,2,0,1:T(8,128)(2,1)S(1)}, bf16[2,2,256,1024]{3,2,0,1:T(8,128)(2,1)S(1)}, u32[]{:S(2)}, u32[]{:S(2)}) collective-permute-start(bf16[2,2,256,1024]{3,2,0,1:T(8,128)(2,1)S(1)} %copy.64), channel_id=1, source_target_pairs={{0,8},{1,9},{2,10},{3,11},{4,12},{5,13},{6,14},{7,15},{8,0},{9,1},... | collective-permute-start | bytes 6291464 | tf_op jit(solution)/shard_map/ppermute | solution.py:528
  605.5 70.7 %collective-permute-start.34 = (bf16[2,2,256,1024]{3,2,1,0:T(8,128)(2,1)S(1)}, bf16[2,2,256,1024]{3,2,1,0:T(8,128)(2,1)S(1)}, u32[]{:S(2)}, u32[]{:S(2)}) collective-permute-start(bf16[2,2,256,1024]{3,2,1,0:T(8,128)(2,1)S(1)} %copy-done.48), channel_id=1, source_target_pairs={{0,16},{1,17},{2,18},{3,19},{4,20},{5,21},{6,22},{7,23},{8,24},{9,... | collective-permute-start | bytes 6291464 | tf_op jit(solution)/shard_map/ppermute | solution.py:528
  608.8 237.0 %collective-permute-start.50 = (f32[24576]{0:T(1024)S(1)}, f32[24576]{0:T(1024)S(1)}, u32[]{:S(2)}, u32[]{:S(2)}) collective-permute-start(f32[24576]{0:T(1024)S(1)} %add.486), channel_id=1, source_target_pairs={{0,1},{1,2},{2,3},{3,0},{4,5},{5,6},{6,7},{7,4},{8,9},{9,10},{10,1... | collective-permute-start | bytes 294920 | tf_op jit(solution)/shard_map/ppermute | solution.py:528
  630.7 215.1 %collective-permute-start.51 = (f32[24576]{0:T(1024)S(1)}, f32[24576]{0:T(1024)S(1)}, u32[]{:S(2)}, u32[]{:S(2)}) collective-permute-start(f32[24576]{0:T(1024)S(1)} %add.486), channel_id=1, source_target_pairs={{0,2},{1,3},{2,0},{3,1},{4,6},{5,7},{6,4},{7,5},{8,10},{9,11},{10,... | collective-permute-start | bytes 294920 | tf_op jit(solution)/shard_map/ppermute | solution.py:528
  634.2 53.2 %collective-permute-start.45 = (bf16[1,1,256,1024]{3,2,1,0:T(8,128)(2,1)S(1)}, bf16[1,1,256,1024]{3,2,1,0:T(8,128)(2,1)S(1)}, u32[]{:S(2)}, u32[]{:S(2)}) collective-permute-start(bf16[1,1,256,1024]{3,2,1,0:T(8,128)(2,1)S(1)} %slice.190), channel_id=1, source_target_pairs={{0,16},{1,17},{2,18},{3,19},{4,20},{5,21},{6,22},{7,23},{8,24},{9,... | collective-permute-start | bytes 1572872 | tf_op jit(solution)/shard_map/ppermute | solution.py:528
  635.4 37.9 %copy-start.17 = (bf16[2,2,256,1024]{3,2,1,0:T(8,128)(2,1)S(1)}, bf16[2,2,256,1024]{3,2,1,0:T(8,128)(2,1)}, u32[]{:S(2)}) copy-start(bf16[2,2,256,1024]{3,2,1,0:T(8,128)(2,1)} %get-tuple-element.236) | copy-start | bytes 6291460
  672.7 16.6 %collective-permute-start.44 = (bf16[1,1,256,1024]{3,2,1,0:T(8,128)(2,1)S(1)}, bf16[1,1,256,1024]{3,2,1,0:T(8,128)(2,1)S(1)}, u32[]{:S(2)}, u32[]{:S(2)}) collective-permute-start(bf16[1,1,256,1024]{3,2,1,0:T(8,128)(2,1)S(1)} %slice.188), channel_id=1, source_target_pairs={{0,8},{1,9},{2,10},{3,11},{4,12},{5,13},{6,14},{7,15},{8,0},{9,1},... | collective-permute-start | bytes 1572872 | tf_op jit(solution)/shard_map/ppermute | solution.py:528
  676.2 20.5 %collective-permute-start.43 = (bf16[1,1,256,1152]{3,2,1,0:T(8,128)(2,1)S(1)}, bf16[1,1,256,1152]{3,2,1,0:T(8,128)(2,1)S(1)}, u32[]{:S(2)}, u32[]{:S(2)}) collective-permute-start(bf16[1,1,256,1152]{3,2,1,0:T(8,128)(2,1)S(1)} %slice.186), channel_id=1, source_target_pairs={{0,16},{1,17},{2,18},{3,19},{4,20},{5,21},{6,22},{7,23},{8,24},{9,... | collective-permute-start | bytes 1769480 | tf_op jit(solution)/shard_map/ppermute | solution.py:528
  687.5 128.4 %collective-permute-start.47 = (bf16[2,256,2048]{2,1,0:T(8,128)(2,1)}, bf16[2,256,2048]{2,1,0:T(8,128)(2,1)}, u32[]{:S(2)}, u32[]{:S(2)}) collective-permute-start(bf16[2,256,2048]{2,1,0:T(8,128)(2,1)} %pad_maximum_fusion.2), channel_id=1, source_target_pairs={{0,2},{1,3},{2,0},{3,1},{4,6},{5,7},{6,4},{7,5},{8,10},{9,11},{10,... | collective-permute-start | bytes 6291464 | tf_op jit(solution)/shard_map/ppermute | solution.py:528
  689.3 11.8 %collective-permute-start.42 = (bf16[1,1,256,1152]{3,2,1,0:T(8,128)(2,1)S(1)}, bf16[1,1,256,1152]{3,2,1,0:T(8,128)(2,1)S(1)}, u32[]{:S(2)}, u32[]{:S(2)}) collective-permute-start(bf16[1,1,256,1152]{3,2,1,0:T(8,128)(2,1)S(1)} %slice.184), channel_id=1, source_target_pairs={{0,8},{1,9},{2,10},{3,11},{4,12},{5,13},{6,14},{7,15},{8,0},{9,1},... | collective-permute-start | bytes 1769480 | tf_op jit(solution)/shard_map/ppermute | solution.py:528
  701.1 17.7 %collective-permute-start.41 = (bf16[2,1,256,1024]{3,2,0,1:T(8,128)(2,1)}, bf16[2,1,256,1024]{3,2,0,1:T(8,128)(2,1)}, u32[]{:S(2)}, u32[]{:S(2)}) collective-permute-start(bf16[2,1,256,1024]{3,2,0,1:T(8,128)(2,1)} %slice.182), channel_id=1, source_target_pairs={{0,16},{1,17},{2,18},{3,19},{4,20},{5,21},{6,22},{7,23},{8,24},{9,... | collective-permute-start | bytes 3145736 | tf_op jit(solution)/shard_map/ppermute | solution.py:528
  703.3 20.0 %collective-permute-start.40 = (bf16[2,1,256,1024]{3,2,1,0:T(8,128)(2,1)}, bf16[2,1,256,1024]{3,2,1,0:T(8,128)(2,1)}, u32[]{:S(2)}, u32[]{:S(2)}) collective-permute-start(bf16[2,1,256,1024]{3,2,1,0:T(8,128)(2,1)} %slice.180), channel_id=1, source_target_pairs={{0,8},{1,9},{2,10},{3,11},{4,12},{5,13},{6,14},{7,15},{8,0},{9,1},... | collective-permute-start | bytes 3145736 | tf_op jit(solution)/shard_map/ppermute | solution.py:528
  718.8 101.8 %collective-permute-start.46 = (bf16[544,512]{1,0:T(8,128)(2,1)}, bf16[544,512]{1,0:T(8,128)(2,1)}, u32[]{:S(2)}, u32[]{:S(2)}) collective-permute-start(bf16[544,512]{1,0:T(8,128)(2,1)} %pad_maximum_fusion.6), channel_id=1, source_target_pairs={{0,1},{1,2},{2,3},{3,0},{4,5},{5,6},{6,7},{7,4},{8,9},{9,10},{10,1... | collective-permute-start | bytes 1671176 | tf_op jit(solution)/shard_map/ppermute | solution.py:528
  723.3 104.6 %collective-permute-start.48 = (bf16[544,512]{1,0:T(8,128)(2,1)}, bf16[544,512]{1,0:T(8,128)(2,1)}, u32[]{:S(2)}, u32[]{:S(2)}) collective-permute-start(bf16[544,512]{1,0:T(8,128)(2,1)} %pad_maximum_fusion.7), channel_id=1, source_target_pairs={{0,2},{1,3},{2,0},{3,1},{4,6},{5,7},{6,4},{7,5},{8,10},{9,11},{10,... | collective-permute-start | bytes 1671176 | tf_op jit(solution)/shard_map/ppermute | solution.py:528
  789.2 28.8 %copy-start.9 = (bf16[2,1,256,1024]{3,2,0,1:T(8,128)(2,1)S(1)}, bf16[2,1,256,1024]{3,2,0,1:T(8,128)(2,1)}, u32[]{:S(2)}) copy-start(bf16[2,1,256,1024]{3,2,0,1:T(8,128)(2,1)} %add_convert_fusion.9) | copy-start | bytes 3145732
  789.2 28.8 %copy-start.10 = (bf16[2,1,256,1024]{3,2,1,0:T(8,128)(2,1)S(1)}, bf16[2,1,256,1024]{3,2,1,0:T(8,128)(2,1)}, u32[]{:S(2)}) copy-start(bf16[2,1,256,1024]{3,2,1,0:T(8,128)(2,1)} %add_convert_fusion.8) | copy-start | bytes 3145732
  815.9 22.6 %collective-permute-start.49 = (bf16[544,512]{1,0:T(8,128)(2,1)S(1)}, bf16[544,512]{1,0:T(8,128)(2,1)S(1)}, u32[]{:S(2)}, u32[]{:S(2)}) collective-permute-start(bf16[544,512]{1,0:T(8,128)(2,1)S(1)} %pad_maximum_fusion.8), channel_id=1, source_target_pairs={{0,3},{1,0},{2,1},{3,2},{4,7},{5,4},{6,5},{7,6},{8,11},{9,8},{10,9... | collective-permute-start | bytes 1671176 | tf_op jit(solution)/shard_map/ppermute | solution.py:528
  820.6 25.3 %collective-permute-start.52 = (f32[24576]{0:T(1024)S(1)}, f32[24576]{0:T(1024)S(1)}, u32[]{:S(2)}, u32[]{:S(2)}) collective-permute-start(f32[24576]{0:T(1024)S(1)} %add.486), channel_id=1, source_target_pairs={{0,3},{1,0},{2,1},{3,2},{4,7},{5,4},{6,5},{7,6},{8,11},{9,8},{10,9... | collective-permute-start | bytes 294920 | tf_op jit(solution)/shard_map/ppermute | solution.py:528
  (49 other events, 450.4 us)
Sparse Core Ops, SparseCore 0:
  27.8 28.4 all-gather.8
  61.4 54.2 all-gather.20
  118.3 53.8 all-gather.10
  175.9 67.0 all-gather.12
  262.1 53.8 all-gather.14
  391.3 151.8 all-gather.16
  544.7 235.4 all-gather.18
